TPU v7x, 256 devices: a whole 4x4x8 slice. The times are simulated.
256 devices in a mesh: dp: 32 (over x, y, core), group: 8 (over z).
Axes of the slice: x: 4, y: 4, z: 8, core: 2. Of those that a mesh axis runs over, the one named last changes fastest.
Arguments:
- grad_codes: bfloat16 [8, 192, 768, 1024], P('group', None, 'dp'), may hold values from -6 to 6
- row_scales: float32 [8, 192, 768], P('group', None, 'dp'), may hold values from 0.3 to 3
- dither: float32 [8, 192, 768], P('group', None, 'dp'), may hold values from -0.5 to 0.5
- owner_table: int32 [192], replicated, may hold values from 0 to 31, as said below
- matrix_kind: int32 [192], replicated, may hold values from 0 to 1
Outputs:
- updates: bfloat16 [192, 768, 1024], P(None, 'dp', 'group')
- slot_norms: float32 [8, 32, 2], P('group', 'dp')
Inputs may be any that keep to these rules, and one draw needn't show every extreme that they name: `owner_table`: within each group of 24 consecutive matrices no owner appears more than 2 times, and in every group some owner appears exactly 2 times. `matrix_kind`: 0 for a gate or up projection, 1 for a down projection stored transposed.
All inputs are finite; a program needn't handle non-finite values.
Results may differ from a plain program's by a relative error of at most 0.018.
Values may be sent and summed in bfloat16 or wider, within the bound.
No kernel may reach another device: no remote copies, remote signals or barrier semaphores. Data moves between devices by JAX's collectives and lax.ppermute only.
A program may use at most 64 MiB of HBM per device.

v0:
```python
import math

import jax
import jax.numpy as jnp
from jax import lax
from jax.sharding import PartitionSpec as P

F = 768
D = 1024
ITERS = 2
CAP = 2


epsilon = 1e-07
first_coef = 3.4445
second_coef = -4.775
third_coef = 2.0315


def newton(assembled, frob_norm):
    current = (assembled.astype(jnp.float32) / (frob_norm[:, None, None] + epsilon)).astype(
        jnp.bfloat16
    )
    for sweep in range(ITERS):
        gram_matrix = jnp.einsum(
            "cfd,cgd->cfg", current, current, preferred_element_type=jnp.float32
        ).astype(jnp.bfloat16)
        squared = jnp.einsum(
            "cfg,cgh->cfh", gram_matrix, gram_matrix, preferred_element_type=jnp.float32
        )
        polynomial = (second_coef * gram_matrix.astype(jnp.float32) + third_coef * squared).astype(
            jnp.bfloat16
        )
        product = jnp.einsum(
            "cfg,cgd->cfd", polynomial, current, preferred_element_type=jnp.float32
        )
        current = (first_coef * current.astype(jnp.float32) + product).astype(jnp.bfloat16)
    return current


def on_device(grad_codes, row_scales, dither, owner_table, matrix_kind):
    group_count = lax.axis_size("group")
    owner_count = lax.axis_size("dp")
    matrices = grad_codes.shape[1]
    per_group = matrices // group_count
    shard_rows = grad_codes.shape[2]
    columns = grad_codes.shape[3]
    height = shard_rows * owner_count
    gate_factor = math.sqrt(max(F, D)) * math.sqrt(max(1.0, F / D))
    down_factor = math.sqrt(max(F, D)) * math.sqrt(max(1.0, D / F))
    norm_scale = 1.0 / math.sqrt(height * columns)
    dequant_terms = (
        row_scales[0][:, :, None] * (grad_codes[0].astype(jnp.float32) + dither[0][:, :, None])
    ).astype(jnp.bfloat16)
    dequant_terms = lax.optimization_barrier(dequant_terms)
    summed = lax.psum_scatter(
        dequant_terms.astype(jnp.float32).astype(jnp.bfloat16),
        "group",
        scatter_dimension=0,
        tiled=True,
    )
    flat_rows = summed.reshape(per_group, shard_rows * columns)
    group_index = lax.axis_index("group")
    owner_index = lax.axis_index("dp")
    owners = lax.dynamic_slice_in_dim(owner_table, group_index * per_group, per_group)
    kind_group = lax.dynamic_slice_in_dim(matrix_kind, group_index * per_group, per_group)
    position = jnp.arange(per_group, dtype=jnp.int32)
    same_owner = owners[:, None] == owners[None, :]
    earlier = position[None, :] < position[:, None]
    slot_of = jnp.sum((same_owner & earlier).astype(jnp.int32), 1)
    factors = jnp.where(kind_group == 1, down_factor, gate_factor).astype(jnp.float32)
    slot_hit = slot_of[:, None] == jnp.arange(CAP, dtype=jnp.int32)[None, :]
    owned_slot = ((owners == owner_index)[:, None] & slot_hit).astype(jnp.float32)
    destination = owners[:, None] == jnp.arange(owner_count, dtype=jnp.int32)[None, :]
    picker = (
        (slot_hit[:, :, None] & destination[:, None, :])
        .reshape(per_group, CAP * owner_count)
        .astype(jnp.bfloat16)
    )
    outgoing = jnp.einsum(
        "mk,mx->kx", picker, flat_rows, preferred_element_type=jnp.float32
    ).astype(jnp.bfloat16)
    outgoing = outgoing.reshape(CAP, owner_count, shard_rows, columns)
    arrived = lax.all_to_all(outgoing, "dp", split_axis=1, concat_axis=1, tiled=True)
    assembled = arrived.reshape(CAP, height, columns)
    frob_norm = jnp.sqrt(jnp.sum(jnp.square(assembled.astype(jnp.float32)), (1, 2)))
    slot_factor = jnp.sum(owned_slot * factors[:, None], 0)
    iterated = newton(assembled, frob_norm)
    scaled_update = (iterated.astype(jnp.float32) * slot_factor[:, None, None]).astype(jnp.bfloat16)
    scaled_update = scaled_update.reshape(CAP, owner_count, shard_rows, columns)
    returned = lax.all_to_all(scaled_update, "dp", split_axis=1, concat_axis=1, tiled=True)
    row_block = jnp.einsum(
        "mk,kx->mx",
        picker,
        returned.reshape(CAP * owner_count, shard_rows * columns),
        preferred_element_type=jnp.float32,
    ).astype(jnp.bfloat16)
    slot_norms = frob_norm * norm_scale
    updates = lax.all_to_all(
        row_block.reshape(per_group, shard_rows, columns),
        "group",
        split_axis=2,
        concat_axis=0,
        tiled=True,
    )
    return (updates, slot_norms.reshape(1, 1, CAP))


def solution(mesh):
    placed = (
        P("group", None, "dp", None),
        P("group", None, "dp"),
        P("group", None, "dp"),
        P(),
        P(),
    )
    return jax.shard_map(
        on_device,
        mesh=mesh,
        in_specs=placed,
        out_specs=(P(None, "dp", "group"), P("group", "dp", None)),
        check_vma=False,
    )
```

profile of v0, /device:TPU:1, one launch (start us, length us, event | category | flops | bytes accessed | tf_op | source)
XLA Modules:
  0.0 337.1 jit_solution(15032967474179184301)
XLA Ops:
  7.2 0.0 reduce-scatter.2.cloned.1.call-start
  7.2 0.8 copy.28
  8.0 0.8 copy.29
  8.9 10.4 %fusion.1 = bf16[192,24,1024]{2,1,0:T(8,128)(2,1)} fusion(bf16[1,192,24,1024]{3,2,1,0:T(8,128)(2,1)} %param.5, f32[192,24]{1,0:T(8,128)S(1)} %copy.29, f32[192,24]{1,0:T(8,128)S(1)} %copy.28), kind=kLoop, calls=%fused_computation.4 | loop fusion | flops 18874368 | bytes 18911232 | tf_op jit(solution)/shard_map/convert_element_type | solution.py:54
  19.3 0.0 copy-start
  19.3 0.0 reduce-scatter.2.cloned.1.call-update
  19.3 0.6 copy-done
  20.0 0.1 broadcast_compare_fusion
  20.1 0.2 convert_reduce_fusion
  20.3 107.8 %reduce-scatter.2.cloned.1.call-done = bf16[24,24,1024]{2,1,0:T(8,128)(2,1)} async-done(((bf16[192,24,1024]{2,1,0:T(8,128)(2,1)}), bf16[24,24,1024]{2,1,0:T(8,128)(2,1)}) %reduce-scatter.2.cloned.1.call-update) | async-done | bytes 1179664 | tf_op jit(solution)/shard_map/reduce_scatter | solution.py:56
  128.1 1.9 copy.36
  130.0 1.0 convolution_convert_fusion
  131.0 1.8 copy.37
  132.8 2.1 copy.30
  134.9 0.0 copy-start.1
  134.9 7.7 %all-to-all-start = ((bf16[2,32,24,1024]{3,2,0,1:T(8,128)(2,1)}), bf16[2,32,24,1024]{3,2,0,1:T(8,128)(2,1)S(1)}, u32[]{:S(2)}, u32[]{:S(2)}) async-start(bf16[2,32,24,1024]{3,2,0,1:T(8,128)(2,1)} %copy.30), calls=%async_computation.1 | async-start | bytes 6291456 | tf_op jit(solution)/shard_map/all_to_all | solution.py:84
  142.7 0.0 copy-done.1
  142.7 0.1 compare_select_fusion
  142.7 0.1 fusion.14
  142.9 39.5 %all-to-all-done = bf16[2,32,24,1024]{3,2,0,1:T(8,128)(2,1)S(1)} async-done(((bf16[2,32,24,1024]{3,2,0,1:T(8,128)(2,1)}), bf16[2,32,24,1024]{3,2,0,1:T(8,128)(2,1)S(1)}, u32[]{:S(2)}, u32[]{:S(2)}) %all-to-all-start) | async-done | bytes 3145760 | tf_op jit(solution)/shard_map/all_to_all | solution.py:84
  182.4 0.9 multiply_reduce_fusion
  183.3 0.5 multiply_bitcast_fusion
  183.8 0.7 copy.31
  184.6 1.0 fusion.2
  185.5 3.9 %convolution_convert_fusion.3 = bf16[2,768,768]{2,1,0:T(8,128)(2,1)} fusion(bf16[2,768,1024]{2,1,0:T(8,128)(2,1)S(1)} %fusion.2), kind=kOutput, calls=%fused_computation.20 | convolution fusion | flops 2417098752 | bytes 5505024 | tf_op jit(solution)/shard_map/cfd,cgd->cfg/dot_general | solution.py:25
  189.4 9.1 %add_convert_fusion.1 = bf16[2,768,1024]{2,1,0:T(8,128)(2,1)} fusion(bf16[2,768,1024]{2,1,0:T(8,128)(2,1)S(1)} %fusion.2, bf16[2,768,768]{2,1,0:T(8,128)(2,1)} %convolution_convert_fusion.3), kind=kOutput, calls=%fused_computation.9 | convolution fusion | flops 4240048128 | bytes 8650752 | tf_op jit(solution)/shard_map/cfg,cgd->cfd/dot_general | solution.py:34
  198.5 6.9 %convolution_convert_fusion.2 = bf16[2,768,768]{2,1,0:T(8,128)(2,1)} fusion(bf16[2,768,1024]{2,1,0:T(8,128)(2,1)} %add_convert_fusion.1), kind=kOutput, calls=%fused_computation.19 | convolution fusion | flops 2417098752 | bytes 5505024 | tf_op jit(solution)/shard_map/cfd,cgd->cfg/dot_general | solution.py:25
  205.5 9.4 %multiply_convert_fusion = bf16[2,768,1024]{2,1,0:T(8,128)(2,1)S(1)} fusion(bf16[2,768,1024]{2,1,0:T(8,128)(2,1)} %add_convert_fusion.1, f32[2]{0:T(128)S(1)} %fusion.14, bf16[2,768,768]{2,1,0:T(8,128)(2,1)} %convolution_convert_fusion.2), kind=kOutput, calls=%fused_computation.7 | convolution fusion | flops 4244766720 | bytes 8650760 | tf_op jit(solution)/shard_map/cfg,cgd->cfd/dot_general | solution.py:34
  214.9 0.4 copy.32
  215.4 43.6 %all_to_all.28 = bf16[2,32,24,1024]{3,2,0,1:T(8,128)(2,1)S(1)} all-to-all(bf16[2,32,24,1024]{3,2,0,1:T(8,128)(2,1)S(1)} %copy.32), channel_id=1, replica_groups=mesh['dp'=32,'group'=8] {'dp'}, dimensions={1} | all-to-all | bytes 6291456 | tf_op jit(solution)/shard_map/all_to_all | solution.py:91
  259.0 0.4 copy.33
  259.3 1.8 copy.38
  261.2 0.6 convolution_convert_fusion.1
  261.8 0.7 copy.39
  262.4 6.1 %copy.34 = bf16[24,24,1024]{1,0,2:T(8,128)(2,1)} copy(bf16[24,24,1024]{2,1,0:T(8,128)(2,1)S(1)} %bitcast.49) | data formatting | bytes 2359296 | tf_op jit(solution)/shard_map/reshape | solution.py:100
  268.5 9.5 %reshape.110 = bf16[8,2,36864]{2,1,0:T(2,128)(2,1)S(1)} reshape(bf16[1024,24,24]{2,1,0:T(8,128)(2,1)} %bitcast.43) | data formatting | bytes 2359296
  278.1 35.8 %all_to_all.29 = bf16[8,2,36864]{2,1,0:T(2,128)(2,1)S(1)} all-to-all(bf16[8,2,36864]{2,1,0:T(2,128)(2,1)S(1)} %reshape.110), channel_id=1, replica_groups=mesh['dp'=32,'group'=8] {'group'}, dimensions={0} | all-to-all | bytes 2359296 | tf_op jit(solution)/shard_map/all_to_all | solution.py:99
  313.9 9.7 %reshape.111 = bf16[1024,24,24]{2,1,0:T(8,128)(2,1)} reshape(bf16[8,2,36864]{2,1,0:T(2,128)(2,1)S(1)} %all_to_all.29) | data formatting | bytes 2359296
  323.6 6.6 %copy.35 = bf16[8,24,24,128]{3,2,1,0:T(8,128)(2,1)} copy(bf16[8,24,24,128]{2,1,3,0:T(8,128)(2,1)} %bitcast.44) | data formatting | bytes 2359296 | tf_op jit(solution)/shard_map/all_to_all | solution.py:99
  (3 shorter events, 0.0 us)
Async XLA Ops:
  7.2 120.9 %reduce-scatter.2.cloned.1.call-start = ((), (), s32[]{:S(2)}) async-start(), calls=%async_computation.4 | async-start | bytes 10616832 | tf_op jit(solution)/shard_map/reduce_scatter | solution.py:56
  19.3 0.7 copy-start
  134.9 7.7 %copy-start.1 = (s32[192]{0:T(256)S(1)}, s32[192]{0:T(256)}, u32[]{:S(2)}) copy-start(s32[192]{0:T(256)} %param.9) | copy-start | bytes 2308
  134.9 47.5 %all-to-all-start = ((bf16[2,32,24,1024]{3,2,0,1:T(8,128)(2,1)}), bf16[2,32,24,1024]{3,2,0,1:T(8,128)(2,1)S(1)}, u32[]{:S(2)}, u32[]{:S(2)}) async-start(bf16[2,32,24,1024]{3,2,0,1:T(8,128)(2,1)} %copy.30), calls=%async_computation.1 | async-start | bytes 6291456 | tf_op jit(solution)/shard_map/all_to_all | solution.py:84
Sparse Core Ops, SparseCore 0:
  19.5 108.5 reduce-scatter.1
where the time goes:
time: 338 us; the launch traced here: 337 us
  waiting for transfers between devices  147 us (43%)
  blocking collectives  79.4 us (23%)
  local copies, waits for them, and re-layouts  44.2 us (13%)
  matrix products  30.9 us (9%)
  between operations  14.2 us (4%)
  other arithmetic  13.3 us (4%)
  starting transfers between devices  7.78 us (2%)
    reduce_scatter x1, waiting for transfers between devices, on_device(): lax.psum_scatter(dequant_terms.astype(jnp.float32).astype(jnp.bfloat16),...  108 us
    all_to_all x1, blocking collectives, on_device(): lax.all_to_all(scaled_update, 'dp', split_axis=1, concat_axis=1, tiled=True)  43.6 us
    all_to_all x1, waiting for transfers between devices, on_device(): lax.all_to_all(outgoing, 'dp', split_axis=1, concat_axis=1, tiled=True)  39.5 us
    all_to_all x1, blocking collectives, on_device(): lax.all_to_all(row_block.reshape(per_group, shard_rows, columns), 'group'...  35.8 us
    unnamed x10, local copies, waits for them, and re-layouts  26.1 us
    dot_general x2, matrix products, newton(): jnp.einsum('cfg,cgd->cfd', polynomial, current, preferred_element_type=jn...  18.6 us
    dot_general x2, matrix products, newton(): jnp.einsum('cfd,cgd->cfg', current, current, preferred_element_type=jnp.f...  10.8 us
    convert_element_type x1, other arithmetic, on_device(): dequant_terms = (row_scales[0][:, :, None] * (grad_codes[0].astype(jnp.fl...  10.4 us
  transfers between devices with their start and end apart: 2, of which 2 were waited for; matrix products, arithmetic and copies ran while one was open for 0% of the time, Pallas kernels for 0%

commit v1 on v0

v1 whole, which is shorter than its diff:
```python
import functools
import math

import jax
import jax.numpy as jnp
from jax import lax
from jax.experimental import pallas as pl
from jax.experimental.pallas import tpu as pltpu
from jax.sharding import PartitionSpec as P

F = 768
D = 1024
ITERS = 2
CAP = 2
STREAMS = 2


epsilon = 1e-07
first_coef = 3.4445
second_coef = -4.775
third_coef = 2.0315


def column_of(table, lane):
    lanes = lax.broadcasted_iota(jnp.int32, table.shape, 1)
    return jnp.sum(jnp.where(lanes == lane, table, 0.0), axis=1, keepdims=True)


def dequantized(codes, scales, shifts, lane):
    return column_of(scales, lane) * (codes.astype(jnp.float32) + column_of(shifts, lane))


def first_kernel(half, targets, up_codes, down_codes, scales_ref, shifts_ref, up_out, down_out):
    per_group = 2 * half
    scales, shifts = scales_ref[...], shifts_ref[...]
    for k in range(half):
        lane = targets[0] * per_group + k
        up_out[k] = dequantized(up_codes[k], scales, shifts, lane).astype(jnp.bfloat16)
        lane = targets[1] * per_group + half + k
        down_out[k] = dequantized(down_codes[k], scales, shifts, lane).astype(jnp.bfloat16)


def second_kernel(
    half,
    targets,
    up_codes,
    down_codes,
    scales_ref,
    shifts_ref,
    up_in,
    down_in,
    up_out,
    down_out,
):
    per_group = 2 * half
    block = pl.program_id(0)
    scales, shifts = scales_ref[...], shifts_ref[...]

    def emit(codes, target, received, out, adding):
        for k in range(half):
            lane = target * per_group + block * half + k
            value = dequantized(codes[k], scales, shifts, lane)
            if adding:
                value = value + received[k].astype(jnp.float32)
            out[k] = value.astype(jnp.bfloat16)

    @pl.when(block == 0)
    def _():
        emit(up_codes, targets[0], up_in, up_out, True)
        emit(down_codes, targets[1], down_in, down_out, False)

    @pl.when(block == 1)
    def _():
        emit(up_codes, targets[0], up_in, up_out, False)
        emit(down_codes, targets[1], down_in, down_out, True)


def later_kernel(
    half,
    targets,
    up_codes,
    down_codes,
    scales_ref,
    shifts_ref,
    up_in,
    down_in,
    up_out,
    down_out,
):
    per_group = 2 * half
    block = pl.program_id(0)
    scales, shifts = scales_ref[...], shifts_ref[...]
    for k in range(half):
        lane = targets[0] * per_group + block * half + k
        value = dequantized(up_codes[k], scales, shifts, lane)
        up_out[k] = (value + up_in[k].astype(jnp.float32)).astype(jnp.bfloat16)
        lane = targets[1] * per_group + block * half + k
        value = dequantized(down_codes[k], scales, shifts, lane)
        down_out[k] = (value + down_in[k].astype(jnp.float32)).astype(jnp.bfloat16)


def last_kernel(count, blocks, targets, codes, scales_ref, shifts_ref, up_in, down_in, out):
    block = pl.program_id(0)
    scales, shifts = scales_ref[...], shifts_ref[...]

    @pl.when(block < blocks)
    def _():
        for k in range(count):
            lane = targets[0] * count * blocks + block * count + k
            value = dequantized(codes[k], scales, shifts, lane)
            value = value + (up_in[k].astype(jnp.float32) + down_in[k].astype(jnp.float32))
            out[k] = value.astype(jnp.bfloat16)

    @pl.when(block >= blocks)
    def _():
        out[...] = jnp.zeros_like(out)


def newton_kernel(
    shard_rows, out_width, factor_ref, *refs
):
    pieces = refs[:STREAMS]
    out_ref, norm_ref, current, gram, poly = refs[STREAMS:]
    height, columns = current.shape
    width = columns // STREAMS
    tile = 8 * shard_rows
    tiles = height // tile
    total = jnp.zeros((1, 1), jnp.float32)
    for stream in range(STREAMS):
        value = pieces[stream][...].astype(jnp.float32)
        total = total + jnp.sum(value * value, keepdims=True)
    norm = jnp.sqrt(total)
    norm_ref[...] = jnp.broadcast_to(norm, norm_ref.shape)
    inverse = 1.0 / (norm + epsilon)
    for stream in range(STREAMS):
        value = pieces[stream][...].astype(jnp.float32)
        current[:, stream * width : (stream + 1) * width] = (value * inverse).astype(jnp.bfloat16)
    for sweep in range(ITERS):
        for i in range(tiles):
            rows = slice(i * tile, (i + 1) * tile)
            product = lax.dot_general(
                current[rows],
                current[...],
                (((1,), (1,)), ((), ())),
                preferred_element_type=jnp.float32,
            )
            gram[rows] = product.astype(jnp.bfloat16)
        for i in range(tiles):
            rows = slice(i * tile, (i + 1) * tile)
            squared = jnp.dot(gram[rows], gram[...], preferred_element_type=jnp.float32)
            poly[rows] = (
                second_coef * gram[rows].astype(jnp.float32) + third_coef * squared
            ).astype(jnp.bfloat16)
        if sweep < ITERS - 1:
            for c in range(columns // 256):
                cols = slice(c * 256, (c + 1) * 256)
                before = current[:, cols]
                product = jnp.dot(poly[...], before, preferred_element_type=jnp.float32)
                current[:, cols] = (
                    first_coef * before.astype(jnp.float32) + product
                ).astype(jnp.bfloat16)
    factor = factor_ref[0]
    per_column = height // shard_rows
    for c in range(columns // 256):
        cols = slice(c * 256, (c + 1) * 256)
        product = jnp.dot(poly[...], current[:, cols], preferred_element_type=jnp.float32)
        result = (first_coef * current[:, cols].astype(jnp.float32) + product).astype(jnp.bfloat16)
        scaled = (result.astype(jnp.float32) * factor).astype(jnp.bfloat16)
        for part in range(256 // out_width):
            first = ((c * 256) // out_width + part) * per_column
            piece = scaled[:, part * out_width : (part + 1) * out_width]
            out_ref[first : first + per_column] = piece.reshape(per_column, shard_rows, out_width)


def on_device(grad_codes, row_scales, dither, owner_table, matrix_kind):
    group_count = lax.axis_size("group")
    owner_count = lax.axis_size("dp")
    matrices = grad_codes.shape[1]
    per_group = matrices // group_count
    shard_rows = grad_codes.shape[2]
    columns = grad_codes.shape[3]
    height = shard_rows * owner_count
    half = per_group // 2
    width = columns // STREAMS
    out_width = columns // group_count
    reach = group_count // 2
    gate_factor = math.sqrt(max(F, D)) * math.sqrt(max(1.0, F / D))
    down_factor = math.sqrt(max(F, D)) * math.sqrt(max(1.0, D / F))
    norm_scale = 1.0 / math.sqrt(height * columns)
    group_index = lax.axis_index("group")
    owner_index = lax.axis_index("dp")
    up = [(i, (i + 1) % group_count) for i in range(group_count)]
    down = [(i, (i - 1) % group_count) for i in range(group_count)]
    codes = grad_codes[0]
    scales = row_scales[0].T
    shifts = dither[0].T
    table = pl.BlockSpec((shard_rows, matrices), lambda i, t: (0, 0))

    def targets_at(distance):
        return jnp.stack(
            [
                lax.rem(group_index + distance, group_count),
                lax.rem(group_index + group_count - distance, group_count),
            ]
        ).astype(jnp.int32)

    def call(kernel, grid, in_specs, out_specs, out_shape, name, operands):
        moved = sum(math.prod(s.shape) * 2 for s in out_shape) * 3
        return pl.pallas_call(
            kernel,
            grid_spec=pltpu.PrefetchScalarGridSpec(
                num_scalar_prefetch=1, grid=grid, in_specs=in_specs, out_specs=out_specs
            ),
            out_shape=out_shape,
            name=name,
            cost_estimate=pl.CostEstimate(flops=0, bytes_accessed=moved, transcendentals=0),
        )(*operands)

    def code_spec(count, blocks, which, first, stream):
        return pl.BlockSpec(
            (count, shard_rows, width), lambda i, t: (t[which] * blocks + first + i, 0, stream)
        )

    block = pl.BlockSpec((half, shard_rows, width), lambda i, t: (i, 0, 0))
    single = pl.BlockSpec((half, shard_rows, width), lambda i, t: (0, 0, 0))
    half_shape = jax.ShapeDtypeStruct((half, shard_rows, width), jnp.bfloat16)
    full_shape = jax.ShapeDtypeStruct((per_group, shard_rows, width), jnp.bfloat16)

    rising = [None] * STREAMS
    falling = [None] * STREAMS
    for step in range(reach):
        distance = reach - step
        targets = targets_at(distance)
        for stream in range(STREAMS):
            if step == 0:
                sends = call(
                    functools.partial(first_kernel, half),
                    (1,),
                    [
                        code_spec(half, 2, 0, 0, stream),
                        code_spec(half, 2, 1, 1, stream),
                        table,
                        table,
                    ],
                    [single, single],
                    [half_shape, half_shape],
                    f"first_{stream}",
                    (targets, codes, codes, scales, shifts),
                )
            else:
                sends = call(
                    functools.partial(second_kernel if step == 1 else later_kernel, half),
                    (2,),
                    [
                        code_spec(half, 2, 0, 0, stream),
                        code_spec(half, 2, 1, 0, stream),
                        table,
                        table,
                        single if step == 1 else block,
                        single if step == 1 else block,
                    ],
                    [block, block],
                    [full_shape, full_shape],
                    f"add_{step}_{stream}",
                    (targets, codes, codes, scales, shifts, rising[stream], falling[stream]),
                )
            rising[stream] = lax.ppermute(sends[0], "group", up)
            falling[stream] = lax.ppermute(sends[1], "group", down)
    pieces = []
    count = math.gcd(per_group, owner_count)
    blocks = per_group // count
    for stream in range(STREAMS):
        received = pl.BlockSpec(
            (count, shard_rows, width), lambda i, t: (jnp.minimum(i, blocks - 1), 0, 0)
        )
        padded = call(
            functools.partial(last_kernel, count, blocks),
            (owner_count // count,),
            [
                pl.BlockSpec(
                    (count, shard_rows, width),
                    lambda i, t: (t[0] * blocks + jnp.minimum(i, blocks - 1), 0, stream),
                ),
                table,
                table,
                received,
                received,
            ],
            [pl.BlockSpec((count, shard_rows, width), lambda i, t: (i, 0, 0))],
            [jax.ShapeDtypeStruct((owner_count, shard_rows, width), jnp.bfloat16)],
            f"last_{stream}",
            (targets_at(0), codes, scales, shifts, rising[stream], falling[stream]),
        )[0]
        arrived = lax.all_to_all(padded, "dp", split_axis=0, concat_axis=0, tiled=True)
        pieces.append(arrived.reshape(height, width))

    owners = lax.dynamic_slice_in_dim(owner_table, group_index * per_group, per_group)
    place = group_index * per_group + jnp.minimum(owner_index, per_group - 1)
    kind = lax.dynamic_slice_in_dim(matrix_kind, place, 1)
    factor = jnp.where(kind == 1, down_factor, gate_factor).astype(jnp.float32)
    whole = pl.BlockSpec(memory_space=pltpu.VMEM)
    blocks_out, norms = pl.pallas_call(
        functools.partial(newton_kernel, shard_rows, out_width),
        in_specs=[pl.BlockSpec(memory_space=pltpu.SMEM)] + [whole] * STREAMS,
        out_specs=[whole, whole],
        out_shape=[
            jax.ShapeDtypeStruct((group_count * owner_count, shard_rows, out_width), jnp.bfloat16),
            jax.ShapeDtypeStruct((8, 128), jnp.float32),
        ],
        scratch_shapes=[
            pltpu.VMEM((height, columns), jnp.bfloat16),
            pltpu.VMEM((height, height), jnp.bfloat16),
            pltpu.VMEM((height, height), jnp.bfloat16),
        ],
        name="newton",
        cost_estimate=pl.CostEstimate(
            flops=2 * ITERS * height * height * (2 * columns + height),
            bytes_accessed=4 * height * columns,
            transcendentals=0,
        ),
        compiler_params=pltpu.CompilerParams(vmem_limit_bytes=40 * 1024 * 1024),
    )(factor, *pieces)
    returned = lax.all_to_all(blocks_out, ("group", "dp"), split_axis=0, concat_axis=0, tiled=True)
    returned = returned.reshape(group_count, owner_count, shard_rows, out_width)
    updates = returned[:, :per_group].reshape(matrices, shard_rows, out_width)

    norms = norms[None]
    stride = 1
    while stride < owner_count:
        partner = [(i, i ^ stride) for i in range(owner_count)]
        other = lax.ppermute(norms, "dp", partner)
        low = (owner_index & stride) == 0
        norms = jnp.concatenate([jnp.where(low, norms, other), jnp.where(low, other, norms)])
        stride *= 2
    all_norms = norms[:per_group, 0, 0]
    position = jnp.arange(per_group, dtype=jnp.int32)
    same_owner = owners[:, None] == owners[None, :]
    earlier = position[None, :] < position[:, None]
    slot_of = jnp.sum((same_owner & earlier).astype(jnp.int32), 1)
    slot_hit = slot_of[:, None] == jnp.arange(CAP, dtype=jnp.int32)[None, :]
    owned_slot = (owners == owner_index)[:, None] & slot_hit
    slot_norms = jnp.sum(jnp.where(owned_slot, all_norms[:, None] * norm_scale, 0.0), 0)
    return (updates, slot_norms.reshape(1, 1, CAP))


def solution(mesh):
    placed = (
        P("group", None, "dp", None),
        P("group", None, "dp"),
        P("group", None, "dp"),
        P(),
        P(),
    )
    return jax.shard_map(
        on_device,
        mesh=mesh,
        in_specs=placed,
        out_specs=(P(None, "dp", "group"), P("group", "dp", None)),
        check_vma=False,
    )
```

time: 338 us -> 213 us (0.63)
  blocking collectives: 79.4 us -> 0 us
  waiting for transfers between devices: 147 us -> 86.5 us
  starting transfers between devices: 7.78 us -> 61.3 us
  Pallas kernels: 0 us -> 44.6 us
  matrix products: 30.9 us -> 0 us
  local copies, waits for them, and re-layouts: 44.2 us -> 14.4 us
  between operations: 14.2 us -> 1.46 us
  other arithmetic: 13.3 us -> 4.28 us
    reduce_scatter x1 -> x0, waiting for transfers between devices: 108 us -> none  [on_device(): lax.psum_scatter(dequant_terms.astype(jnp.float32).astype(jnp.bfloat16),...]
    all_to_all x2 -> x0, blocking collectives: 79.4 us -> none  [the longest x1 43.6 us: on_device(): lax.all_to_all(scaled_update, 'dp', split_axis=1, concat_axis=1, tiled=True)]
    ppermute x0 -> x21, waiting for transfers between devices: none -> 52.7 us  [the longest x8 36.8 us: on_device(): rising[stream] = lax.ppermute(sends[0], 'group', up)]
    pallas_call x0 -> x11, Pallas kernels: none -> 44.6 us  [the longest x10 34.4 us: call(): pl.pallas_call(kernel, grid_spec=pltpu.PrefetchScalarGridSpec(num_scalar_...]
    dot_general x6 -> x0, matrix products: 30.9 us -> none  [the longest x2 18.6 us: newton(): jnp.einsum('cfg,cgd->cfd', polynomial, current, preferred_element_type=jn...]
    ppermute x0 -> x21, starting transfers between devices: none -> 29.2 us  [the longest x8 21.8 us: on_device(): falling[stream] = lax.ppermute(sends[1], 'group', down)]
    all_to_all x1 -> x3, starting transfers between devices: 7.74 us -> 32.1 us  [the longest x2 24.1 us: on_device(): lax.all_to_all(padded, 'dp', split_axis=0, concat_axis=0, tiled=True)]
    unnamed x10 -> x36, local copies, waits for them, and re-layouts: 26.1 us -> 12.6 us
  transfers between devices with their start and end apart: 2 -> 24, of which waited for: 2 -> 13; matrix products, arithmetic and copies ran while one was open for 0% -> 2% of each run, Pallas kernels for 0% -> 13%
where the time goes in v1:
time: 213 us
  waiting for transfers between devices  86.5 us (41%)
  starting transfers between devices  61.3 us (29%)
  Pallas kernels  44.6 us (21%)
  local copies, waits for them, and re-layouts  14.4 us (7%)
  other arithmetic  4.28 us (2%)
    ppermute x8, waiting for transfers between devices, on_device(): rising[stream] = lax.ppermute(sends[0], 'group', up)  36.8 us
    pallas_call x10, Pallas kernels, call(): pl.pallas_call(kernel, grid_spec=pltpu.PrefetchScalarGridSpec(num_scalar_...  34.4 us
    all_to_all x2, starting transfers between devices, on_device(): lax.all_to_all(padded, 'dp', split_axis=0, concat_axis=0, tiled=True)  24.1 us
    ppermute x8, starting transfers between devices, on_device(): falling[stream] = lax.ppermute(sends[1], 'group', down)  21.8 us
    all_to_all x1, waiting for transfers between devices, on_device(): lax.all_to_all(blocks_out, ('group', 'dp'), split_axis=0, concat_axis=0,...  20.9 us
    ppermute x5, waiting for transfers between devices, on_device(): other = lax.ppermute(norms, 'dp', partner)  15.8 us
    all_to_all x2, waiting for transfers between devices, on_device(): lax.all_to_all(padded, 'dp', split_axis=0, concat_axis=0, tiled=True)  13 us
    unnamed x36, local copies, waits for them, and re-layouts  12.6 us
  transfers between devices with their start and end apart: 24, of which 13 were waited for; matrix products, arithmetic and copies ran while one was open for 2% of the time, Pallas kernels for 13%

profile of v1, /device:TPU:1, one launch (start us, length us, event | category | flops | bytes accessed | tf_op | source)
XLA Modules:
  0.0 212.6 jit_solution(942051039327379657)
XLA Ops:
  1.3 2.8 %first_1.1 = (bf16[12,24,512]{2,1,0:T(8,128)(2,1)}, bf16[12,24,512]{2,1,0:T(8,128)(2,1)}) custom-call(s32[2]{0:T(128)} %pad_add_fusion.4.targets, bf16[192,24,1024]{2,1,0:T(8,128)(2,1)} %bitcast.27, bf16[192,24,1024]{2,1,0:T(8,128)(2,1)} %bitcast.28, f32[24,192]{1,0:T(8,128)} %bitcast.46, f32[24,192]{1,0:T(8,128)} %bitcast.56), custom_call_target="tpu_custom_call" | custom-call | bytes 1769472 | tf_op jit(solution)/shard_map/first_1/pallas_call | solution.py:209
  4.1 2.5 %collective-permute-start.8 = (bf16[12,24,512]{2,1,0:T(8,128)(2,1)}, bf16[12,24,512]{2,1,0:T(8,128)(2,1)S(1)}, u32[]{:S(2)}, u32[]{:S(2)}) collective-permute-start(bf16[12,24,512]{2,1,0:T(8,128)(2,1)} %get-tuple-element.28), channel_id=1, source_target_pairs={{0,1},{1,2},{2,3},{3,4},{4,5},{5,6},{6,7},{7,0},{8,9},{9,10},{10,1... | collective-permute-start | bytes 884744 | tf_op jit(solution)/shard_map/ppermute | solution.py:267
  6.5 3.9 %collective-permute-start.9 = (bf16[12,24,512]{2,1,0:T(8,128)(2,1)}, bf16[12,24,512]{2,1,0:T(8,128)(2,1)S(1)}, u32[]{:S(2)}, u32[]{:S(2)}) collective-permute-start(bf16[12,24,512]{2,1,0:T(8,128)(2,1)} %get-tuple-element.29), channel_id=1, source_target_pairs={{0,7},{1,0},{2,1},{3,2},{4,3},{5,4},{6,5},{7,6},{8,15},{9,8},{10,9... | collective-permute-start | bytes 884744 | tf_op jit(solution)/shard_map/ppermute | solution.py:268
  11.0 6.4 %collective-permute-done.8.up_in = bf16[12,24,512]{2,1,0:T(8,128)(2,1)S(1)} collective-permute-done((bf16[12,24,512]{2,1,0:T(8,128)(2,1)}, bf16[12,24,512]{2,1,0:T(8,128)(2,1)S(1)}, u32[]{:S(2)}, u32[]{:S(2)}) %collective-permute-start.8) | collective-permute-done | bytes 294944 | tf_op jit(solution)/shard_map/ppermute | solution.py:267
  18.8 3.4 %add_1_1.1 = (bf16[24,24,512]{2,1,0:T(8,128)(2,1)}, bf16[24,24,512]{2,1,0:T(8,128)(2,1)}) custom-call(s32[2]{0:T(128)} %pad_add_fusion.3.targets, bf16[192,24,1024]{2,1,0:T(8,128)(2,1)} %bitcast.29, bf16[192,24,1024]{2,1,0:T(8,128)(2,1)} %bitcast.30, f32[24,192]{1,0:T(8,128)} %bitcast.47, f32[24,192]{1,0:T(8,128)} %bitcast.57, ...), custom_call_target="tpu_custom_call" | custom-call | bytes 3538944 | tf_op jit(solution)/shard_map/add_1_1/pallas_call | solution.py:209
  22.2 2.7 %collective-permute-start.11 = (bf16[24,24,512]{2,1,0:T(8,128)(2,1)}, bf16[24,24,512]{2,1,0:T(8,128)(2,1)S(1)}, u32[]{:S(2)}, u32[]{:S(2)}) collective-permute-start(bf16[24,24,512]{2,1,0:T(8,128)(2,1)} %get-tuple-element.31), channel_id=1, source_target_pairs={{0,7},{1,0},{2,1},{3,2},{4,3},{5,4},{6,5},{7,6},{8,15},{9,8},{10,9... | collective-permute-start | bytes 1769480 | tf_op jit(solution)/shard_map/ppermute | solution.py:268
  24.9 2.8 %first_0.1 = (bf16[12,24,512]{2,1,0:T(8,128)(2,1)}, bf16[12,24,512]{2,1,0:T(8,128)(2,1)}) custom-call(s32[2]{0:T(128)} %pad_add_fusion.4.targets, bf16[192,24,1024]{2,1,0:T(8,128)(2,1)} %bitcast.31, bf16[192,24,1024]{2,1,0:T(8,128)(2,1)} %bitcast.32, f32[24,192]{1,0:T(8,128)} %bitcast.48, f32[24,192]{1,0:T(8,128)} %bitcast.58), custom_call_target="tpu_custom_call" | custom-call | bytes 1769472 | tf_op jit(solution)/shard_map/first_0/pallas_call | solution.py:209
  27.7 2.7 %collective-permute-start.1 = (bf16[12,24,512]{2,1,0:T(8,128)(2,1)}, bf16[12,24,512]{2,1,0:T(8,128)(2,1)S(1)}, u32[]{:S(2)}, u32[]{:S(2)}) collective-permute-start(bf16[12,24,512]{2,1,0:T(8,128)(2,1)} %get-tuple-element.21), channel_id=1, source_target_pairs={{0,7},{1,0},{2,1},{3,2},{4,3},{5,4},{6,5},{7,6},{8,15},{9,8},{10,9... | collective-permute-start | bytes 884744 | tf_op jit(solution)/shard_map/ppermute | solution.py:268
  31.0 6.3 %collective-permute-done.10.up_in = bf16[24,24,512]{2,1,0:T(8,128)(2,1)S(1)} collective-permute-done((bf16[24,24,512]{2,1,0:T(8,128)(2,1)}, bf16[24,24,512]{2,1,0:T(8,128)(2,1)S(1)}, u32[]{:S(2)}, u32[]{:S(2)}) %collective-permute-start.10) | collective-permute-done | bytes 589856 | tf_op jit(solution)/shard_map/ppermute | solution.py:267
  37.3 0.8 copy-done.7
  38.1 0.8 copy-done.9
  38.9 3.4 %add_2_1.1 = (bf16[24,24,512]{2,1,0:T(8,128)(2,1)}, bf16[24,24,512]{2,1,0:T(8,128)(2,1)}) custom-call(s32[2]{0:T(128)} %pad_add_fusion.2.targets, bf16[192,24,1024]{2,1,0:T(8,128)(2,1)} %bitcast.33, bf16[192,24,1024]{2,1,0:T(8,128)(2,1)} %bitcast.34, f32[24,192]{1,0:T(8,128)} %bitcast.49, f32[24,192]{1,0:T(8,128)} %bitcast.59, ...), custom_call_target="tpu_custom_call" | custom-call | bytes 3538944 | tf_op jit(solution)/shard_map/add_2_1/pallas_call | solution.py:209
  42.3 2.7 %collective-permute-start.13 = (bf16[24,24,512]{2,1,0:T(8,128)(2,1)}, bf16[24,24,512]{2,1,0:T(8,128)(2,1)S(1)}, u32[]{:S(2)}, u32[]{:S(2)}) collective-permute-start(bf16[24,24,512]{2,1,0:T(8,128)(2,1)} %get-tuple-element.33), channel_id=1, source_target_pairs={{0,7},{1,0},{2,1},{3,2},{4,3},{5,4},{6,5},{7,6},{8,15},{9,8},{10,9... | collective-permute-start | bytes 1769480 | tf_op jit(solution)/shard_map/ppermute | solution.py:268
  46.5 3.4 %add_1_0.1 = (bf16[24,24,512]{2,1,0:T(8,128)(2,1)}, bf16[24,24,512]{2,1,0:T(8,128)(2,1)}) custom-call(s32[2]{0:T(128)} %pad_add_fusion.3.targets, bf16[192,24,1024]{2,1,0:T(8,128)(2,1)} %bitcast.35, bf16[192,24,1024]{2,1,0:T(8,128)(2,1)} %bitcast.36, f32[24,192]{1,0:T(8,128)} %bitcast.50, f32[24,192]{1,0:T(8,128)} %bitcast.60, ...), custom_call_target="tpu_custom_call" | custom-call | bytes 3538944 | tf_op jit(solution)/shard_map/add_1_0/pallas_call | solution.py:209
  49.9 2.7 %collective-permute-start.3 = (bf16[24,24,512]{2,1,0:T(8,128)(2,1)}, bf16[24,24,512]{2,1,0:T(8,128)(2,1)S(1)}, u32[]{:S(2)}, u32[]{:S(2)}) collective-permute-start(bf16[24,24,512]{2,1,0:T(8,128)(2,1)} %get-tuple-element.23), channel_id=1, source_target_pairs={{0,7},{1,0},{2,1},{3,2},{4,3},{5,4},{6,5},{7,6},{8,15},{9,8},{10,9... | collective-permute-start | bytes 1769480 | tf_op jit(solution)/shard_map/ppermute | solution.py:268
  53.1 1.7 collective-permute-done.12.up_in
  54.8 0.8 copy-done
  56.4 3.4 %add_3_1.1 = (bf16[24,24,512]{2,1,0:T(8,128)(2,1)}, bf16[24,24,512]{2,1,0:T(8,128)(2,1)}) custom-call(s32[2]{0:T(128)} %pad_add_fusion.1.targets, bf16[192,24,1024]{2,1,0:T(8,128)(2,1)} %bitcast.37, bf16[192,24,1024]{2,1,0:T(8,128)(2,1)} %bitcast.38, f32[24,192]{1,0:T(8,128)} %bitcast.51, f32[24,192]{1,0:T(8,128)} %bitcast.61, bf16[24,24,512]{2,1,0:T(8,128)(2,1)} %copy-done, ...), custom_call_target="tpu_custom_call" | custom-call | bytes 3538944 | tf_op jit(solution)/shard_map/add_3_1/pallas_call | solution.py:209
  59.9 2.7 %collective-permute-start.15 = (bf16[24,24,512]{2,1,0:T(8,128)(2,1)}, bf16[24,24,512]{2,1,0:T(8,128)(2,1)S(1)}, u32[]{:S(2)}, u32[]{:S(2)}) collective-permute-start(bf16[24,24,512]{2,1,0:T(8,128)(2,1)} %get-tuple-element.35), channel_id=1, source_target_pairs={{0,7},{1,0},{2,1},{3,2},{4,3},{5,4},{6,5},{7,6},{8,15},{9,8},{10,9... | collective-permute-start | bytes 1769480 | tf_op jit(solution)/shard_map/ppermute | solution.py:268
  62.6 4.9 %collective-permute-done.2.up_in = bf16[24,24,512]{2,1,0:T(8,128)(2,1)S(1)} collective-permute-done((bf16[24,24,512]{2,1,0:T(8,128)(2,1)}, bf16[24,24,512]{2,1,0:T(8,128)(2,1)S(1)}, u32[]{:S(2)}, u32[]{:S(2)}) %collective-permute-start.2) | collective-permute-done | bytes 589856 | tf_op jit(solution)/shard_map/ppermute | solution.py:267
  68.3 0.8 copy-done.4
  69.1 3.4 %add_2_0.1 = (bf16[24,24,512]{2,1,0:T(8,128)(2,1)}, bf16[24,24,512]{2,1,0:T(8,128)(2,1)}) custom-call(s32[2]{0:T(128)} %pad_add_fusion.2.targets, bf16[192,24,1024]{2,1,0:T(8,128)(2,1)} %bitcast.39, bf16[192,24,1024]{2,1,0:T(8,128)(2,1)} %bitcast.40, f32[24,192]{1,0:T(8,128)} %bitcast.52, f32[24,192]{1,0:T(8,128)} %bitcast.62, ...), custom_call_target="tpu_custom_call" | custom-call | bytes 3538944 | tf_op jit(solution)/shard_map/add_2_0/pallas_call | solution.py:209
  72.5 2.7 %collective-permute-start.5 = (bf16[24,24,512]{2,1,0:T(8,128)(2,1)}, bf16[24,24,512]{2,1,0:T(8,128)(2,1)S(1)}, u32[]{:S(2)}, u32[]{:S(2)}) collective-permute-start(bf16[24,24,512]{2,1,0:T(8,128)(2,1)} %get-tuple-element.25), channel_id=1, source_target_pairs={{0,7},{1,0},{2,1},{3,2},{4,3},{5,4},{6,5},{7,6},{8,15},{9,8},{10,9... | collective-permute-start | bytes 1769480 | tf_op jit(solution)/shard_map/ppermute | solution.py:268
  75.8 4.2 %collective-permute-done.14.up_in = bf16[24,24,512]{2,1,0:T(8,128)(2,1)S(1)} collective-permute-done((bf16[24,24,512]{2,1,0:T(8,128)(2,1)}, bf16[24,24,512]{2,1,0:T(8,128)(2,1)S(1)}, u32[]{:S(2)}, u32[]{:S(2)}) %collective-permute-start.14) | collective-permute-done | bytes 589856 | tf_op jit(solution)/shard_map/ppermute | solution.py:267
  80.9 0.8 copy-done.5
  81.7 4.2 %last_1.1 = bf16[32,24,512]{2,1,0:T(8,128)(2,1)} custom-call(s32[2]{0:T(128)} %pad_add_fusion.targets, bf16[192,24,1024]{2,1,0:T(8,128)(2,1)} %bitcast.41, f32[24,192]{1,0:T(8,128)} %bitcast.53, f32[24,192]{1,0:T(8,128)} %bitcast.63, bf16[24,24,512]{2,1,0:T(8,128)(2,1)} %copy-done.2, bf16[24,24,512]{2,1,0:T(8,128)(2,1)} %copy-done.5), custom_call_target="tpu_custom_call" | custom-call | bytes 2359296 | tf_op jit(solution)/shard_map/last_1/pallas_call | solution.py:209
  85.9 16.0 %all-to-all-start.1 = ((bf16[32,24,512]{2,1,0:T(8,128)(2,1)}), bf16[32,24,512]{2,1,0:T(8,128)(2,1)S(1)}, u32[]{:S(2)}, u32[]{:S(2)}) async-start(bf16[32,24,512]{2,1,0:T(8,128)(2,1)} %last_1.1), calls=%async_computation.1 | async-start | bytes 1572864 | tf_op jit(solution)/shard_map/all_to_all | solution.py:294
  102.8 0.8 copy-done.8
  103.6 3.4 %add_3_0.1 = (bf16[24,24,512]{2,1,0:T(8,128)(2,1)}, bf16[24,24,512]{2,1,0:T(8,128)(2,1)}) custom-call(s32[2]{0:T(128)} %pad_add_fusion.1.targets, bf16[192,24,1024]{2,1,0:T(8,128)(2,1)} %bitcast.42, bf16[192,24,1024]{2,1,0:T(8,128)(2,1)} %bitcast.43, f32[24,192]{1,0:T(8,128)} %bitcast.54, f32[24,192]{1,0:T(8,128)} %bitcast.64, ...), custom_call_target="tpu_custom_call" | custom-call | bytes 3538944 | tf_op jit(solution)/shard_map/add_3_0/pallas_call | solution.py:209
  107.0 0.8 collective-permute-start.6
  107.9 1.8 collective-permute-start.7
  109.7 13.4 %collective-permute-done.6.up_in = bf16[24,24,512]{2,1,0:T(8,128)(2,1)S(1)} collective-permute-done((bf16[24,24,512]{2,1,0:T(8,128)(2,1)}, bf16[24,24,512]{2,1,0:T(8,128)(2,1)S(1)}, u32[]{:S(2)}, u32[]{:S(2)}) %collective-permute-start.6) | collective-permute-done | bytes 589856 | tf_op jit(solution)/shard_map/ppermute | solution.py:267
  123.1 0.8 copy-done.10
  123.9 0.8 copy-done.11
  124.7 4.1 %last_0.1 = bf16[32,24,512]{2,1,0:T(8,128)(2,1)} custom-call(s32[2]{0:T(128)} %pad_add_fusion.targets, bf16[192,24,1024]{2,1,0:T(8,128)(2,1)} %bitcast.44, f32[24,192]{1,0:T(8,128)} %bitcast.55, f32[24,192]{1,0:T(8,128)} %bitcast.65, bf16[24,24,512]{2,1,0:T(8,128)(2,1)} %copy-done.10, bf16[24,24,512]{2,1,0:T(8,128)(2,1)} %copy-done.11), custom_call_target="tpu_custom_call" | custom-call | bytes 2359296 | tf_op jit(solution)/shard_map/last_0/pallas_call | solution.py:209
  128.8 8.1 %all-to-all-start = ((bf16[32,24,512]{2,1,0:T(8,128)(2,1)}), bf16[32,24,512]{2,1,0:T(8,128)(2,1)S(1)}, u32[]{:S(2)}, u32[]{:S(2)}) async-start(bf16[32,24,512]{2,1,0:T(8,128)(2,1)} %last_0.1), calls=%async_computation | async-start | bytes 1572864 | tf_op jit(solution)/shard_map/all_to_all | solution.py:294
  138.2 13.0 %all-to-all-done = bf16[32,24,512]{2,1,0:T(8,128)(2,1)S(1)} async-done(((bf16[32,24,512]{2,1,0:T(8,128)(2,1)}), bf16[32,24,512]{2,1,0:T(8,128)(2,1)S(1)}, u32[]{:S(2)}, u32[]{:S(2)}) %all-to-all-start) | async-done | bytes 786464 | tf_op jit(solution)/shard_map/all_to_all | solution.py:294
  151.2 10.2 %newton.1 = (bf16[256,24,128]{2,1,0:T(8,128)(2,1)}, f32[8,128]{1,0:T(8,128)S(1)}) custom-call(f32[1]{0:T(128)S(6)} %select_n.75.factor_ref, bf16[768,512]{1,0:T(8,128)(2,1)S(1)} %bitcast.25, bf16[768,512]{1,0:T(8,128)(2,1)S(1)} %bitcast.24), custom_call_target="tpu_custom_call" | custom-call | flops 6643777536 | bytes 3145728 | tf_op jit(solution)/shard_map/newton/pallas_call | solution.py:302
  161.4 8.0 %all-to-all-start.2 = ((bf16[256,24,128]{2,1,0:T(8,128)(2,1)}), bf16[256,24,128]{2,1,0:T(8,128)(2,1)S(1)}, u32[]{:S(2)}, u32[]{:S(2)}) async-start(bf16[256,24,128]{2,1,0:T(8,128)(2,1)} %get-tuple-element.36), calls=%async_computation.2 | async-start | bytes 3145728 | tf_op jit(solution)/shard_map/all_to_all | solution.py:323
  169.3 2.2 %collective-permute-start.16 = (f32[1,8,128]{2,1,0:T(8,128)S(1)}, f32[1,8,128]{2,1,0:T(8,128)S(1)}, u32[]{:S(2)}, u32[]{:S(2)}) collective-permute-start(f32[1,8,128]{2,1,0:T(8,128)S(1)} %bitcast.26), channel_id=1, source_target_pairs={{0,8},{8,0},{16,24},{24,16},{32,40},{40,32},{48,56},{56,48},{64,72... | collective-permute-start | bytes 12296 | tf_op jit(solution)/shard_map/ppermute | solution.py:331
  171.6 0.8 collective-permute-done.16
  172.4 3.1 %collective-permute-done.17 = f32[2,8,128]{2,1,0:T(8,128)S(1)} collective-permute-done((f32[2,8,128]{2,1,0:T(8,128)S(1)}, f32[2,8,128]{2,1,0:T(8,128)S(1)}, u32[]{:S(2)}, u32[]{:S(2)}) %collective-permute-start.17) | collective-permute-done | bytes 8224 | tf_op jit(solution)/shard_map/ppermute | solution.py:331
  175.5 1.3 collective-permute-start.18
  176.8 3.4 %collective-permute-done.18 = f32[4,8,128]{2,1,0:T(8,128)S(1)} collective-permute-done((f32[4,8,128]{2,1,0:T(8,128)S(1)}, f32[4,8,128]{2,1,0:T(8,128)S(1)}, u32[]{:S(2)}, u32[]{:S(2)}) %collective-permute-start.18) | collective-permute-done | bytes 16416 | tf_op jit(solution)/shard_map/ppermute | solution.py:331
  180.5 3.5 %collective-permute-done.19 = f32[8,8,128]{2,1,0:T(8,128)S(1)} collective-permute-done((f32[8,8,128]{2,1,0:T(8,128)S(1)}, f32[8,8,128]{2,1,0:T(8,128)S(1)}, u32[]{:S(2)}, u32[]{:S(2)}) %collective-permute-start.19) | collective-permute-done | bytes 32800 | tf_op jit(solution)/shard_map/ppermute | solution.py:331
  184.5 5.0 %collective-permute-done.20 = f32[16,8,128]{2,1,0:T(8,128)S(1)} collective-permute-done((f32[16,8,128]{2,1,0:T(8,128)S(1)}, f32[16,8,128]{2,1,0:T(8,128)S(1)}, u32[]{:S(2)}, u32[]{:S(2)}) %collective-permute-start.20) | collective-permute-done | bytes 65568 | tf_op jit(solution)/shard_map/ppermute | solution.py:331
  190.5 20.9 %all-to-all-done.2 = bf16[256,24,128]{2,1,0:T(8,128)(2,1)S(1)} async-done(((bf16[256,24,128]{2,1,0:T(8,128)(2,1)}), bf16[256,24,128]{2,1,0:T(8,128)(2,1)S(1)}, u32[]{:S(2)}, u32[]{:S(2)}) %all-to-all-start.2) | async-done | bytes 1572896 | tf_op jit(solution)/shard_map/all_to_all | solution.py:323
  211.3 1.2 slice.8
  (67 shorter events, 11.5 us)
Async XLA Ops:
  4.1 13.3 %collective-permute-start.8 = (bf16[12,24,512]{2,1,0:T(8,128)(2,1)}, bf16[12,24,512]{2,1,0:T(8,128)(2,1)S(1)}, u32[]{:S(2)}, u32[]{:S(2)}) collective-permute-start(bf16[12,24,512]{2,1,0:T(8,128)(2,1)} %get-tuple-element.28), channel_id=1, source_target_pairs={{0,1},{1,2},{2,3},{3,4},{4,5},{5,6},{6,7},{7,0},{8,9},{9,10},{10,1... | collective-permute-start | bytes 884744 | tf_op jit(solution)/shard_map/ppermute | solution.py:267
  6.5 10.9 %collective-permute-start.9 = (bf16[12,24,512]{2,1,0:T(8,128)(2,1)}, bf16[12,24,512]{2,1,0:T(8,128)(2,1)S(1)}, u32[]{:S(2)}, u32[]{:S(2)}) collective-permute-start(bf16[12,24,512]{2,1,0:T(8,128)(2,1)} %get-tuple-element.29), channel_id=1, source_target_pairs={{0,7},{1,0},{2,1},{3,2},{4,3},{5,4},{6,5},{7,6},{8,15},{9,8},{10,9... | collective-permute-start | bytes 884744 | tf_op jit(solution)/shard_map/ppermute | solution.py:268
  17.4 0.7 copy-start.14
  18.1 0.7 copy-start.15
  22.2 15.1 %collective-permute-start.10 = (bf16[24,24,512]{2,1,0:T(8,128)(2,1)}, bf16[24,24,512]{2,1,0:T(8,128)(2,1)S(1)}, u32[]{:S(2)}, u32[]{:S(2)}) collective-permute-start(bf16[24,24,512]{2,1,0:T(8,128)(2,1)} %get-tuple-element.30), channel_id=1, source_target_pairs={{0,1},{1,2},{2,3},{3,4},{4,5},{5,6},{6,7},{7,0},{8,9},{9,10},{10,1... | collective-permute-start | bytes 1769480 | tf_op jit(solution)/shard_map/ppermute | solution.py:267
  22.2 15.1 %collective-permute-start.11 = (bf16[24,24,512]{2,1,0:T(8,128)(2,1)}, bf16[24,24,512]{2,1,0:T(8,128)(2,1)S(1)}, u32[]{:S(2)}, u32[]{:S(2)}) collective-permute-start(bf16[24,24,512]{2,1,0:T(8,128)(2,1)} %get-tuple-element.31), channel_id=1, source_target_pairs={{0,7},{1,0},{2,1},{3,2},{4,3},{5,4},{6,5},{7,6},{8,15},{9,8},{10,9... | collective-permute-start | bytes 1769480 | tf_op jit(solution)/shard_map/ppermute | solution.py:268
  27.7 17.3 %collective-permute-start = (bf16[12,24,512]{2,1,0:T(8,128)(2,1)}, bf16[12,24,512]{2,1,0:T(8,128)(2,1)S(1)}, u32[]{:S(2)}, u32[]{:S(2)}) collective-permute-start(bf16[12,24,512]{2,1,0:T(8,128)(2,1)} %get-tuple-element.20), channel_id=1, source_target_pairs={{0,1},{1,2},{2,3},{3,4},{4,5},{5,6},{6,7},{7,0},{8,9},{9,10},{10,1... | collective-permute-start | bytes 884744 | tf_op jit(solution)/shard_map/ppermute | solution.py:267
  27.7 17.3 %collective-permute-start.1 = (bf16[12,24,512]{2,1,0:T(8,128)(2,1)}, bf16[12,24,512]{2,1,0:T(8,128)(2,1)S(1)}, u32[]{:S(2)}, u32[]{:S(2)}) collective-permute-start(bf16[12,24,512]{2,1,0:T(8,128)(2,1)} %get-tuple-element.21), channel_id=1, source_target_pairs={{0,7},{1,0},{2,1},{3,2},{4,3},{5,4},{6,5},{7,6},{8,15},{9,8},{10,9... | collective-permute-start | bytes 884744 | tf_op jit(solution)/shard_map/ppermute | solution.py:268
  37.2 0.8 copy-start.7
  38.1 0.8 copy-start.9
  42.3 12.5 %collective-permute-start.12 = (bf16[24,24,512]{2,1,0:T(8,128)(2,1)}, bf16[24,24,512]{2,1,0:T(8,128)(2,1)S(1)}, u32[]{:S(2)}, u32[]{:S(2)}) collective-permute-start(bf16[24,24,512]{2,1,0:T(8,128)(2,1)} %get-tuple-element.32), channel_id=1, source_target_pairs={{0,1},{1,2},{2,3},{3,4},{4,5},{5,6},{6,7},{7,0},{8,9},{9,10},{10,1... | collective-permute-start | bytes 1769480 | tf_op jit(solution)/shard_map/ppermute | solution.py:267
  42.3 12.5 %collective-permute-start.13 = (bf16[24,24,512]{2,1,0:T(8,128)(2,1)}, bf16[24,24,512]{2,1,0:T(8,128)(2,1)S(1)}, u32[]{:S(2)}, u32[]{:S(2)}) collective-permute-start(bf16[24,24,512]{2,1,0:T(8,128)(2,1)} %get-tuple-element.33), channel_id=1, source_target_pairs={{0,7},{1,0},{2,1},{3,2},{4,3},{5,4},{6,5},{7,6},{8,15},{9,8},{10,9... | collective-permute-start | bytes 1769480 | tf_op jit(solution)/shard_map/ppermute | solution.py:268
  45.0 0.7 copy-start.12
  45.7 0.7 copy-start.13
  49.8 17.6 %collective-permute-start.2 = (bf16[24,24,512]{2,1,0:T(8,128)(2,1)}, bf16[24,24,512]{2,1,0:T(8,128)(2,1)S(1)}, u32[]{:S(2)}, u32[]{:S(2)}) collective-permute-start(bf16[24,24,512]{2,1,0:T(8,128)(2,1)} %get-tuple-element.22), channel_id=1, source_target_pairs={{0,1},{1,2},{2,3},{3,4},{4,5},{5,6},{6,7},{7,0},{8,9},{9,10},{10,1... | collective-permute-start | bytes 1769480 | tf_op jit(solution)/shard_map/ppermute | solution.py:267
  49.9 17.6 %collective-permute-start.3 = (bf16[24,24,512]{2,1,0:T(8,128)(2,1)}, bf16[24,24,512]{2,1,0:T(8,128)(2,1)S(1)}, u32[]{:S(2)}, u32[]{:S(2)}) collective-permute-start(bf16[24,24,512]{2,1,0:T(8,128)(2,1)} %get-tuple-element.23), channel_id=1, source_target_pairs={{0,7},{1,0},{2,1},{3,2},{4,3},{5,4},{6,5},{7,6},{8,15},{9,8},{10,9... | collective-permute-start | bytes 1769480 | tf_op jit(solution)/shard_map/ppermute | solution.py:268
  54.8 0.8 copy-start
  55.6 0.8 copy-start.3
  59.9 20.2 %collective-permute-start.14 = (bf16[24,24,512]{2,1,0:T(8,128)(2,1)}, bf16[24,24,512]{2,1,0:T(8,128)(2,1)S(1)}, u32[]{:S(2)}, u32[]{:S(2)}) collective-permute-start(bf16[24,24,512]{2,1,0:T(8,128)(2,1)} %get-tuple-element.34), channel_id=1, source_target_pairs={{0,1},{1,2},{2,3},{3,4},{4,5},{5,6},{6,7},{7,0},{8,9},{9,10},{10,1... | collective-permute-start | bytes 1769480 | tf_op jit(solution)/shard_map/ppermute | solution.py:267
  59.9 20.2 %collective-permute-start.15 = (bf16[24,24,512]{2,1,0:T(8,128)(2,1)}, bf16[24,24,512]{2,1,0:T(8,128)(2,1)S(1)}, u32[]{:S(2)}, u32[]{:S(2)}) collective-permute-start(bf16[24,24,512]{2,1,0:T(8,128)(2,1)} %get-tuple-element.35), channel_id=1, source_target_pairs={{0,7},{1,0},{2,1},{3,2},{4,3},{5,4},{6,5},{7,6},{8,15},{9,8},{10,9... | collective-permute-start | bytes 1769480 | tf_op jit(solution)/shard_map/ppermute | solution.py:268
  67.4 0.8 copy-start.1
  68.3 0.8 copy-start.4
  72.5 29.4 %collective-permute-start.4 = (bf16[24,24,512]{2,1,0:T(8,128)(2,1)}, bf16[24,24,512]{2,1,0:T(8,128)(2,1)S(1)}, u32[]{:S(2)}, u32[]{:S(2)}) collective-permute-start(bf16[24,24,512]{2,1,0:T(8,128)(2,1)} %get-tuple-element.24), channel_id=1, source_target_pairs={{0,1},{1,2},{2,3},{3,4},{4,5},{5,6},{6,7},{7,0},{8,9},{9,10},{10,1... | collective-permute-start | bytes 1769480 | tf_op jit(solution)/shard_map/ppermute | solution.py:267
  72.5 29.4 %collective-permute-start.5 = (bf16[24,24,512]{2,1,0:T(8,128)(2,1)}, bf16[24,24,512]{2,1,0:T(8,128)(2,1)S(1)}, u32[]{:S(2)}, u32[]{:S(2)}) collective-permute-start(bf16[24,24,512]{2,1,0:T(8,128)(2,1)} %get-tuple-element.25), channel_id=1, source_target_pairs={{0,7},{1,0},{2,1},{3,2},{4,3},{5,4},{6,5},{7,6},{8,15},{9,8},{10,9... | collective-permute-start | bytes 1769480 | tf_op jit(solution)/shard_map/ppermute | solution.py:268
  80.1 0.8 copy-start.2
  80.9 0.8 copy-start.5
  85.9 42.9 %all-to-all-start.1 = ((bf16[32,24,512]{2,1,0:T(8,128)(2,1)}), bf16[32,24,512]{2,1,0:T(8,128)(2,1)S(1)}, u32[]{:S(2)}, u32[]{:S(2)}) async-start(bf16[32,24,512]{2,1,0:T(8,128)(2,1)} %last_1.1), calls=%async_computation.1 | async-start | bytes 1572864 | tf_op jit(solution)/shard_map/all_to_all | solution.py:294
  101.9 0.8 copy-start.6
  102.8 0.8 copy-start.8
  107.0 16.1 %collective-permute-start.6 = (bf16[24,24,512]{2,1,0:T(8,128)(2,1)}, bf16[24,24,512]{2,1,0:T(8,128)(2,1)S(1)}, u32[]{:S(2)}, u32[]{:S(2)}) collective-permute-start(bf16[24,24,512]{2,1,0:T(8,128)(2,1)} %get-tuple-element.26), channel_id=1, source_target_pairs={{0,1},{1,2},{2,3},{3,4},{4,5},{5,6},{6,7},{7,0},{8,9},{9,10},{10,1... | collective-permute-start | bytes 1769480 | tf_op jit(solution)/shard_map/ppermute | solution.py:267
  107.9 15.2 %collective-permute-start.7 = (bf16[24,24,512]{2,1,0:T(8,128)(2,1)}, bf16[24,24,512]{2,1,0:T(8,128)(2,1)S(1)}, u32[]{:S(2)}, u32[]{:S(2)}) collective-permute-start(bf16[24,24,512]{2,1,0:T(8,128)(2,1)} %get-tuple-element.27), channel_id=1, source_target_pairs={{0,7},{1,0},{2,1},{3,2},{4,3},{5,4},{6,5},{7,6},{8,15},{9,8},{10,9... | collective-permute-start | bytes 1769480 | tf_op jit(solution)/shard_map/ppermute | solution.py:268
  123.1 0.8 copy-start.10
  123.9 0.8 copy-start.11
  128.8 8.1 %copy-start.17 = (s32[192]{0:T(256)S(1)}, s32[192]{0:T(256)}, u32[]{:S(2)}) copy-start(s32[192]{0:T(256)} %param.9) | copy-start | bytes 2308
  128.8 22.3 %all-to-all-start = ((bf16[32,24,512]{2,1,0:T(8,128)(2,1)}), bf16[32,24,512]{2,1,0:T(8,128)(2,1)S(1)}, u32[]{:S(2)}, u32[]{:S(2)}) async-start(bf16[32,24,512]{2,1,0:T(8,128)(2,1)} %last_0.1), calls=%async_computation | async-start | bytes 1572864 | tf_op jit(solution)/shard_map/all_to_all | solution.py:294
  161.4 19.0 %copy-start.16 = (s32[192]{0:T(256)S(1)}, s32[192]{0:T(256)}, u32[]{:S(2)}) copy-start(s32[192]{0:T(256)} %param.8) | copy-start | bytes 2308
  161.4 50.0 %all-to-all-start.2 = ((bf16[256,24,128]{2,1,0:T(8,128)(2,1)}), bf16[256,24,128]{2,1,0:T(8,128)(2,1)S(1)}, u32[]{:S(2)}, u32[]{:S(2)}) async-start(bf16[256,24,128]{2,1,0:T(8,128)(2,1)} %get-tuple-element.36), calls=%async_computation.2 | async-start | bytes 3145728 | tf_op jit(solution)/shard_map/all_to_all | solution.py:323
  169.3 3.1 %collective-permute-start.16 = (f32[1,8,128]{2,1,0:T(8,128)S(1)}, f32[1,8,128]{2,1,0:T(8,128)S(1)}, u32[]{:S(2)}, u32[]{:S(2)}) collective-permute-start(f32[1,8,128]{2,1,0:T(8,128)S(1)} %bitcast.26), channel_id=1, source_target_pairs={{0,8},{8,0},{16,24},{24,16},{32,40},{40,32},{48,56},{56,48},{64,72... | collective-permute-start | bytes 12296 | tf_op jit(solution)/shard_map/ppermute | solution.py:331
  172.4 3.1 %collective-permute-start.17 = (f32[2,8,128]{2,1,0:T(8,128)S(1)}, f32[2,8,128]{2,1,0:T(8,128)S(1)}, u32[]{:S(2)}, u32[]{:S(2)}) collective-permute-start(f32[2,8,128]{2,1,0:T(8,128)S(1)} %pad_maximum_fusion.4), channel_id=1, source_target_pairs={{0,16},{8,24},{16,0},{24,8},{32,48},{40,56},{48,32},{56,40},{64,80... | collective-permute-start | bytes 24584 | tf_op jit(solution)/shard_map/ppermute | solution.py:331
  175.5 4.8 %collective-permute-start.18 = (f32[4,8,128]{2,1,0:T(8,128)S(1)}, f32[4,8,128]{2,1,0:T(8,128)S(1)}, u32[]{:S(2)}, u32[]{:S(2)}) collective-permute-start(f32[4,8,128]{2,1,0:T(8,128)S(1)} %pad_maximum_fusion.2), channel_id=1, source_target_pairs={{0,32},{8,40},{16,48},{24,56},{32,0},{40,8},{48,16},{56,24},{64,96... | collective-permute-start | bytes 49160 | tf_op jit(solution)/shard_map/ppermute | solution.py:331
  180.3 3.7 %collective-permute-start.19 = (f32[8,8,128]{2,1,0:T(8,128)S(1)}, f32[8,8,128]{2,1,0:T(8,128)S(1)}, u32[]{:S(2)}, u32[]{:S(2)}) collective-permute-start(f32[8,8,128]{2,1,0:T(8,128)S(1)} %pad_maximum_fusion.1), channel_id=1, source_target_pairs={{0,64},{8,72},{16,80},{24,88},{32,96},{40,104},{48,112},{56,120},{... | collective-permute-start | bytes 98312 | tf_op jit(solution)/shard_map/ppermute | solution.py:331
  183.9 5.6 %collective-permute-start.20 = (f32[16,8,128]{2,1,0:T(8,128)S(1)}, f32[16,8,128]{2,1,0:T(8,128)S(1)}, u32[]{:S(2)}, u32[]{:S(2)}) collective-permute-start(f32[16,8,128]{2,1,0:T(8,128)S(1)} %pad_maximum_fusion), channel_id=1, source_target_pairs={{0,128},{8,136},{16,144},{24,152},{32,160},{40,168},{48,176},{56,1... | collective-permute-start | bytes 196616 | tf_op jit(solution)/shard_map/ppermute | solution.py:331

commit v2 on v1

v2 whole, which is shorter than its diff:
```python
import functools
import math

import jax
import jax.numpy as jnp
from jax import lax
from jax.experimental import pallas as pl
from jax.experimental.pallas import tpu as pltpu
from jax.sharding import PartitionSpec as P

F = 768
D = 1024
ITERS = 2
CAP = 2
STREAMS = 2


epsilon = 1e-07
first_coef = 3.4445
second_coef = -4.775
third_coef = 2.0315


def columns_of(table_ref, scratch, target, per_group):
    lanes = table_ref.shape[1]
    scratch[:, :lanes] = table_ref[...]
    wide = scratch.shape[1]
    return pltpu.roll(scratch[...], wide - target * per_group, axis=1)


def dequantized(codes, scales, shifts, k):
    return scales[:, k : k + 1] * (codes.astype(jnp.float32) + shifts[:, k : k + 1])


def hop_kernel(step, half, first_col, targets, codes, scales_ref, shifts_ref, *refs):
    received, (up_out, down_out), scratch = refs[: len(refs) - 5], refs[-5:-3], refs[-3:]
    held, table, sems = scratch
    per_group = 2 * half
    width = held.shape[3]
    parts = ((0, 1), (1, 0)) if step == 0 else ((0, 0), (1, 1), (0, 1), (1, 0))
    copies = []
    for index, (side, part) in enumerate(parts):
        start = targets[side] * per_group + (1 - part if step == 0 else part) * half
        copies.append(
            pltpu.make_async_copy(
                codes.at[pl.ds(start, half), :, pl.ds(first_col, width)],
                held.at[index],
                sems.at[index],
            )
        )
        copies[-1].start()
    tables = [
        [columns_of(ref, table, targets[side], per_group) for ref in (scales_ref, shifts_ref)]
        for side in range(2)
    ]
    for index, (side, part) in enumerate(parts):
        copies[index].wait()
        scales, shifts = tables[side]
        out = (up_out, down_out)[side]
        for k in range(half):
            if step == 0:
                value = dequantized(held[index, k], scales, shifts, (1 - part) * half + k)
                out[k] = value.astype(jnp.bfloat16)
                continue
            value = dequantized(held[index, k], scales, shifts, part * half + k)
            if step > 1:
                value = value + received[side][part * half + k].astype(jnp.float32)
            elif part == side:
                value = value + received[side][k].astype(jnp.float32)
            out[part * half + k] = value.astype(jnp.bfloat16)


def last_kernel(
    half, first_col, targets, codes, scales_ref, shifts_ref, up_in, down_in, out, held, table, sums, sems
):
    per_group = 2 * half
    width = held.shape[3]
    spare = sums.shape[0] - per_group
    copies = []
    for part in range(2):
        copies.append(
            pltpu.make_async_copy(
                codes.at[
                    pl.ds(targets[0] * per_group + part * half, half), :, pl.ds(first_col, width)
                ],
                held.at[part],
                sems.at[part],
            )
        )
        copies[-1].start()
    sums[per_group:] = jnp.zeros((spare,) + sums.shape[1:], sums.dtype)
    scales = columns_of(scales_ref, table, targets[0], per_group)
    shifts = columns_of(shifts_ref, table, targets[0], per_group)
    for part in range(2):
        copies[part].wait()
        for k in range(half):
            place = part * half + k
            value = dequantized(held[part, k], scales, shifts, place)
            value = value + (up_in[place].astype(jnp.float32) + down_in[place].astype(jnp.float32))
            sums[place] = value.astype(jnp.bfloat16)
    store = pltpu.make_async_copy(sums, out, sems.at[2])
    store.start()
    store.wait()


def newton_kernel(
    shard_rows, out_width, factor_ref, *refs
):
    pieces = refs[:STREAMS]
    out_ref, norm_ref, current, gram, poly = refs[STREAMS:]
    height, columns = current.shape
    width = columns // STREAMS
    tile = 8 * shard_rows
    tiles = height // tile
    total = jnp.zeros((1, 1), jnp.float32)
    for stream in range(STREAMS):
        value = pieces[stream][...].astype(jnp.float32)
        total = total + jnp.sum(value * value, keepdims=True)
    norm = jnp.sqrt(total)
    norm_ref[...] = jnp.broadcast_to(norm, norm_ref.shape)
    inverse = 1.0 / (norm + epsilon)
    for stream in range(STREAMS):
        value = pieces[stream][...].astype(jnp.float32)
        current[:, stream * width : (stream + 1) * width] = (value * inverse).astype(jnp.bfloat16)
    for sweep in range(ITERS):
        for i in range(tiles):
            rows = slice(i * tile, (i + 1) * tile)
            product = lax.dot_general(
                current[rows],
                current[...],
                (((1,), (1,)), ((), ())),
                preferred_element_type=jnp.float32,
            )
            gram[rows] = product.astype(jnp.bfloat16)
        for i in range(tiles):
            rows = slice(i * tile, (i + 1) * tile)
            squared = jnp.dot(gram[rows], gram[...], preferred_element_type=jnp.float32)
            poly[rows] = (
                second_coef * gram[rows].astype(jnp.float32) + third_coef * squared
            ).astype(jnp.bfloat16)
        if sweep < ITERS - 1:
            for c in range(columns // 256):
                cols = slice(c * 256, (c + 1) * 256)
                before = current[:, cols]
                product = jnp.dot(poly[...], before, preferred_element_type=jnp.float32)
                current[:, cols] = (
                    first_coef * before.astype(jnp.float32) + product
                ).astype(jnp.bfloat16)
    factor = factor_ref[0]
    per_column = height // shard_rows
    for c in range(columns // 256):
        cols = slice(c * 256, (c + 1) * 256)
        product = jnp.dot(poly[...], current[:, cols], preferred_element_type=jnp.float32)
        result = (first_coef * current[:, cols].astype(jnp.float32) + product).astype(jnp.bfloat16)
        scaled = (result.astype(jnp.float32) * factor).astype(jnp.bfloat16)
        for part in range(256 // out_width):
            first = ((c * 256) // out_width + part) * per_column
            piece = scaled[:, part * out_width : (part + 1) * out_width]
            out_ref[first : first + per_column] = piece.reshape(per_column, shard_rows, out_width)


def program(grad_codes, row_scales, dither, owner_table, matrix_kind):
    group_count = lax.axis_size("group")
    owner_count = lax.axis_size("dp")
    matrices = grad_codes.shape[1]
    per_group = matrices // group_count
    shard_rows = grad_codes.shape[2]
    columns = grad_codes.shape[3]
    height = shard_rows * owner_count
    half = per_group // 2
    width = columns // STREAMS
    out_width = columns // group_count
    reach = group_count // 2
    gate_factor = math.sqrt(max(F, D)) * math.sqrt(max(1.0, F / D))
    down_factor = math.sqrt(max(F, D)) * math.sqrt(max(1.0, D / F))
    norm_scale = 1.0 / math.sqrt(height * columns)
    group_index = lax.axis_index("group")
    owner_index = lax.axis_index("dp")
    up = [(i, (i + 1) % group_count) for i in range(group_count)]
    down = [(i, (i - 1) % group_count) for i in range(group_count)]
    codes = grad_codes[0]
    scales = row_scales[0].T
    shifts = dither[0].T
    whole = pl.BlockSpec(memory_space=pltpu.VMEM)
    anywhere = pl.BlockSpec(memory_space=pl.ANY)
    scalars = pl.BlockSpec(memory_space=pltpu.SMEM)
    table_scratch = pltpu.VMEM((shard_rows, 256), jnp.float32)

    def targets_at(distance):
        return jnp.stack(
            [
                lax.rem(group_index + distance, group_count),
                lax.rem(group_index + group_count - distance, group_count),
            ]
        ).astype(jnp.int32)

    def shape_of(count):
        return jax.ShapeDtypeStruct((count, shard_rows, width), jnp.bfloat16)

    def local(x):
        return pltpu.with_memory_space_constraint(x, pltpu.VMEM)

    def hop(step, stream, targets, received):
        count = half if step == 0 else per_group
        buffers = 2 if step == 0 else 4
        return pl.pallas_call(
            functools.partial(hop_kernel, step, half, stream * width),
            in_specs=[scalars, anywhere, whole, whole] + [whole] * len(received),
            out_specs=[whole, whole],
            out_shape=[pltpu.VMEM(shape_of(count).shape, jnp.bfloat16)] * 2,
            scratch_shapes=[
                pltpu.VMEM((buffers, half, shard_rows, width), jnp.bfloat16),
                table_scratch,
                pltpu.SemaphoreType.DMA((buffers,)),
            ],
            cost_estimate=pl.CostEstimate(
                flops=0, bytes_accessed=6 * count * shard_rows * width, transcendentals=0
            ),
        )(targets, codes, scales, shifts, *[local(x) for x in received])

    def send(blocks):
        rising = lax.ppermute(blocks[0], "group", up)
        falling = lax.ppermute(blocks[1], "group", down)
        return rising, falling

    pending = [()] * STREAMS
    previous = None
    for step in range(reach):
        for stream in range(STREAMS):
            targets = targets_at(reach - step)
            if previous is not None:
                targets, blocks = lax.optimization_barrier((targets, previous[2]))
                pending[previous[1]] = send(blocks)
            previous = (step, stream, hop(step, stream, targets, pending[stream]))
    targets, blocks = lax.optimization_barrier((targets_at(0), previous[2]))
    pending[previous[1]] = send(blocks)
    pieces = []
    for stream in range(STREAMS):
        padded = pl.pallas_call(
            functools.partial(last_kernel, half, stream * width),
            in_specs=[scalars, anywhere, whole, whole, whole, whole],
            out_specs=anywhere,
            out_shape=shape_of(owner_count),
            scratch_shapes=[
                pltpu.VMEM((2, half, shard_rows, width), jnp.bfloat16),
                table_scratch,
                pltpu.VMEM((owner_count, shard_rows, width), jnp.bfloat16),
                pltpu.SemaphoreType.DMA((3,)),
            ],
            cost_estimate=pl.CostEstimate(
                flops=0, bytes_accessed=6 * owner_count * shard_rows * width, transcendentals=0
            ),
        )(targets, codes, scales, shifts, *[local(x) for x in pending[stream]])
        targets, padded = lax.optimization_barrier((targets, padded))
        arrived = lax.all_to_all(padded, "dp", split_axis=0, concat_axis=0, tiled=True)
        pieces.append(arrived.reshape(height, width))

    owners = lax.dynamic_slice_in_dim(owner_table, group_index * per_group, per_group)
    place = group_index * per_group + jnp.minimum(owner_index, per_group - 1)
    kind = lax.dynamic_slice_in_dim(matrix_kind, place, 1)
    factor = jnp.where(kind == 1, down_factor, gate_factor).astype(jnp.float32)
    blocks_out, norms = pl.pallas_call(
        functools.partial(newton_kernel, shard_rows, out_width),
        in_specs=[scalars] + [whole] * STREAMS,
        out_specs=[whole, whole],
        out_shape=[
            jax.ShapeDtypeStruct((group_count * owner_count, shard_rows, out_width), jnp.bfloat16),
            jax.ShapeDtypeStruct((8, 128), jnp.float32),
        ],
        scratch_shapes=[
            pltpu.VMEM((height, columns), jnp.bfloat16),
            pltpu.VMEM((height, height), jnp.bfloat16),
            pltpu.VMEM((height, height), jnp.bfloat16),
        ],
        name="newton",
        cost_estimate=pl.CostEstimate(
            flops=2 * ITERS * height * height * (2 * columns + height),
            bytes_accessed=4 * height * columns,
            transcendentals=0,
        ),
        compiler_params=pltpu.CompilerParams(vmem_limit_bytes=40 * 1024 * 1024),
    )(factor, *pieces)
    returned = lax.all_to_all(blocks_out, ("group", "dp"), split_axis=0, concat_axis=0, tiled=True)
    returned = returned.reshape(group_count, owner_count, shard_rows, out_width)
    updates = returned[:, :per_group].reshape(matrices, shard_rows, out_width)

    norms = norms[None]
    stride = 1
    while stride < owner_count:
        partner = [(i, i ^ stride) for i in range(owner_count)]
        other = lax.ppermute(norms, "dp", partner)
        low = (owner_index & stride) == 0
        norms = jnp.concatenate([jnp.where(low, norms, other), jnp.where(low, other, norms)])
        stride *= 2
    all_norms = norms[:per_group, 0, 0]
    position = jnp.arange(per_group, dtype=jnp.int32)
    same_owner = owners[:, None] == owners[None, :]
    earlier = position[None, :] < position[:, None]
    slot_of = jnp.sum((same_owner & earlier).astype(jnp.int32), 1)
    slot_hit = slot_of[:, None] == jnp.arange(CAP, dtype=jnp.int32)[None, :]
    owned_slot = (owners == owner_index)[:, None] & slot_hit
    slot_norms = jnp.sum(jnp.where(owned_slot, all_norms[:, None] * norm_scale, 0.0), 0)
    return (updates, slot_norms.reshape(1, 1, CAP))


def solution(mesh):
    placed = (
        P("group", None, "dp", None),
        P("group", None, "dp"),
        P("group", None, "dp"),
        P(),
        P(),
    )
    return jax.shard_map(
        program,
        mesh=mesh,
        in_specs=placed,
        out_specs=(P(None, "dp", "group"), P("group", "dp", None)),
        check_vma=False,
    )
```

time: 213 us -> 205 us (0.962)
  blocking collectives: 0 us -> 24.2 us
  starting transfers between devices: 61.3 us -> 41.8 us
  local copies, waits for them, and re-layouts: 14.4 us -> 4.5 us
  Pallas kernels: 44.6 us -> 40 us
    all_to_all x0 -> x1, blocking collectives: none -> 24.2 us  [program(): lax.all_to_all(padded, 'dp', split_axis=0, concat_axis=0, tiled=True)]
    all_to_all x3 -> x2, starting transfers between devices: 32.1 us -> 11.9 us  [the longest x1 7.96 us: program(): lax.all_to_all(blocks_out, ('group', 'dp'), split_axis=0, concat_axis=0,...]
    unnamed x36 -> x10, local copies, waits for them, and re-layouts: 12.6 us -> 2.7 us
    pallas_call x11, Pallas kernels: 44.6 us -> 40 us  [the longest x8 23.9 us: hop(): pl.pallas_call(functools.partial(hop_kernel, step, half, stream * width),...]
    all_to_all x3 -> x2, waiting for transfers between devices: 33.8 us -> 33.7 us  [the longest x1 20.9 us: program(): lax.all_to_all(blocks_out, ('group', 'dp'), split_axis=0, concat_axis=0,...]
  transfers between devices with their start and end apart: 24 -> 23, of which waited for: 13 -> 15; matrix products, arithmetic and copies ran while one was open for 2% -> 2% of each run, Pallas kernels for 13% -> 12%
where the time goes in v2:
time: 205 us; the launch traced here: 204 us
  waiting for transfers between devices  87.8 us (43%)
  starting transfers between devices  41.8 us (20%)
  Pallas kernels  40 us (20%)
  blocking collectives  24.2 us (12%)
  local copies, waits for them, and re-layouts  4.5 us (2%)
  other arithmetic  4.18 us (2%)
    ppermute x8, waiting for transfers between devices, send(): rising = lax.ppermute(blocks[0], 'group', up)  38.3 us
    all_to_all x1, blocking collectives, program(): lax.all_to_all(padded, 'dp', split_axis=0, concat_axis=0, tiled=True)  24.2 us
    pallas_call x8, Pallas kernels, hop(): pl.pallas_call(functools.partial(hop_kernel, step, half, stream * width),...  23.9 us
    all_to_all x1, waiting for transfers between devices, program(): lax.all_to_all(blocks_out, ('group', 'dp'), split_axis=0, concat_axis=0,...  20.9 us
    ppermute x8, starting transfers between devices, send(): falling = lax.ppermute(blocks[1], 'group', down)  18.7 us
    ppermute x5, waiting for transfers between devices, program(): other = lax.ppermute(norms, 'dp', partner)  15.8 us
    all_to_all x1, waiting for transfers between devices, program(): lax.all_to_all(padded, 'dp', split_axis=0, concat_axis=0, tiled=True)  12.8 us
    pallas_call x1, Pallas kernels, program(): pl.pallas_call(functools.partial(newton_kernel, shard_rows, out_width), i...  10.2 us
  transfers between devices with their start and end apart: 23, of which 15 were waited for; matrix products, arithmetic and copies ran while one was open for 2% of the time, Pallas kernels for 12%

profile of v2, /device:TPU:1, one launch (start us, length us, event | category | flops | bytes accessed | tf_op | source)
XLA Modules:
  0.0 204.1 jit_solution(17044844228270752344)
XLA Ops:
  0.6 0.7 pad_add_fusion.4.targets
  1.3 2.1 %shard_map.68 = (bf16[12,24,512]{2,1,0:T(8,128)(2,1)S(1)}, bf16[12,24,512]{2,1,0:T(8,128)(2,1)S(1)}) custom-call(s32[2]{0:T(128)} %pad_add_fusion.4.targets, bf16[192,24,1024]{2,1,0:T(8,128)(2,1)} %bitcast.27, f32[24,192]{1,0:T(8,128)} %bitcast.38, f32[24,192]{1,0:T(8,128)} %bitcast.48), custom_call_target="tpu_custom_call" | custom-call | bytes 884736 | tf_op jit(solution)/shard_map/pallas_call | solution.py:206
  3.4 2.5 %collective-permute-start = (bf16[12,24,512]{2,1,0:T(8,128)(2,1)S(1)}, bf16[12,24,512]{2,1,0:T(8,128)(2,1)S(1)}, u32[]{:S(2)}, u32[]{:S(2)}) collective-permute-start(bf16[12,24,512]{2,1,0:T(8,128)(2,1)S(1)} %get-tuple-element.53), channel_id=1, source_target_pairs={{0,1},{1,2},{2,3},{3,4},{4,5},{5,6},{6,7},{7,0},{8,9},{9,10},{10,1... | collective-permute-start | bytes 884744 | tf_op jit(solution)/shard_map/ppermute | solution.py:222
  5.9 4.0 %collective-permute-start.1 = (bf16[12,24,512]{2,1,0:T(8,128)(2,1)S(1)}, bf16[12,24,512]{2,1,0:T(8,128)(2,1)S(1)}, u32[]{:S(2)}, u32[]{:S(2)}) collective-permute-start(bf16[12,24,512]{2,1,0:T(8,128)(2,1)S(1)} %get-tuple-element.54), channel_id=1, source_target_pairs={{0,7},{1,0},{2,1},{3,2},{4,3},{5,4},{6,5},{7,6},{8,15},{9,8},{10,9... | collective-permute-start | bytes 884744 | tf_op jit(solution)/shard_map/ppermute | solution.py:223
  10.5 2.1 %shard_map.69 = (bf16[12,24,512]{2,1,0:T(8,128)(2,1)S(1)}, bf16[12,24,512]{2,1,0:T(8,128)(2,1)S(1)}) custom-call(s32[2]{0:T(128)} %pad_add_fusion.4.targets, bf16[192,24,1024]{2,1,0:T(8,128)(2,1)} %bitcast.28, f32[24,192]{1,0:T(8,128)} %bitcast.39, f32[24,192]{1,0:T(8,128)} %bitcast.49), custom_call_target="tpu_custom_call" | custom-call | bytes 884736 | tf_op jit(solution)/shard_map/pallas_call | solution.py:206
  12.7 2.7 %collective-permute-start.3 = (bf16[12,24,512]{2,1,0:T(8,128)(2,1)S(1)}, bf16[12,24,512]{2,1,0:T(8,128)(2,1)S(1)}, u32[]{:S(2)}, u32[]{:S(2)}) collective-permute-start(bf16[12,24,512]{2,1,0:T(8,128)(2,1)S(1)} %get-tuple-element.59), channel_id=1, source_target_pairs={{0,7},{1,0},{2,1},{3,2},{4,3},{5,4},{6,5},{7,6},{8,15},{9,8},{10,9... | collective-permute-start | bytes 884744 | tf_op jit(solution)/shard_map/ppermute | solution.py:223
  16.6 3.3 %shard_map.70 = (bf16[24,24,512]{2,1,0:T(8,128)(2,1)}, bf16[24,24,512]{2,1,0:T(8,128)(2,1)}) custom-call(s32[2]{0:T(128)} %pad_add_fusion.3.targets, bf16[192,24,1024]{2,1,0:T(8,128)(2,1)} %bitcast.29, f32[24,192]{1,0:T(8,128)} %bitcast.40, f32[24,192]{1,0:T(8,128)} %bitcast.50, bf16[12,24,512]{2,1,0:T(8,128)(2,1)S(1)} %collective-permute-done.refs_0_, ...), custom_call_target="tpu_custom_call" | custom-call | bytes 1769472 | tf_op jit(solution)/shard_map/pallas_call | solution.py:206
  20.0 2.7 %collective-permute-start.5 = (bf16[24,24,512]{2,1,0:T(8,128)(2,1)}, bf16[24,24,512]{2,1,0:T(8,128)(2,1)S(1)}, u32[]{:S(2)}, u32[]{:S(2)}) collective-permute-start(bf16[24,24,512]{2,1,0:T(8,128)(2,1)} %get-tuple-element.64), channel_id=1, source_target_pairs={{0,7},{1,0},{2,1},{3,2},{4,3},{5,4},{6,5},{7,6},{8,15},{9,8},{10,9... | collective-permute-start | bytes 1769480 | tf_op jit(solution)/shard_map/ppermute | solution.py:223
  23.0 3.3 %shard_map.71 = (bf16[24,24,512]{2,1,0:T(8,128)(2,1)}, bf16[24,24,512]{2,1,0:T(8,128)(2,1)}) custom-call(s32[2]{0:T(128)} %pad_add_fusion.3.targets, bf16[192,24,1024]{2,1,0:T(8,128)(2,1)} %bitcast.30, f32[24,192]{1,0:T(8,128)} %bitcast.41, f32[24,192]{1,0:T(8,128)} %bitcast.51, bf16[12,24,512]{2,1,0:T(8,128)(2,1)S(1)} %collective-permute-done.2.refs_0_, ...), custom_call_target="tpu_custom_call" | custom-call | bytes 1769472 | tf_op jit(solution)/shard_map/pallas_call | solution.py:206
  26.4 2.7 %collective-permute-start.7 = (bf16[24,24,512]{2,1,0:T(8,128)(2,1)}, bf16[24,24,512]{2,1,0:T(8,128)(2,1)S(1)}, u32[]{:S(2)}, u32[]{:S(2)}) collective-permute-start(bf16[24,24,512]{2,1,0:T(8,128)(2,1)} %get-tuple-element.69), channel_id=1, source_target_pairs={{0,7},{1,0},{2,1},{3,2},{4,3},{5,4},{6,5},{7,6},{8,15},{9,8},{10,9... | collective-permute-start | bytes 1769480 | tf_op jit(solution)/shard_map/ppermute | solution.py:223
  29.7 4.6 %collective-permute-done.4.refs_0_ = bf16[24,24,512]{2,1,0:T(8,128)(2,1)S(1)} collective-permute-done((bf16[24,24,512]{2,1,0:T(8,128)(2,1)}, bf16[24,24,512]{2,1,0:T(8,128)(2,1)S(1)}, u32[]{:S(2)}, u32[]{:S(2)}) %collective-permute-start.4) | collective-permute-done | bytes 589856 | tf_op jit(solution)/shard_map/ppermute | solution.py:222
  34.2 0.8 copy-done
  35.0 1.1 copy-done.1
  36.1 3.3 %shard_map.72 = (bf16[24,24,512]{2,1,0:T(8,128)(2,1)}, bf16[24,24,512]{2,1,0:T(8,128)(2,1)}) custom-call(s32[2]{0:T(128)} %pad_add_fusion.2.targets, bf16[192,24,1024]{2,1,0:T(8,128)(2,1)} %bitcast.31, f32[24,192]{1,0:T(8,128)} %bitcast.42, f32[24,192]{1,0:T(8,128)} %bitcast.52, bf16[24,24,512]{2,1,0:T(8,128)(2,1)S(1)} %collective-permute-done.4.refs_0_, ...), custom_call_target="tpu_custom_call" | custom-call | bytes 1769472 | tf_op jit(solution)/shard_map/pallas_call | solution.py:206
  39.4 1.0 collective-permute-start.8
  40.5 1.7 collective-permute-start.9
  42.2 4.7 %collective-permute-done.6.refs_0_ = bf16[24,24,512]{2,1,0:T(8,128)(2,1)S(1)} collective-permute-done((bf16[24,24,512]{2,1,0:T(8,128)(2,1)}, bf16[24,24,512]{2,1,0:T(8,128)(2,1)S(1)}, u32[]{:S(2)}, u32[]{:S(2)}) %collective-permute-start.6) | collective-permute-done | bytes 589856 | tf_op jit(solution)/shard_map/ppermute | solution.py:222
  46.9 3.3 %shard_map.73 = (bf16[24,24,512]{2,1,0:T(8,128)(2,1)}, bf16[24,24,512]{2,1,0:T(8,128)(2,1)}) custom-call(s32[2]{0:T(128)} %pad_add_fusion.2.targets, bf16[192,24,1024]{2,1,0:T(8,128)(2,1)} %bitcast.32, f32[24,192]{1,0:T(8,128)} %bitcast.43, f32[24,192]{1,0:T(8,128)} %bitcast.53, bf16[24,24,512]{2,1,0:T(8,128)(2,1)S(1)} %collective-permute-done.6.refs_0_, ...), custom_call_target="tpu_custom_call" | custom-call | bytes 1769472 | tf_op jit(solution)/shard_map/pallas_call | solution.py:206
  50.2 1.0 collective-permute-start.10
  51.2 1.7 collective-permute-start.11
  53.5 6.0 %collective-permute-done.8.refs_0_ = bf16[24,24,512]{2,1,0:T(8,128)(2,1)S(1)} collective-permute-done((bf16[24,24,512]{2,1,0:T(8,128)(2,1)}, bf16[24,24,512]{2,1,0:T(8,128)(2,1)S(1)}, u32[]{:S(2)}, u32[]{:S(2)}) %collective-permute-start.8) | collective-permute-done | bytes 589856 | tf_op jit(solution)/shard_map/ppermute | solution.py:222
  59.5 3.7 %shard_map.74 = (bf16[24,24,512]{2,1,0:T(8,128)(2,1)}, bf16[24,24,512]{2,1,0:T(8,128)(2,1)}) custom-call(s32[2]{0:T(128)} %pad_add_fusion.1.targets, bf16[192,24,1024]{2,1,0:T(8,128)(2,1)} %bitcast.33, f32[24,192]{1,0:T(8,128)} %bitcast.44, f32[24,192]{1,0:T(8,128)} %bitcast.54, bf16[24,24,512]{2,1,0:T(8,128)(2,1)S(1)} %collective-permute-done.8.refs_0_, ...), custom_call_target="tpu_custom_call" | custom-call | bytes 1769472 | tf_op jit(solution)/shard_map/pallas_call | solution.py:206
  63.2 1.2 collective-permute-start.12
  64.3 1.6 collective-permute-start.13
  65.9 6.2 %collective-permute-done.10.refs_0_ = bf16[24,24,512]{2,1,0:T(8,128)(2,1)S(1)} collective-permute-done((bf16[24,24,512]{2,1,0:T(8,128)(2,1)}, bf16[24,24,512]{2,1,0:T(8,128)(2,1)S(1)}, u32[]{:S(2)}, u32[]{:S(2)}) %collective-permute-start.10) | collective-permute-done | bytes 589856 | tf_op jit(solution)/shard_map/ppermute | solution.py:222
  72.1 2.8 %shard_map.75 = (bf16[24,24,512]{2,1,0:T(8,128)(2,1)S(1)}, bf16[24,24,512]{2,1,0:T(8,128)(2,1)S(1)}) custom-call(s32[2]{0:T(128)} %pad_add_fusion.1.targets, bf16[192,24,1024]{2,1,0:T(8,128)(2,1)} %bitcast.34, f32[24,192]{1,0:T(8,128)} %bitcast.45, f32[24,192]{1,0:T(8,128)} %bitcast.55, bf16[24,24,512]{2,1,0:T(8,128)(2,1)S(1)} %collective-permute-done.10.refs_0_, ...), custom_call_target="tpu_custom_call" | custom-call | bytes 1769472 | tf_op jit(solution)/shard_map/pallas_call | solution.py:206
  75.0 0.8 copy-done.2
  75.8 1.1 collective-permute-start.14
  76.9 1.6 collective-permute-start.15
  78.5 6.3 %collective-permute-done.12.up_in = bf16[24,24,512]{2,1,0:T(8,128)(2,1)S(1)} collective-permute-done((bf16[24,24,512]{2,1,0:T(8,128)(2,1)}, bf16[24,24,512]{2,1,0:T(8,128)(2,1)S(1)}, u32[]{:S(2)}, u32[]{:S(2)}) %collective-permute-start.12) | collective-permute-done | bytes 589856 | tf_op jit(solution)/shard_map/ppermute | solution.py:222
  84.8 3.0 %shard_map.76 = bf16[32,24,512]{2,1,0:T(8,128)(2,1)} custom-call(s32[2]{0:T(128)} %pad_add_fusion.targets, bf16[192,24,1024]{2,1,0:T(8,128)(2,1)} %bitcast.35, f32[24,192]{1,0:T(8,128)} %bitcast.46, f32[24,192]{1,0:T(8,128)} %bitcast.56, bf16[24,24,512]{2,1,0:T(8,128)(2,1)S(1)} %collective-permute-done.12.up_in, ...), custom_call_target="tpu_custom_call" | custom-call | bytes 2359296 | tf_op jit(solution)/shard_map/pallas_call | solution.py:239
  87.8 9.7 %collective-permute-done.14.up_in = bf16[24,24,512]{2,1,0:T(8,128)(2,1)S(1)} collective-permute-done((bf16[24,24,512]{2,1,0:T(8,128)(2,1)}, bf16[24,24,512]{2,1,0:T(8,128)(2,1)S(1)}, u32[]{:S(2)}, u32[]{:S(2)}) %collective-permute-start.14) | collective-permute-done | bytes 589856 | tf_op jit(solution)/shard_map/ppermute | solution.py:222
  97.4 3.0 %shard_map.77 = bf16[32,24,512]{2,1,0:T(8,128)(2,1)} custom-call(s32[2]{0:T(128)} %pad_add_fusion.targets, bf16[192,24,1024]{2,1,0:T(8,128)(2,1)} %bitcast.36, f32[24,192]{1,0:T(8,128)} %bitcast.47, f32[24,192]{1,0:T(8,128)} %bitcast.57, bf16[24,24,512]{2,1,0:T(8,128)(2,1)S(1)} %collective-permute-done.14.up_in, ...), custom_call_target="tpu_custom_call" | custom-call | bytes 2359296 | tf_op jit(solution)/shard_map/pallas_call | solution.py:239
  100.4 24.2 %all_to_all.15 = bf16[32,24,512]{2,1,0:T(8,128)(2,1)S(1)} all-to-all(bf16[32,24,512]{2,1,0:T(8,128)(2,1)} %shard_map.77), channel_id=1, replica_groups=mesh['dp'=32,'group'=8] {'dp'}, dimensions={0} | all-to-all | bytes 1572864 | tf_op jit(solution)/shard_map/all_to_all | solution.py:255
  124.6 3.9 %all-to-all-start = ((bf16[32,24,512]{2,1,0:T(8,128)(2,1)}), bf16[32,24,512]{2,1,0:T(8,128)(2,1)S(1)}, u32[]{:S(2)}, u32[]{:S(2)}) async-start(bf16[32,24,512]{2,1,0:T(8,128)(2,1)} %shard_map.76), calls=%async_computation | async-start | bytes 1572864 | tf_op jit(solution)/shard_map/all_to_all | solution.py:255
  129.8 12.8 %all-to-all-done = bf16[32,24,512]{2,1,0:T(8,128)(2,1)S(1)} async-done(((bf16[32,24,512]{2,1,0:T(8,128)(2,1)}), bf16[32,24,512]{2,1,0:T(8,128)(2,1)S(1)}, u32[]{:S(2)}, u32[]{:S(2)}) %all-to-all-start) | async-done | bytes 786464 | tf_op jit(solution)/shard_map/all_to_all | solution.py:255
  142.7 10.2 %newton.1 = (bf16[256,24,128]{2,1,0:T(8,128)(2,1)}, f32[8,128]{1,0:T(8,128)S(1)}) custom-call(f32[1]{0:T(128)S(6)} %select_n.75.factor_ref, bf16[768,512]{1,0:T(8,128)(2,1)S(1)} %bitcast.25, bf16[768,512]{1,0:T(8,128)(2,1)S(1)} %bitcast.24), custom_call_target="tpu_custom_call" | custom-call | flops 6643777536 | bytes 3145728 | tf_op jit(solution)/shard_map/newton/pallas_call | solution.py:262
  152.9 8.0 %all-to-all-start.2 = ((bf16[256,24,128]{2,1,0:T(8,128)(2,1)}), bf16[256,24,128]{2,1,0:T(8,128)(2,1)S(1)}, u32[]{:S(2)}, u32[]{:S(2)}) async-start(bf16[256,24,128]{2,1,0:T(8,128)(2,1)} %get-tuple-element.90), calls=%async_computation.2 | async-start | bytes 3145728 | tf_op jit(solution)/shard_map/all_to_all | solution.py:283
  160.8 2.2 %collective-permute-start.16 = (f32[1,8,128]{2,1,0:T(8,128)S(1)}, f32[1,8,128]{2,1,0:T(8,128)S(1)}, u32[]{:S(2)}, u32[]{:S(2)}) collective-permute-start(f32[1,8,128]{2,1,0:T(8,128)S(1)} %bitcast.26), channel_id=1, source_target_pairs={{0,8},{8,0},{16,24},{24,16},{32,40},{40,32},{48,56},{56,48},{64,72... | collective-permute-start | bytes 12296 | tf_op jit(solution)/shard_map/ppermute | solution.py:291
  163.1 0.8 collective-permute-done.16
  163.9 3.1 %collective-permute-done.17 = f32[2,8,128]{2,1,0:T(8,128)S(1)} collective-permute-done((f32[2,8,128]{2,1,0:T(8,128)S(1)}, f32[2,8,128]{2,1,0:T(8,128)S(1)}, u32[]{:S(2)}, u32[]{:S(2)}) %collective-permute-start.17) | collective-permute-done | bytes 8224 | tf_op jit(solution)/shard_map/ppermute | solution.py:291
  167.0 1.3 collective-permute-start.18
  168.3 3.4 %collective-permute-done.18 = f32[4,8,128]{2,1,0:T(8,128)S(1)} collective-permute-done((f32[4,8,128]{2,1,0:T(8,128)S(1)}, f32[4,8,128]{2,1,0:T(8,128)S(1)}, u32[]{:S(2)}, u32[]{:S(2)}) %collective-permute-start.18) | collective-permute-done | bytes 16416 | tf_op jit(solution)/shard_map/ppermute | solution.py:291
  172.0 3.5 %collective-permute-done.19 = f32[8,8,128]{2,1,0:T(8,128)S(1)} collective-permute-done((f32[8,8,128]{2,1,0:T(8,128)S(1)}, f32[8,8,128]{2,1,0:T(8,128)S(1)}, u32[]{:S(2)}, u32[]{:S(2)}) %collective-permute-start.19) | collective-permute-done | bytes 32800 | tf_op jit(solution)/shard_map/ppermute | solution.py:291
  176.0 5.0 %collective-permute-done.20 = f32[16,8,128]{2,1,0:T(8,128)S(1)} collective-permute-done((f32[16,8,128]{2,1,0:T(8,128)S(1)}, f32[16,8,128]{2,1,0:T(8,128)S(1)}, u32[]{:S(2)}, u32[]{:S(2)}) %collective-permute-start.20) | collective-permute-done | bytes 65568 | tf_op jit(solution)/shard_map/ppermute | solution.py:291
  181.3 0.6 fusion.3
  182.0 20.9 %all-to-all-done.2 = bf16[256,24,128]{2,1,0:T(8,128)(2,1)S(1)} async-done(((bf16[256,24,128]{2,1,0:T(8,128)(2,1)}), bf16[256,24,128]{2,1,0:T(8,128)(2,1)S(1)}, u32[]{:S(2)}, u32[]{:S(2)}) %all-to-all-start.2) | async-done | bytes 1572896 | tf_op jit(solution)/shard_map/all_to_all | solution.py:283
  202.8 1.2 slice.8
  (40 shorter events, 5.2 us)
Async XLA Ops:
  3.4 13.2 %collective-permute-start = (bf16[12,24,512]{2,1,0:T(8,128)(2,1)S(1)}, bf16[12,24,512]{2,1,0:T(8,128)(2,1)S(1)}, u32[]{:S(2)}, u32[]{:S(2)}) collective-permute-start(bf16[12,24,512]{2,1,0:T(8,128)(2,1)S(1)} %get-tuple-element.53), channel_id=1, source_target_pairs={{0,1},{1,2},{2,3},{3,4},{4,5},{5,6},{6,7},{7,0},{8,9},{9,10},{10,1... | collective-permute-start | bytes 884744 | tf_op jit(solution)/shard_map/ppermute | solution.py:222
  5.9 10.7 %collective-permute-start.1 = (bf16[12,24,512]{2,1,0:T(8,128)(2,1)S(1)}, bf16[12,24,512]{2,1,0:T(8,128)(2,1)S(1)}, u32[]{:S(2)}, u32[]{:S(2)}) collective-permute-start(bf16[12,24,512]{2,1,0:T(8,128)(2,1)S(1)} %get-tuple-element.54), channel_id=1, source_target_pairs={{0,7},{1,0},{2,1},{3,2},{4,3},{5,4},{6,5},{7,6},{8,15},{9,8},{10,9... | collective-permute-start | bytes 884744 | tf_op jit(solution)/shard_map/ppermute | solution.py:223
  12.6 10.3 %collective-permute-start.2 = (bf16[12,24,512]{2,1,0:T(8,128)(2,1)S(1)}, bf16[12,24,512]{2,1,0:T(8,128)(2,1)S(1)}, u32[]{:S(2)}, u32[]{:S(2)}) collective-permute-start(bf16[12,24,512]{2,1,0:T(8,128)(2,1)S(1)} %get-tuple-element.58), channel_id=1, source_target_pairs={{0,1},{1,2},{2,3},{3,4},{4,5},{5,6},{6,7},{7,0},{8,9},{9,10},{10,1... | collective-permute-start | bytes 884744 | tf_op jit(solution)/shard_map/ppermute | solution.py:222
  12.7 10.2 %collective-permute-start.3 = (bf16[12,24,512]{2,1,0:T(8,128)(2,1)S(1)}, bf16[12,24,512]{2,1,0:T(8,128)(2,1)S(1)}, u32[]{:S(2)}, u32[]{:S(2)}) collective-permute-start(bf16[12,24,512]{2,1,0:T(8,128)(2,1)S(1)} %get-tuple-element.59), channel_id=1, source_target_pairs={{0,7},{1,0},{2,1},{3,2},{4,3},{5,4},{6,5},{7,6},{8,15},{9,8},{10,9... | collective-permute-start | bytes 884744 | tf_op jit(solution)/shard_map/ppermute | solution.py:223
  19.9 14.4 %collective-permute-start.4 = (bf16[24,24,512]{2,1,0:T(8,128)(2,1)}, bf16[24,24,512]{2,1,0:T(8,128)(2,1)S(1)}, u32[]{:S(2)}, u32[]{:S(2)}) collective-permute-start(bf16[24,24,512]{2,1,0:T(8,128)(2,1)} %get-tuple-element.63), channel_id=1, source_target_pairs={{0,1},{1,2},{2,3},{3,4},{4,5},{5,6},{6,7},{7,0},{8,9},{9,10},{10,1... | collective-permute-start | bytes 1769480 | tf_op jit(solution)/shard_map/ppermute | solution.py:222
  20.0 14.3 %collective-permute-start.5 = (bf16[24,24,512]{2,1,0:T(8,128)(2,1)}, bf16[24,24,512]{2,1,0:T(8,128)(2,1)S(1)}, u32[]{:S(2)}, u32[]{:S(2)}) collective-permute-start(bf16[24,24,512]{2,1,0:T(8,128)(2,1)} %get-tuple-element.64), channel_id=1, source_target_pairs={{0,7},{1,0},{2,1},{3,2},{4,3},{5,4},{6,5},{7,6},{8,15},{9,8},{10,9... | collective-permute-start | bytes 1769480 | tf_op jit(solution)/shard_map/ppermute | solution.py:223
  26.3 20.6 %collective-permute-start.6 = (bf16[24,24,512]{2,1,0:T(8,128)(2,1)}, bf16[24,24,512]{2,1,0:T(8,128)(2,1)S(1)}, u32[]{:S(2)}, u32[]{:S(2)}) collective-permute-start(bf16[24,24,512]{2,1,0:T(8,128)(2,1)} %get-tuple-element.68), channel_id=1, source_target_pairs={{0,1},{1,2},{2,3},{3,4},{4,5},{5,6},{6,7},{7,0},{8,9},{9,10},{10,1... | collective-permute-start | bytes 1769480 | tf_op jit(solution)/shard_map/ppermute | solution.py:222
  26.4 20.5 %collective-permute-start.7 = (bf16[24,24,512]{2,1,0:T(8,128)(2,1)}, bf16[24,24,512]{2,1,0:T(8,128)(2,1)S(1)}, u32[]{:S(2)}, u32[]{:S(2)}) collective-permute-start(bf16[24,24,512]{2,1,0:T(8,128)(2,1)} %get-tuple-element.69), channel_id=1, source_target_pairs={{0,7},{1,0},{2,1},{3,2},{4,3},{5,4},{6,5},{7,6},{8,15},{9,8},{10,9... | collective-permute-start | bytes 1769480 | tf_op jit(solution)/shard_map/ppermute | solution.py:223
  34.2 0.8 copy-start
  35.0 1.1 copy-start.1
  39.4 20.1 %collective-permute-start.8 = (bf16[24,24,512]{2,1,0:T(8,128)(2,1)}, bf16[24,24,512]{2,1,0:T(8,128)(2,1)S(1)}, u32[]{:S(2)}, u32[]{:S(2)}) collective-permute-start(bf16[24,24,512]{2,1,0:T(8,128)(2,1)} %get-tuple-element.73), channel_id=1, source_target_pairs={{0,1},{1,2},{2,3},{3,4},{4,5},{5,6},{6,7},{7,0},{8,9},{9,10},{10,1... | collective-permute-start | bytes 1769480 | tf_op jit(solution)/shard_map/ppermute | solution.py:222
  40.5 19.0 %collective-permute-start.9 = (bf16[24,24,512]{2,1,0:T(8,128)(2,1)}, bf16[24,24,512]{2,1,0:T(8,128)(2,1)}, u32[]{:S(2)}, u32[]{:S(2)}) collective-permute-start(bf16[24,24,512]{2,1,0:T(8,128)(2,1)} %get-tuple-element.74), channel_id=1, source_target_pairs={{0,7},{1,0},{2,1},{3,2},{4,3},{5,4},{6,5},{7,6},{8,15},{9,8},{10,9... | collective-permute-start | bytes 1769480 | tf_op jit(solution)/shard_map/ppermute | solution.py:223
  50.2 22.0 %collective-permute-start.10 = (bf16[24,24,512]{2,1,0:T(8,128)(2,1)}, bf16[24,24,512]{2,1,0:T(8,128)(2,1)S(1)}, u32[]{:S(2)}, u32[]{:S(2)}) collective-permute-start(bf16[24,24,512]{2,1,0:T(8,128)(2,1)} %get-tuple-element.78), channel_id=1, source_target_pairs={{0,1},{1,2},{2,3},{3,4},{4,5},{5,6},{6,7},{7,0},{8,9},{9,10},{10,1... | collective-permute-start | bytes 1769480 | tf_op jit(solution)/shard_map/ppermute | solution.py:222
  51.2 20.9 %collective-permute-start.11 = (bf16[24,24,512]{2,1,0:T(8,128)(2,1)}, bf16[24,24,512]{2,1,0:T(8,128)(2,1)}, u32[]{:S(2)}, u32[]{:S(2)}) collective-permute-start(bf16[24,24,512]{2,1,0:T(8,128)(2,1)} %get-tuple-element.79), channel_id=1, source_target_pairs={{0,7},{1,0},{2,1},{3,2},{4,3},{5,4},{6,5},{7,6},{8,15},{9,8},{10,9... | collective-permute-start | bytes 1769480 | tf_op jit(solution)/shard_map/ppermute | solution.py:223
  63.2 21.6 %collective-permute-start.12 = (bf16[24,24,512]{2,1,0:T(8,128)(2,1)}, bf16[24,24,512]{2,1,0:T(8,128)(2,1)S(1)}, u32[]{:S(2)}, u32[]{:S(2)}) collective-permute-start(bf16[24,24,512]{2,1,0:T(8,128)(2,1)} %get-tuple-element.83), channel_id=1, source_target_pairs={{0,1},{1,2},{2,3},{3,4},{4,5},{5,6},{6,7},{7,0},{8,9},{9,10},{10,1... | collective-permute-start | bytes 1769480 | tf_op jit(solution)/shard_map/ppermute | solution.py:222
  64.3 20.4 %collective-permute-start.13 = (bf16[24,24,512]{2,1,0:T(8,128)(2,1)}, bf16[24,24,512]{2,1,0:T(8,128)(2,1)S(1)}, u32[]{:S(2)}, u32[]{:S(2)}) collective-permute-start(bf16[24,24,512]{2,1,0:T(8,128)(2,1)} %get-tuple-element.84), channel_id=1, source_target_pairs={{0,7},{1,0},{2,1},{3,2},{4,3},{5,4},{6,5},{7,6},{8,15},{9,8},{10,9... | collective-permute-start | bytes 1769480 | tf_op jit(solution)/shard_map/ppermute | solution.py:223
  75.0 0.8 copy-start.2
  75.8 21.6 %collective-permute-start.14 = (bf16[24,24,512]{2,1,0:T(8,128)(2,1)}, bf16[24,24,512]{2,1,0:T(8,128)(2,1)S(1)}, u32[]{:S(2)}, u32[]{:S(2)}) collective-permute-start(bf16[24,24,512]{2,1,0:T(8,128)(2,1)} %copy-done.2), channel_id=1, source_target_pairs={{0,1},{1,2},{2,3},{3,4},{4,5},{5,6},{6,7},{7,0},{8,9},{9,10},{10,1... | collective-permute-start | bytes 1769480 | tf_op jit(solution)/shard_map/ppermute | solution.py:222
  76.9 20.6 %collective-permute-start.15 = (bf16[24,24,512]{2,1,0:T(8,128)(2,1)S(1)}, bf16[24,24,512]{2,1,0:T(8,128)(2,1)S(1)}, u32[]{:S(2)}, u32[]{:S(2)}) collective-permute-start(bf16[24,24,512]{2,1,0:T(8,128)(2,1)S(1)} %get-tuple-element.88), channel_id=1, source_target_pairs={{0,7},{1,0},{2,1},{3,2},{4,3},{5,4},{6,5},{7,6},{8,15},{9,8},{10,9... | collective-permute-start | bytes 1769480 | tf_op jit(solution)/shard_map/ppermute | solution.py:223
  100.4 28.2 %copy-start.4 = (s32[192]{0:T(256)S(1)}, s32[192]{0:T(256)}, u32[]{:S(2)}) copy-start(s32[192]{0:T(256)} %param.9) | copy-start | bytes 2308
  124.6 18.0 %all-to-all-start = ((bf16[32,24,512]{2,1,0:T(8,128)(2,1)}), bf16[32,24,512]{2,1,0:T(8,128)(2,1)S(1)}, u32[]{:S(2)}, u32[]{:S(2)}) async-start(bf16[32,24,512]{2,1,0:T(8,128)(2,1)} %shard_map.76), calls=%async_computation | async-start | bytes 1572864 | tf_op jit(solution)/shard_map/all_to_all | solution.py:255
  152.9 19.0 %copy-start.3 = (s32[192]{0:T(256)S(1)}, s32[192]{0:T(256)}, u32[]{:S(2)}) copy-start(s32[192]{0:T(256)} %param.8) | copy-start | bytes 2308
  152.9 50.0 %all-to-all-start.2 = ((bf16[256,24,128]{2,1,0:T(8,128)(2,1)}), bf16[256,24,128]{2,1,0:T(8,128)(2,1)S(1)}, u32[]{:S(2)}, u32[]{:S(2)}) async-start(bf16[256,24,128]{2,1,0:T(8,128)(2,1)} %get-tuple-element.90), calls=%async_computation.2 | async-start | bytes 3145728 | tf_op jit(solution)/shard_map/all_to_all | solution.py:283
  160.8 3.1 %collective-permute-start.16 = (f32[1,8,128]{2,1,0:T(8,128)S(1)}, f32[1,8,128]{2,1,0:T(8,128)S(1)}, u32[]{:S(2)}, u32[]{:S(2)}) collective-permute-start(f32[1,8,128]{2,1,0:T(8,128)S(1)} %bitcast.26), channel_id=1, source_target_pairs={{0,8},{8,0},{16,24},{24,16},{32,40},{40,32},{48,56},{56,48},{64,72... | collective-permute-start | bytes 12296 | tf_op jit(solution)/shard_map/ppermute | solution.py:291
  163.9 3.1 %collective-permute-start.17 = (f32[2,8,128]{2,1,0:T(8,128)S(1)}, f32[2,8,128]{2,1,0:T(8,128)S(1)}, u32[]{:S(2)}, u32[]{:S(2)}) collective-permute-start(f32[2,8,128]{2,1,0:T(8,128)S(1)} %pad_maximum_fusion.4), channel_id=1, source_target_pairs={{0,16},{8,24},{16,0},{24,8},{32,48},{40,56},{48,32},{56,40},{64,80... | collective-permute-start | bytes 24584 | tf_op jit(solution)/shard_map/ppermute | solution.py:291
  167.0 4.8 %collective-permute-start.18 = (f32[4,8,128]{2,1,0:T(8,128)S(1)}, f32[4,8,128]{2,1,0:T(8,128)S(1)}, u32[]{:S(2)}, u32[]{:S(2)}) collective-permute-start(f32[4,8,128]{2,1,0:T(8,128)S(1)} %pad_maximum_fusion.2), channel_id=1, source_target_pairs={{0,32},{8,40},{16,48},{24,56},{32,0},{40,8},{48,16},{56,24},{64,96... | collective-permute-start | bytes 49160 | tf_op jit(solution)/shard_map/ppermute | solution.py:291
  171.8 3.7 %collective-permute-start.19 = (f32[8,8,128]{2,1,0:T(8,128)S(1)}, f32[8,8,128]{2,1,0:T(8,128)S(1)}, u32[]{:S(2)}, u32[]{:S(2)}) collective-permute-start(f32[8,8,128]{2,1,0:T(8,128)S(1)} %pad_maximum_fusion.1), channel_id=1, source_target_pairs={{0,64},{8,72},{16,80},{24,88},{32,96},{40,104},{48,112},{56,120},{... | collective-permute-start | bytes 98312 | tf_op jit(solution)/shard_map/ppermute | solution.py:291
  175.4 5.6 %collective-permute-start.20 = (f32[16,8,128]{2,1,0:T(8,128)S(1)}, f32[16,8,128]{2,1,0:T(8,128)S(1)}, u32[]{:S(2)}, u32[]{:S(2)}) collective-permute-start(f32[16,8,128]{2,1,0:T(8,128)S(1)} %pad_maximum_fusion), channel_id=1, source_target_pairs={{0,128},{8,136},{16,144},{24,152},{32,160},{40,168},{48,176},{56,1... | collective-permute-start | bytes 196616 | tf_op jit(solution)/shard_map/ppermute | solution.py:291

commit v3 on v2

v3 whole, which is shorter than its diff:
```python
import functools
import math

import jax
import jax.numpy as jnp
from jax import lax
from jax.experimental import pallas as pl
from jax.experimental.pallas import tpu as pltpu
from jax.sharding import PartitionSpec as P

F = 768
D = 1024
ITERS = 2
CAP = 2
WIDTHS = (384, 640)
STREAMS = len(WIDTHS)
STARTS = tuple(sum(WIDTHS[:stream]) for stream in range(STREAMS))
TILE = 256


epsilon = 1e-07
first_coef = 3.4445
second_coef = -4.775
third_coef = 2.0315


def fetch_tables(tables, kept, sems):
    fetches = [
        pltpu.make_async_copy(table, kept.at[index], sems.at[index])
        for index, table in enumerate(tables)
    ]
    for fetch in fetches:
        fetch.start()
    return fetches


def columns_of(kept, index, scratch, target, per_group):
    lanes = kept.shape[2]
    scratch[:, :lanes] = kept[index]
    wide = scratch.shape[1]
    return pltpu.roll(scratch[...], wide - target * per_group, axis=1)


def dequantized(codes, scales, shifts, k):
    return scales[:, k : k + 1] * (codes.astype(jnp.float32) + shifts[:, k : k + 1])


def hop_kernel(step, half, first_col, groups, codes, scales_ref, shifts_ref, *refs):
    received, (up_out, down_out), scratch = refs[: len(refs) - 9], refs[-9:-7], refs[-7:]
    held, made, kept, table, firsts, loads, stores = scratch
    per_group = 2 * half
    width = held.shape[3]
    here = lax.axis_index("group")
    distance = groups // 2 - step
    targets = (
        lax.rem(here + distance, groups),
        lax.rem(here + groups - distance, groups),
    )
    parts = ((0, 0), (1, 1)) if step == 0 else ((0, 0), (1, 1), (0, 1), (1, 0))
    table_fetches = fetch_tables((scales_ref, shifts_ref), kept, firsts)
    fetches, writes = [], []
    for index, (side, part) in enumerate(parts):
        start = targets[side] * per_group + part * half
        fetches.append(
            pltpu.make_async_copy(
                codes.at[pl.ds(start, half), :, pl.ds(first_col, width)],
                held.at[index],
                loads.at[index],
            )
        )
        fetches[-1].start()
    for fetch in table_fetches:
        fetch.wait()
    tables = [
        [columns_of(kept, index, table, targets[side], per_group) for index in range(2)]
        for side in range(2)
    ]
    for index, (side, part) in enumerate(parts):
        fetches[index].wait()
        scales, shifts = tables[side]
        for k in range(half):
            value = dequantized(held[index, k], scales, shifts, part * half + k)
            if step > 1:
                value = value + received[side][part * half + k].astype(jnp.float32)
            elif step == 1 and part == side:
                value = value + received[side][k].astype(jnp.float32)
            made[index, k] = value.astype(jnp.bfloat16)
        out = (up_out, down_out)[side]
        place = out if step == 0 else out.at[pl.ds(part * half, half)]
        writes.append(pltpu.make_async_copy(made.at[index], place, stores.at[index]))
        writes[-1].start()
    for write in writes:
        write.wait()


def last_kernel(
    half, first_col, codes, scales_ref, shifts_ref, up_in, down_in, out, held, kept, table, sums, firsts, loads, stores
):
    per_group = 2 * half
    width = held.shape[3]
    spare = sums.shape[0] - per_group
    here = lax.axis_index("group")
    table_fetches = fetch_tables((scales_ref, shifts_ref), kept, firsts)
    fetches = []
    for part in range(2):
        fetches.append(
            pltpu.make_async_copy(
                codes.at[pl.ds(here * per_group + part * half, half), :, pl.ds(first_col, width)],
                held.at[part],
                loads.at[part],
            )
        )
        fetches[-1].start()
    sums[per_group:] = jnp.zeros((spare,) + sums.shape[1:], sums.dtype)
    spans = ((per_group, spare), (0, half), (half, half))
    writes = [
        pltpu.make_async_copy(sums.at[pl.ds(*span)], out.at[pl.ds(*span)], stores.at[index])
        for index, span in enumerate(spans)
    ]
    writes[0].start()
    for fetch in table_fetches:
        fetch.wait()
    scales = columns_of(kept, 0, table, here, per_group)
    shifts = columns_of(kept, 1, table, here, per_group)
    for part in range(2):
        fetches[part].wait()
        for k in range(half):
            place = part * half + k
            value = dequantized(held[part, k], scales, shifts, place)
            value = value + (up_in[place].astype(jnp.float32) + down_in[place].astype(jnp.float32))
            sums[place] = value.astype(jnp.bfloat16)
        writes[1 + part].start()
    for write in writes:
        write.wait()


def blocks_of(size):
    return [slice(first, first + TILE) for first in range(0, size, TILE)]


def columns_at(pieces, rows, cols):
    found = []
    for piece, start in zip(pieces, STARTS):
        low = max(cols.start - start, 0)
        high = min(cols.stop - start, piece.shape[1])
        if low < high:
            found.append(piece[rows, low:high])
    return found[0] if len(found) == 1 else jnp.concatenate(found, axis=1)


def newton_kernel(shard_rows, out_width, factor_ref, *refs):
    pieces = refs[:STREAMS]
    out_ref, norm_ref, current, raw, gram, poly, staged, stores = refs[STREAMS:]
    height, columns = current.shape
    row_blocks, col_blocks = blocks_of(height), blocks_of(columns)
    everything = slice(0, height)
    pairs = [(i, j) for i in range(len(row_blocks)) for j in range(i, len(row_blocks))]

    def outer(left, right):
        return lax.dot_general(
            left, right, (((1,), (1,)), ((), ())), preferred_element_type=jnp.float32
        )

    def mirrored(ref, i, j, block):
        ref[row_blocks[i], row_blocks[j]] = block.astype(jnp.bfloat16)
        if i != j:
            ref[row_blocks[j], row_blocks[i]] = block.T.astype(jnp.bfloat16)

    total = jnp.zeros((1, 1), jnp.float32)
    diagonal = lax.broadcasted_iota(jnp.int32, (TILE, TILE), 0) == lax.broadcasted_iota(
        jnp.int32, (TILE, TILE), 1
    )
    span = slice(0, columns)
    for i, j in pairs:
        product = outer(
            columns_at(pieces, row_blocks[i], span), columns_at(pieces, row_blocks[j], span)
        )
        raw[row_blocks[i], row_blocks[j]] = product
        if i == j:
            total = total + jnp.sum(jnp.where(diagonal, product, 0.0), keepdims=True)
    norm = jnp.sqrt(total)
    norm_ref[...] = jnp.broadcast_to(norm, norm_ref.shape)
    inverse = 1.0 / (norm + epsilon)
    for i, j in pairs:
        mirrored(gram, i, j, raw[row_blocks[i], row_blocks[j]] * inverse * inverse)
    writes = []
    for sweep in range(ITERS):
        if sweep > 0:
            for i, j in pairs:
                mirrored(gram, i, j, outer(current[row_blocks[i]], current[row_blocks[j]]))
        for i, j in pairs:
            squared = jnp.dot(
                gram[row_blocks[i]], gram[:, row_blocks[j]], preferred_element_type=jnp.float32
            )
            block = gram[row_blocks[i], row_blocks[j]].astype(jnp.float32)
            mirrored(poly, i, j, second_coef * block + third_coef * squared)
        for index, cols in enumerate(col_blocks):
            before = columns_at(pieces, everything, cols) if sweep == 0 else current[:, cols]
            product = jnp.dot(poly[...], before, preferred_element_type=jnp.float32)
            result = first_coef * before.astype(jnp.float32) + product
            if sweep == 0:
                result = result * inverse
            result = result.astype(jnp.bfloat16)
            if sweep < ITERS - 1:
                current[:, cols] = result
                continue
            scaled = (result.astype(jnp.float32) * factor_ref[0]).astype(jnp.bfloat16)
            per_column = height // shard_rows
            slot = index % 2
            if index >= 2:
                writes[index - 2].wait()
            for part in range(TILE // out_width):
                piece = scaled[:, part * out_width : (part + 1) * out_width]
                staged[slot, part * per_column : (part + 1) * per_column] = piece.reshape(
                    per_column, shard_rows, out_width
                )
            count = TILE // out_width * per_column
            writes.append(
                pltpu.make_async_copy(
                    staged.at[slot], out_ref.at[pl.ds(index * count, count)], stores.at[slot]
                )
            )
            writes[-1].start()
    for write in writes[-2:]:
        write.wait()


def program(grad_codes, row_scales, dither, owner_table, matrix_kind):
    group_count = lax.axis_size("group")
    owner_count = lax.axis_size("dp")
    matrices = grad_codes.shape[1]
    per_group = matrices // group_count
    shard_rows = grad_codes.shape[2]
    columns = grad_codes.shape[3]
    height = shard_rows * owner_count
    half = per_group // 2
    out_width = columns // group_count
    reach = group_count // 2
    gate_factor = math.sqrt(max(F, D)) * math.sqrt(max(1.0, F / D))
    down_factor = math.sqrt(max(F, D)) * math.sqrt(max(1.0, D / F))
    norm_scale = 1.0 / math.sqrt(height * columns)
    group_index = lax.axis_index("group")
    owner_index = lax.axis_index("dp")
    up = [(i, (i + 1) % group_count) for i in range(group_count)]
    down = [(i, (i - 1) % group_count) for i in range(group_count)]
    codes = grad_codes[0]
    scales = row_scales[0].T
    shifts = dither[0].T
    whole = pl.BlockSpec(memory_space=pltpu.VMEM)
    anywhere = pl.BlockSpec(memory_space=pl.ANY)
    scalars = pl.BlockSpec(memory_space=pltpu.SMEM)
    table_scratch = pltpu.VMEM((shard_rows, 256), jnp.float32)

    def shape_of(count, stream):
        return jax.ShapeDtypeStruct((count, shard_rows, WIDTHS[stream]), jnp.bfloat16)

    def buffers_of(count, stream):
        return pltpu.VMEM((count, half, shard_rows, WIDTHS[stream]), jnp.bfloat16)

    def local(x):
        return pltpu.with_memory_space_constraint(x, pltpu.VMEM)

    def cost_of(count, stream):
        moved = 6 * count * shard_rows * WIDTHS[stream]
        return pl.CostEstimate(flops=0, bytes_accessed=moved, transcendentals=0)

    def hop(step, stream, tables, received):
        count = half if step == 0 else per_group
        buffers = 2 if step == 0 else 4
        return pl.pallas_call(
            functools.partial(hop_kernel, step, half, STARTS[stream], group_count),
            in_specs=[anywhere] * 3 + [whole] * len(received),
            out_specs=[anywhere, anywhere],
            out_shape=[shape_of(count, stream)] * 2,
            scratch_shapes=[
                buffers_of(buffers, stream),
                buffers_of(buffers, stream),
                pltpu.VMEM((2, shard_rows, matrices), jnp.float32),
                table_scratch,
                pltpu.SemaphoreType.DMA((2,)),
                pltpu.SemaphoreType.DMA((buffers,)),
                pltpu.SemaphoreType.DMA((buffers,)),
            ],
            cost_estimate=cost_of(count, stream),
        )(codes, *tables, *[local(x) for x in received])

    def send(blocks):
        rising = lax.ppermute(blocks[0], "group", up)
        falling = lax.ppermute(blocks[1], "group", down)
        return rising, falling

    pending = [()] * STREAMS
    tables = (scales, shifts)
    previous = None
    for step in range(reach):
        for stream in range(STREAMS):
            if previous is not None:
                tables, blocks = lax.optimization_barrier((tables, previous[2]))
                pending[previous[1]] = send(blocks)
            previous = (step, stream, hop(step, stream, tables, pending[stream]))
    tables, blocks = lax.optimization_barrier((tables, previous[2]))
    pending[previous[1]] = send(blocks)
    pieces = []
    for stream in range(STREAMS):
        padded = pl.pallas_call(
            functools.partial(last_kernel, half, STARTS[stream]),
            in_specs=[anywhere] * 3 + [whole] * 2,
            out_specs=anywhere,
            out_shape=shape_of(owner_count, stream),
            scratch_shapes=[
                buffers_of(2, stream),
                pltpu.VMEM((2, shard_rows, matrices), jnp.float32),
                table_scratch,
                pltpu.VMEM(shape_of(owner_count, stream).shape, jnp.bfloat16),
                pltpu.SemaphoreType.DMA((2,)),
                pltpu.SemaphoreType.DMA((2,)),
                pltpu.SemaphoreType.DMA((3,)),
            ],
            cost_estimate=cost_of(owner_count, stream),
        )(codes, *tables, *[local(x) for x in pending[stream]])
        tables, padded = lax.optimization_barrier((tables, padded))
        arrived = lax.all_to_all(padded, "dp", split_axis=0, concat_axis=0, tiled=True)
        pieces.append(arrived.reshape(height, WIDTHS[stream]))

    owners = lax.dynamic_slice_in_dim(owner_table, group_index * per_group, per_group)
    place = group_index * per_group + jnp.minimum(owner_index, per_group - 1)
    kind = lax.dynamic_slice_in_dim(matrix_kind, place, 1)
    factor = jnp.where(kind == 1, down_factor, gate_factor).astype(jnp.float32)
    blocks_out, norms = pl.pallas_call(
        functools.partial(newton_kernel, shard_rows, out_width),
        in_specs=[scalars] + [whole] * STREAMS,
        out_specs=[anywhere, whole],
        out_shape=[
            jax.ShapeDtypeStruct((group_count * owner_count, shard_rows, out_width), jnp.bfloat16),
            jax.ShapeDtypeStruct((8, 128), jnp.float32),
        ],
        scratch_shapes=[
            pltpu.VMEM((height, columns), jnp.bfloat16),
            pltpu.VMEM((height, height), jnp.float32),
            pltpu.VMEM((height, height), jnp.bfloat16),
            pltpu.VMEM((height, height), jnp.bfloat16),
            pltpu.VMEM((2, TILE // out_width * owner_count, shard_rows, out_width), jnp.bfloat16),
            pltpu.SemaphoreType.DMA((2,)),
        ],
        name="newton",
        cost_estimate=pl.CostEstimate(
            flops=2 * ITERS * height * height * (2 * columns + height),
            bytes_accessed=4 * height * columns,
            transcendentals=0,
        ),
        compiler_params=pltpu.CompilerParams(vmem_limit_bytes=40 * 1024 * 1024),
    )(factor, *[local(x) for x in pieces])
    returned = lax.all_to_all(blocks_out, ("group", "dp"), split_axis=0, concat_axis=0, tiled=True)
    returned = returned.reshape(group_count, owner_count, shard_rows, out_width)
    updates = returned[:, :per_group].reshape(matrices, shard_rows, out_width)

    norms = norms[None]
    stride = 1
    while stride < owner_count:
        partner = [(i, i ^ stride) for i in range(owner_count)]
        other = lax.ppermute(norms, "dp", partner)
        low = (owner_index & stride) == 0
        norms = jnp.concatenate([jnp.where(low, norms, other), jnp.where(low, other, norms)])
        stride *= 2
    all_norms = norms[:per_group, 0, 0]
    position = jnp.arange(per_group, dtype=jnp.int32)
    same_owner = owners[:, None] == owners[None, :]
    earlier = position[None, :] < position[:, None]
    slot_of = jnp.sum((same_owner & earlier).astype(jnp.int32), 1)
    slot_hit = slot_of[:, None] == jnp.arange(CAP, dtype=jnp.int32)[None, :]
    owned_slot = (owners == owner_index)[:, None] & slot_hit
    slot_norms = jnp.sum(jnp.where(owned_slot, all_norms[:, None] * norm_scale, 0.0), 0)
    return (updates, slot_norms.reshape(1, 1, CAP))


def solution(mesh):
    placed = (
        P("group", None, "dp", None),
        P("group", None, "dp"),
        P("group", None, "dp"),
        P(),
        P(),
    )
    return jax.shard_map(
        program,
        mesh=mesh,
        in_specs=placed,
        out_specs=(P(None, "dp", "group"), P("group", "dp", None)),
        check_vma=False,
    )
```

time: 205 us -> 212 us (1.034)
  waiting for transfers between devices: 87.8 us -> 118 us
  blocking collectives: 24.2 us -> 0 us
  starting transfers between devices: 41.8 us -> 55.9 us
  Pallas kernels: 40 us -> 32.9 us
  other arithmetic: 4.18 us -> 1.21 us
  local copies, waits for them, and re-layouts: 4.5 us -> 1.84 us
    all_to_all x1 -> x0, blocking collectives: 24.2 us -> none  [program(): lax.all_to_all(padded, 'dp', split_axis=0, concat_axis=0, tiled=True)]
    ppermute x8, waiting for transfers between devices: 38.3 us -> 56.3 us  [send(): rising = lax.ppermute(blocks[0], 'group', up)]
    all_to_all x1 -> x2, starting transfers between devices: 3.92 us -> 18.5 us  [program(): lax.all_to_all(padded, 'dp', split_axis=0, concat_axis=0, tiled=True)]
    all_to_all x1 -> x2, waiting for transfers between devices: 12.8 us -> 24.6 us  [program(): lax.all_to_all(padded, 'dp', split_axis=0, concat_axis=0, tiled=True)]
    pallas_call x10, Pallas kernels: 29.9 us -> 25.1 us  [the longest x8 20.7 us: hop(): pl.pallas_call(functools.partial(hop_kernel, step, half, STARTS[stream],...]
    another operation x5 -> x0, other arithmetic: 2.97 us -> none  [targets_at(): jnp.stack([lax.rem(group_index + distance, group_count), lax.rem(group_in...]
    ppermute x8, starting transfers between devices: 7.11 us -> 4.44 us  [send(): rising = lax.ppermute(blocks[0], 'group', up)]
    unnamed x10 -> x16, local copies, waits for them, and re-layouts: 2.7 us -> 0.04 us
  transfers between devices with their start and end apart: 23 -> 24, of which waited for: 15 -> 12; matrix products, arithmetic and copies ran while one was open for 2% -> 1% of each run, Pallas kernels for 12% -> 7%
where the time goes in v3:
time: 212 us; the launch traced here: 211 us
  waiting for transfers between devices  118 us (56%)
  starting transfers between devices  55.9 us (26%)
  Pallas kernels  32.9 us (16%)
    ppermute x8, waiting for transfers between devices, send(): rising = lax.ppermute(blocks[0], 'group', up)  56.3 us
    all_to_all x2, waiting for transfers between devices, program(): lax.all_to_all(padded, 'dp', split_axis=0, concat_axis=0, tiled=True)  24.6 us
    ppermute x8, starting transfers between devices, send(): falling = lax.ppermute(blocks[1], 'group', down)  21.1 us
    all_to_all x1, waiting for transfers between devices, program(): lax.all_to_all(blocks_out, ('group', 'dp'), split_axis=0, concat_axis=0,...  20.9 us
    pallas_call x8, Pallas kernels, hop(): pl.pallas_call(functools.partial(hop_kernel, step, half, STARTS[stream],...  20.7 us
    all_to_all x2, starting transfers between devices, program(): lax.all_to_all(padded, 'dp', split_axis=0, concat_axis=0, tiled=True)  18.5 us
    ppermute x5, waiting for transfers between devices, program(): other = lax.ppermute(norms, 'dp', partner)  15.8 us
    pallas_call x1, Pallas kernels, program(): pl.pallas_call(functools.partial(newton_kernel, shard_rows, out_width), i...  7.78 us
  transfers between devices with their start and end apart: 24, of which 12 were waited for; matrix products, arithmetic and copies ran while one was open for 1% of the time, Pallas kernels for 7%

profile of v3, /device:TPU:1, one launch (start us, length us, event | category | flops | bytes accessed | tf_op | source)
XLA Modules:
  0.0 211.0 jit_solution(4101693530402106726)
XLA Ops:
  0.6 2.1 shard_map.68
  2.7 2.2 %shard_map.69 = (bf16[12,24,640]{2,1,0:T(8,128)(2,1)}, bf16[12,24,640]{2,1,0:T(8,128)(2,1)}) custom-call(bf16[192,24,1024]{2,1,0:T(8,128)(2,1)} %bitcast.19, f32[24,192]{1,0:T(8,128)} %bitcast.30, f32[24,192]{1,0:T(8,128)} %bitcast.40), custom_call_target="tpu_custom_call" | custom-call | bytes 1105920 | tf_op jit(solution)/shard_map/pallas_call | solution.py:270
  4.9 2.5 %collective-permute-start.2 = (bf16[12,24,640]{2,1,0:T(8,128)(2,1)}, bf16[12,24,640]{2,1,0:T(8,128)(2,1)S(1)}, u32[]{:S(2)}, u32[]{:S(2)}) collective-permute-start(bf16[12,24,640]{2,1,0:T(8,128)(2,1)} %get-tuple-element.70), channel_id=1, source_target_pairs={{0,1},{1,2},{2,3},{3,4},{4,5},{5,6},{6,7},{7,0},{8,9},{9,10},{10,1... | collective-permute-start | bytes 1105928 | tf_op jit(solution)/shard_map/ppermute | solution.py:288
  7.5 4.0 %collective-permute-start.3 = (bf16[12,24,640]{2,1,0:T(8,128)(2,1)}, bf16[12,24,640]{2,1,0:T(8,128)(2,1)S(1)}, u32[]{:S(2)}, u32[]{:S(2)}) collective-permute-start(bf16[12,24,640]{2,1,0:T(8,128)(2,1)} %get-tuple-element.71), channel_id=1, source_target_pairs={{0,7},{1,0},{2,1},{3,2},{4,3},{5,4},{6,5},{7,6},{8,15},{9,8},{10,9... | collective-permute-start | bytes 1105928 | tf_op jit(solution)/shard_map/ppermute | solution.py:289
  11.5 2.7 %collective-permute-start.1 = (bf16[12,24,384]{2,1,0:T(8,128)(2,1)S(1)}, bf16[12,24,384]{2,1,0:T(8,128)(2,1)S(1)}, u32[]{:S(2)}, u32[]{:S(2)}) collective-permute-start(bf16[12,24,384]{2,1,0:T(8,128)(2,1)S(1)} %copy-done.5), channel_id=1, source_target_pairs={{0,7},{1,0},{2,1},{3,2},{4,3},{5,4},{6,5},{7,6},{8,15},{9,8},{10,9... | collective-permute-start | bytes 663560 | tf_op jit(solution)/shard_map/ppermute | solution.py:289
  14.2 10.5 %collective-permute-done.refs_0_ = bf16[12,24,384]{2,1,0:T(8,128)(2,1)S(1)} collective-permute-done((bf16[12,24,384]{2,1,0:T(8,128)(2,1)S(1)}, bf16[12,24,384]{2,1,0:T(8,128)(2,1)S(1)}, u32[]{:S(2)}, u32[]{:S(2)}) %collective-permute-start) | collective-permute-done | bytes 221216 | tf_op jit(solution)/shard_map/ppermute | solution.py:288
  24.7 2.6 %shard_map.70 = (bf16[24,24,384]{2,1,0:T(8,128)(2,1)}, bf16[24,24,384]{2,1,0:T(8,128)(2,1)}) custom-call(bf16[192,24,1024]{2,1,0:T(8,128)(2,1)} %bitcast.20, f32[24,192]{1,0:T(8,128)} %bitcast.31, f32[24,192]{1,0:T(8,128)} %bitcast.41, bf16[12,24,384]{2,1,0:T(8,128)(2,1)S(1)} %collective-permute-done.refs_0_, ...), custom_call_target="tpu_custom_call" | custom-call | bytes 1327104 | tf_op jit(solution)/shard_map/pallas_call | solution.py:270
  27.4 2.8 %shard_map.71 = (bf16[24,24,640]{2,1,0:T(8,128)(2,1)}, bf16[24,24,640]{2,1,0:T(8,128)(2,1)}) custom-call(bf16[192,24,1024]{2,1,0:T(8,128)(2,1)} %bitcast.21, f32[24,192]{1,0:T(8,128)} %bitcast.32, f32[24,192]{1,0:T(8,128)} %bitcast.42, bf16[12,24,640]{2,1,0:T(8,128)(2,1)S(1)} %collective-permute-done.2.refs_0_, ...), custom_call_target="tpu_custom_call" | custom-call | bytes 2211840 | tf_op jit(solution)/shard_map/pallas_call | solution.py:270
  30.2 0.1 collective-permute-start.6
  30.3 2.7 %collective-permute-start.7 = (bf16[24,24,640]{2,1,0:T(8,128)(2,1)}, bf16[24,24,640]{2,1,0:T(8,128)(2,1)S(1)}, u32[]{:S(2)}, u32[]{:S(2)}) collective-permute-start(bf16[24,24,640]{2,1,0:T(8,128)(2,1)} %get-tuple-element.83), channel_id=1, source_target_pairs={{0,7},{1,0},{2,1},{3,2},{4,3},{5,4},{6,5},{7,6},{8,15},{9,8},{10,9... | collective-permute-start | bytes 2211848 | tf_op jit(solution)/shard_map/ppermute | solution.py:289
  33.0 2.7 %collective-permute-start.5 = (bf16[24,24,384]{2,1,0:T(8,128)(2,1)S(1)}, bf16[24,24,384]{2,1,0:T(8,128)(2,1)S(1)}, u32[]{:S(2)}, u32[]{:S(2)}) collective-permute-start(bf16[24,24,384]{2,1,0:T(8,128)(2,1)S(1)} %copy-done.1), channel_id=1, source_target_pairs={{0,7},{1,0},{2,1},{3,2},{4,3},{5,4},{6,5},{7,6},{8,15},{9,8},{10,9... | collective-permute-start | bytes 1327112 | tf_op jit(solution)/shard_map/ppermute | solution.py:289
  35.6 22.3 %collective-permute-done.4.refs_0_ = bf16[24,24,384]{2,1,0:T(8,128)(2,1)S(1)} collective-permute-done((bf16[24,24,384]{2,1,0:T(8,128)(2,1)S(1)}, bf16[24,24,384]{2,1,0:T(8,128)(2,1)S(1)}, u32[]{:S(2)}, u32[]{:S(2)}) %collective-permute-start.4) | collective-permute-done | bytes 442400 | tf_op jit(solution)/shard_map/ppermute | solution.py:288
  58.0 2.6 %shard_map.72 = (bf16[24,24,384]{2,1,0:T(8,128)(2,1)}, bf16[24,24,384]{2,1,0:T(8,128)(2,1)}) custom-call(bf16[192,24,1024]{2,1,0:T(8,128)(2,1)} %bitcast.22, f32[24,192]{1,0:T(8,128)} %bitcast.33, f32[24,192]{1,0:T(8,128)} %bitcast.43, bf16[24,24,384]{2,1,0:T(8,128)(2,1)S(1)} %collective-permute-done.4.refs_0_, ...), custom_call_target="tpu_custom_call" | custom-call | bytes 1327104 | tf_op jit(solution)/shard_map/pallas_call | solution.py:270
  60.7 2.9 %shard_map.73 = (bf16[24,24,640]{2,1,0:T(8,128)(2,1)}, bf16[24,24,640]{2,1,0:T(8,128)(2,1)}) custom-call(bf16[192,24,1024]{2,1,0:T(8,128)(2,1)} %bitcast.23, f32[24,192]{1,0:T(8,128)} %bitcast.34, f32[24,192]{1,0:T(8,128)} %bitcast.44, bf16[24,24,640]{2,1,0:T(8,128)(2,1)S(1)} %collective-permute-done.6.refs_0_, ...), custom_call_target="tpu_custom_call" | custom-call | bytes 2211840 | tf_op jit(solution)/shard_map/pallas_call | solution.py:270
  63.5 1.1 collective-permute-start.10
  64.7 1.6 collective-permute-start.11
  66.3 2.7 %collective-permute-start.9 = (bf16[24,24,384]{2,1,0:T(8,128)(2,1)S(1)}, bf16[24,24,384]{2,1,0:T(8,128)(2,1)S(1)}, u32[]{:S(2)}, u32[]{:S(2)}) collective-permute-start(bf16[24,24,384]{2,1,0:T(8,128)(2,1)S(1)} %copy-done.2), channel_id=1, source_target_pairs={{0,7},{1,0},{2,1},{3,2},{4,3},{5,4},{6,5},{7,6},{8,15},{9,8},{10,9... | collective-permute-start | bytes 1327112 | tf_op jit(solution)/shard_map/ppermute | solution.py:289
  69.0 21.5 %collective-permute-done.8.refs_0_ = bf16[24,24,384]{2,1,0:T(8,128)(2,1)S(1)} collective-permute-done((bf16[24,24,384]{2,1,0:T(8,128)(2,1)S(1)}, bf16[24,24,384]{2,1,0:T(8,128)(2,1)S(1)}, u32[]{:S(2)}, u32[]{:S(2)}) %collective-permute-start.8) | collective-permute-done | bytes 442400 | tf_op jit(solution)/shard_map/ppermute | solution.py:288
  90.4 2.6 %shard_map.74 = (bf16[24,24,384]{2,1,0:T(8,128)(2,1)}, bf16[24,24,384]{2,1,0:T(8,128)(2,1)}) custom-call(bf16[192,24,1024]{2,1,0:T(8,128)(2,1)} %bitcast.24, f32[24,192]{1,0:T(8,128)} %bitcast.35, f32[24,192]{1,0:T(8,128)} %bitcast.45, bf16[24,24,384]{2,1,0:T(8,128)(2,1)S(1)} %collective-permute-done.8.refs_0_, ...), custom_call_target="tpu_custom_call" | custom-call | bytes 1327104 | tf_op jit(solution)/shard_map/pallas_call | solution.py:270
  93.1 0.6 collective-permute-start.12
  93.7 2.2 %collective-permute-start.13 = (bf16[24,24,384]{2,1,0:T(8,128)(2,1)}, bf16[24,24,384]{2,1,0:T(8,128)(2,1)S(1)}, u32[]{:S(2)}, u32[]{:S(2)}) collective-permute-start(bf16[24,24,384]{2,1,0:T(8,128)(2,1)} %get-tuple-element.101), channel_id=1, source_target_pairs={{0,7},{1,0},{2,1},{3,2},{4,3},{5,4},{6,5},{7,6},{8,15},{9,8},{10,9... | collective-permute-start | bytes 1327112 | tf_op jit(solution)/shard_map/ppermute | solution.py:289
  95.9 2.8 %shard_map.75 = (bf16[24,24,640]{2,1,0:T(8,128)(2,1)}, bf16[24,24,640]{2,1,0:T(8,128)(2,1)}) custom-call(bf16[192,24,1024]{2,1,0:T(8,128)(2,1)} %bitcast.25, f32[24,192]{1,0:T(8,128)} %bitcast.36, f32[24,192]{1,0:T(8,128)} %bitcast.46, bf16[24,24,640]{2,1,0:T(8,128)(2,1)S(1)} %collective-permute-done.10.refs_0_, ...), custom_call_target="tpu_custom_call" | custom-call | bytes 2211840 | tf_op jit(solution)/shard_map/pallas_call | solution.py:270
  98.7 0.1 collective-permute-start.14
  98.7 2.7 %collective-permute-start.15 = (bf16[24,24,640]{2,1,0:T(8,128)(2,1)}, bf16[24,24,640]{2,1,0:T(8,128)(2,1)S(1)}, u32[]{:S(2)}, u32[]{:S(2)}) collective-permute-start(bf16[24,24,640]{2,1,0:T(8,128)(2,1)} %get-tuple-element.106), channel_id=1, source_target_pairs={{0,7},{1,0},{2,1},{3,2},{4,3},{5,4},{6,5},{7,6},{8,15},{9,8},{10,9... | collective-permute-start | bytes 2211848 | tf_op jit(solution)/shard_map/ppermute | solution.py:289
  101.4 2.0 collective-permute-done.12.up_in
  103.4 2.1 %shard_map.76 = bf16[32,24,384]{2,1,0:T(8,128)(2,1)} custom-call(bf16[192,24,1024]{2,1,0:T(8,128)(2,1)} %bitcast.26, f32[24,192]{1,0:T(8,128)} %bitcast.37, f32[24,192]{1,0:T(8,128)} %bitcast.47, bf16[24,24,384]{2,1,0:T(8,128)(2,1)S(1)} %collective-permute-done.12.up_in, bf16[24,24,384]{2,1,0:T(8,128)(2,1)S(1)} %collective-permute-done.13.down_in), custom_call_target="tpu_custom_call" | custom-call | bytes 1769472 | tf_op jit(solution)/shard_map/pallas_call | solution.py:305
  105.5 14.6 %all-to-all-start = ((bf16[32,24,384]{2,1,0:T(8,128)(2,1)}), bf16[32,24,384]{2,1,0:T(8,128)(2,1)S(1)}, u32[]{:S(2)}, u32[]{:S(2)}) async-start(bf16[32,24,384]{2,1,0:T(8,128)(2,1)} %shard_map.76), calls=%async_computation | async-start | bytes 1179648 | tf_op jit(solution)/shard_map/all_to_all | solution.py:322
  120.1 2.3 %shard_map.77 = bf16[32,24,640]{2,1,0:T(8,128)(2,1)} custom-call(bf16[192,24,1024]{2,1,0:T(8,128)(2,1)} %bitcast.27, f32[24,192]{1,0:T(8,128)} %bitcast.38, f32[24,192]{1,0:T(8,128)} %bitcast.48, bf16[24,24,640]{2,1,0:T(8,128)(2,1)S(1)} %collective-permute-done.14.up_in, bf16[24,24,640]{2,1,0:T(8,128)(2,1)S(1)} %collective-permute-done.15.down_in), custom_call_target="tpu_custom_call" | custom-call | bytes 2949120 | tf_op jit(solution)/shard_map/pallas_call | solution.py:305
  122.4 9.9 %all-to-all-done = bf16[32,24,384]{2,1,0:T(8,128)(2,1)S(1)} async-done(((bf16[32,24,384]{2,1,0:T(8,128)(2,1)}), bf16[32,24,384]{2,1,0:T(8,128)(2,1)S(1)}, u32[]{:S(2)}, u32[]{:S(2)}) %all-to-all-start) | async-done | bytes 589856 | tf_op jit(solution)/shard_map/all_to_all | solution.py:322
  132.3 3.9 %all-to-all-start.1 = ((bf16[32,24,640]{2,1,0:T(8,128)(2,1)}), bf16[32,24,640]{2,1,0:T(8,128)(2,1)S(1)}, u32[]{:S(2)}, u32[]{:S(2)}) async-start(bf16[32,24,640]{2,1,0:T(8,128)(2,1)} %shard_map.77), calls=%async_computation.1 | async-start | bytes 1966080 | tf_op jit(solution)/shard_map/all_to_all | solution.py:322
  136.3 0.6 dynamic_slice.6
  137.5 14.7 %all-to-all-done.1 = bf16[32,24,640]{2,1,0:T(8,128)(2,1)S(1)} async-done(((bf16[32,24,640]{2,1,0:T(8,128)(2,1)}), bf16[32,24,640]{2,1,0:T(8,128)(2,1)S(1)}, u32[]{:S(2)}, u32[]{:S(2)}) %all-to-all-start.1) | async-done | bytes 983072 | tf_op jit(solution)/shard_map/all_to_all | solution.py:322
  152.2 7.8 %newton.1 = (bf16[256,24,128]{2,1,0:T(8,128)(2,1)}, f32[8,128]{1,0:T(8,128)S(1)}) custom-call(f32[1]{0:T(128)S(6)} %select_n.75.factor_ref, bf16[768,384]{1,0:T(8,128)(2,1)S(1)} %bitcast.16, bf16[768,640]{1,0:T(8,128)(2,1)S(1)} %bitcast.15), custom_call_target="tpu_custom_call" | custom-call | flops 6643777536 | bytes 3145728 | tf_op jit(solution)/shard_map/newton/pallas_call | solution.py:329
  160.0 7.7 %all-to-all-start.2 = ((bf16[256,24,128]{2,1,0:T(8,128)(2,1)}), bf16[256,24,128]{2,1,0:T(8,128)(2,1)S(1)}, u32[]{:S(2)}, u32[]{:S(2)}) async-start(bf16[256,24,128]{2,1,0:T(8,128)(2,1)} %get-tuple-element.108), calls=%async_computation.2 | async-start | bytes 3145728 | tf_op jit(solution)/shard_map/all_to_all | solution.py:353
  167.8 2.2 %collective-permute-start.16 = (f32[1,8,128]{2,1,0:T(8,128)S(1)}, f32[1,8,128]{2,1,0:T(8,128)S(1)}, u32[]{:S(2)}, u32[]{:S(2)}) collective-permute-start(f32[1,8,128]{2,1,0:T(8,128)S(1)} %bitcast.17), channel_id=1, source_target_pairs={{0,8},{8,0},{16,24},{24,16},{32,40},{40,32},{48,56},{56,48},{64,72... | collective-permute-start | bytes 12296 | tf_op jit(solution)/shard_map/ppermute | solution.py:361
  170.0 0.8 collective-permute-done.16
  170.8 3.1 %collective-permute-done.17 = f32[2,8,128]{2,1,0:T(8,128)S(1)} collective-permute-done((f32[2,8,128]{2,1,0:T(8,128)S(1)}, f32[2,8,128]{2,1,0:T(8,128)S(1)}, u32[]{:S(2)}, u32[]{:S(2)}) %collective-permute-start.17) | collective-permute-done | bytes 8224 | tf_op jit(solution)/shard_map/ppermute | solution.py:361
  173.9 1.3 collective-permute-start.18
  175.3 3.4 %collective-permute-done.18 = f32[4,8,128]{2,1,0:T(8,128)S(1)} collective-permute-done((f32[4,8,128]{2,1,0:T(8,128)S(1)}, f32[4,8,128]{2,1,0:T(8,128)S(1)}, u32[]{:S(2)}, u32[]{:S(2)}) %collective-permute-start.18) | collective-permute-done | bytes 16416 | tf_op jit(solution)/shard_map/ppermute | solution.py:361
  178.7 0.1 collective-permute-start.19
  178.9 3.5 %collective-permute-done.19 = f32[8,8,128]{2,1,0:T(8,128)S(1)} collective-permute-done((f32[8,8,128]{2,1,0:T(8,128)S(1)}, f32[8,8,128]{2,1,0:T(8,128)S(1)}, u32[]{:S(2)}, u32[]{:S(2)}) %collective-permute-start.19) | collective-permute-done | bytes 32800 | tf_op jit(solution)/shard_map/ppermute | solution.py:361
  182.4 0.4 collective-permute-start.20
  182.8 0.2 convert_reduce_fusion
  183.0 5.0 %collective-permute-done.20 = f32[16,8,128]{2,1,0:T(8,128)S(1)} collective-permute-done((f32[16,8,128]{2,1,0:T(8,128)S(1)}, f32[16,8,128]{2,1,0:T(8,128)S(1)}, u32[]{:S(2)}, u32[]{:S(2)}) %collective-permute-start.20) | collective-permute-done | bytes 65568 | tf_op jit(solution)/shard_map/ppermute | solution.py:361
  188.0 0.3 fusion.2
  188.3 0.6 fusion.3
  188.9 20.9 %all-to-all-done.2 = bf16[256,24,128]{2,1,0:T(8,128)(2,1)S(1)} async-done(((bf16[256,24,128]{2,1,0:T(8,128)(2,1)}), bf16[256,24,128]{2,1,0:T(8,128)(2,1)S(1)}, u32[]{:S(2)}, u32[]{:S(2)}) %all-to-all-start.2) | async-done | bytes 1572896 | tf_op jit(solution)/shard_map/all_to_all | solution.py:353
  209.8 1.2 slice.8
  (42 shorter events, 0.2 us)
Async XLA Ops:
  2.7 8.8 %copy-start.6 = (bf16[12,24,384]{2,1,0:T(8,128)(2,1)S(1)}, bf16[12,24,384]{2,1,0:T(8,128)(2,1)}, u32[]{:S(2)}) copy-start(bf16[12,24,384]{2,1,0:T(8,128)(2,1)} %get-tuple-element.64) | copy-start | bytes 663556
  2.7 8.8 %copy-start.5 = (bf16[12,24,384]{2,1,0:T(8,128)(2,1)S(1)}, bf16[12,24,384]{2,1,0:T(8,128)(2,1)}, u32[]{:S(2)}) copy-start(bf16[12,24,384]{2,1,0:T(8,128)(2,1)} %get-tuple-element.65) | copy-start | bytes 663556
  4.9 22.4 %collective-permute-start.2 = (bf16[12,24,640]{2,1,0:T(8,128)(2,1)}, bf16[12,24,640]{2,1,0:T(8,128)(2,1)S(1)}, u32[]{:S(2)}, u32[]{:S(2)}) collective-permute-start(bf16[12,24,640]{2,1,0:T(8,128)(2,1)} %get-tuple-element.70), channel_id=1, source_target_pairs={{0,1},{1,2},{2,3},{3,4},{4,5},{5,6},{6,7},{7,0},{8,9},{9,10},{10,1... | collective-permute-start | bytes 1105928 | tf_op jit(solution)/shard_map/ppermute | solution.py:288
  7.5 19.9 %collective-permute-start.3 = (bf16[12,24,640]{2,1,0:T(8,128)(2,1)}, bf16[12,24,640]{2,1,0:T(8,128)(2,1)S(1)}, u32[]{:S(2)}, u32[]{:S(2)}) collective-permute-start(bf16[12,24,640]{2,1,0:T(8,128)(2,1)} %get-tuple-element.71), channel_id=1, source_target_pairs={{0,7},{1,0},{2,1},{3,2},{4,3},{5,4},{6,5},{7,6},{8,15},{9,8},{10,9... | collective-permute-start | bytes 1105928 | tf_op jit(solution)/shard_map/ppermute | solution.py:289
  11.5 13.2 %collective-permute-start = (bf16[12,24,384]{2,1,0:T(8,128)(2,1)S(1)}, bf16[12,24,384]{2,1,0:T(8,128)(2,1)S(1)}, u32[]{:S(2)}, u32[]{:S(2)}) collective-permute-start(bf16[12,24,384]{2,1,0:T(8,128)(2,1)S(1)} %copy-done.6), channel_id=1, source_target_pairs={{0,1},{1,2},{2,3},{3,4},{4,5},{5,6},{6,7},{7,0},{8,9},{9,10},{10,1... | collective-permute-start | bytes 663560 | tf_op jit(solution)/shard_map/ppermute | solution.py:288
  11.5 13.1 %collective-permute-start.1 = (bf16[12,24,384]{2,1,0:T(8,128)(2,1)S(1)}, bf16[12,24,384]{2,1,0:T(8,128)(2,1)S(1)}, u32[]{:S(2)}, u32[]{:S(2)}) collective-permute-start(bf16[12,24,384]{2,1,0:T(8,128)(2,1)S(1)} %copy-done.5), channel_id=1, source_target_pairs={{0,7},{1,0},{2,1},{3,2},{4,3},{5,4},{6,5},{7,6},{8,15},{9,8},{10,9... | collective-permute-start | bytes 663560 | tf_op jit(solution)/shard_map/ppermute | solution.py:289
  27.3 5.6 %copy-start.3 = (bf16[24,24,384]{2,1,0:T(8,128)(2,1)S(1)}, bf16[24,24,384]{2,1,0:T(8,128)(2,1)}, u32[]{:S(2)}) copy-start(bf16[24,24,384]{2,1,0:T(8,128)(2,1)} %get-tuple-element.76) | copy-start | bytes 1327108
  27.3 5.6 %copy-start.1 = (bf16[24,24,384]{2,1,0:T(8,128)(2,1)S(1)}, bf16[24,24,384]{2,1,0:T(8,128)(2,1)}, u32[]{:S(2)}) copy-start(bf16[24,24,384]{2,1,0:T(8,128)(2,1)} %get-tuple-element.77) | copy-start | bytes 1327108
  30.2 30.5 %collective-permute-start.6 = (bf16[24,24,640]{2,1,0:T(8,128)(2,1)}, bf16[24,24,640]{2,1,0:T(8,128)(2,1)S(1)}, u32[]{:S(2)}, u32[]{:S(2)}) collective-permute-start(bf16[24,24,640]{2,1,0:T(8,128)(2,1)} %get-tuple-element.82), channel_id=1, source_target_pairs={{0,1},{1,2},{2,3},{3,4},{4,5},{5,6},{6,7},{7,0},{8,9},{9,10},{10,1... | collective-permute-start | bytes 2211848 | tf_op jit(solution)/shard_map/ppermute | solution.py:288
  30.3 30.4 %collective-permute-start.7 = (bf16[24,24,640]{2,1,0:T(8,128)(2,1)}, bf16[24,24,640]{2,1,0:T(8,128)(2,1)S(1)}, u32[]{:S(2)}, u32[]{:S(2)}) collective-permute-start(bf16[24,24,640]{2,1,0:T(8,128)(2,1)} %get-tuple-element.83), channel_id=1, source_target_pairs={{0,7},{1,0},{2,1},{3,2},{4,3},{5,4},{6,5},{7,6},{8,15},{9,8},{10,9... | collective-permute-start | bytes 2211848 | tf_op jit(solution)/shard_map/ppermute | solution.py:289
  32.9 25.0 %collective-permute-start.4 = (bf16[24,24,384]{2,1,0:T(8,128)(2,1)S(1)}, bf16[24,24,384]{2,1,0:T(8,128)(2,1)S(1)}, u32[]{:S(2)}, u32[]{:S(2)}) collective-permute-start(bf16[24,24,384]{2,1,0:T(8,128)(2,1)S(1)} %copy-done.3), channel_id=1, source_target_pairs={{0,1},{1,2},{2,3},{3,4},{4,5},{5,6},{6,7},{7,0},{8,9},{9,10},{10,1... | collective-permute-start | bytes 1327112 | tf_op jit(solution)/shard_map/ppermute | solution.py:288
  33.0 25.0 %collective-permute-start.5 = (bf16[24,24,384]{2,1,0:T(8,128)(2,1)S(1)}, bf16[24,24,384]{2,1,0:T(8,128)(2,1)S(1)}, u32[]{:S(2)}, u32[]{:S(2)}) collective-permute-start(bf16[24,24,384]{2,1,0:T(8,128)(2,1)S(1)} %copy-done.1), channel_id=1, source_target_pairs={{0,7},{1,0},{2,1},{3,2},{4,3},{5,4},{6,5},{7,6},{8,15},{9,8},{10,9... | collective-permute-start | bytes 1327112 | tf_op jit(solution)/shard_map/ppermute | solution.py:289
  60.6 5.7 %copy-start.4 = (bf16[24,24,384]{2,1,0:T(8,128)(2,1)S(1)}, bf16[24,24,384]{2,1,0:T(8,128)(2,1)}, u32[]{:S(2)}) copy-start(bf16[24,24,384]{2,1,0:T(8,128)(2,1)} %get-tuple-element.88) | copy-start | bytes 1327108
  60.6 5.7 %copy-start.2 = (bf16[24,24,384]{2,1,0:T(8,128)(2,1)S(1)}, bf16[24,24,384]{2,1,0:T(8,128)(2,1)}, u32[]{:S(2)}) copy-start(bf16[24,24,384]{2,1,0:T(8,128)(2,1)} %get-tuple-element.89) | copy-start | bytes 1327108
  63.5 32.3 %collective-permute-start.10 = (bf16[24,24,640]{2,1,0:T(8,128)(2,1)}, bf16[24,24,640]{2,1,0:T(8,128)(2,1)S(1)}, u32[]{:S(2)}, u32[]{:S(2)}) collective-permute-start(bf16[24,24,640]{2,1,0:T(8,128)(2,1)} %get-tuple-element.94), channel_id=1, source_target_pairs={{0,1},{1,2},{2,3},{3,4},{4,5},{5,6},{6,7},{7,0},{8,9},{9,10},{10,1... | collective-permute-start | bytes 2211848 | tf_op jit(solution)/shard_map/ppermute | solution.py:288
  64.7 31.2 %collective-permute-start.11 = (bf16[24,24,640]{2,1,0:T(8,128)(2,1)}, bf16[24,24,640]{2,1,0:T(8,128)(2,1)S(1)}, u32[]{:S(2)}, u32[]{:S(2)}) collective-permute-start(bf16[24,24,640]{2,1,0:T(8,128)(2,1)} %get-tuple-element.95), channel_id=1, source_target_pairs={{0,7},{1,0},{2,1},{3,2},{4,3},{5,4},{6,5},{7,6},{8,15},{9,8},{10,9... | collective-permute-start | bytes 2211848 | tf_op jit(solution)/shard_map/ppermute | solution.py:289
  66.3 24.2 %collective-permute-start.8 = (bf16[24,24,384]{2,1,0:T(8,128)(2,1)S(1)}, bf16[24,24,384]{2,1,0:T(8,128)(2,1)S(1)}, u32[]{:S(2)}, u32[]{:S(2)}) collective-permute-start(bf16[24,24,384]{2,1,0:T(8,128)(2,1)S(1)} %copy-done.4), channel_id=1, source_target_pairs={{0,1},{1,2},{2,3},{3,4},{4,5},{5,6},{6,7},{7,0},{8,9},{9,10},{10,1... | collective-permute-start | bytes 1327112 | tf_op jit(solution)/shard_map/ppermute | solution.py:288
  66.3 24.2 %collective-permute-start.9 = (bf16[24,24,384]{2,1,0:T(8,128)(2,1)S(1)}, bf16[24,24,384]{2,1,0:T(8,128)(2,1)S(1)}, u32[]{:S(2)}, u32[]{:S(2)}) collective-permute-start(bf16[24,24,384]{2,1,0:T(8,128)(2,1)S(1)} %copy-done.2), channel_id=1, source_target_pairs={{0,7},{1,0},{2,1},{3,2},{4,3},{5,4},{6,5},{7,6},{8,15},{9,8},{10,9... | collective-permute-start | bytes 1327112 | tf_op jit(solution)/shard_map/ppermute | solution.py:289
  93.1 10.3 %collective-permute-start.12 = (bf16[24,24,384]{2,1,0:T(8,128)(2,1)}, bf16[24,24,384]{2,1,0:T(8,128)(2,1)S(1)}, u32[]{:S(2)}, u32[]{:S(2)}) collective-permute-start(bf16[24,24,384]{2,1,0:T(8,128)(2,1)} %get-tuple-element.100), channel_id=1, source_target_pairs={{0,1},{1,2},{2,3},{3,4},{4,5},{5,6},{6,7},{7,0},{8,9},{9,10},{10,1... | collective-permute-start | bytes 1327112 | tf_op jit(solution)/shard_map/ppermute | solution.py:288
  93.7 9.7 %collective-permute-start.13 = (bf16[24,24,384]{2,1,0:T(8,128)(2,1)}, bf16[24,24,384]{2,1,0:T(8,128)(2,1)S(1)}, u32[]{:S(2)}, u32[]{:S(2)}) collective-permute-start(bf16[24,24,384]{2,1,0:T(8,128)(2,1)} %get-tuple-element.101), channel_id=1, source_target_pairs={{0,7},{1,0},{2,1},{3,2},{4,3},{5,4},{6,5},{7,6},{8,15},{9,8},{10,9... | collective-permute-start | bytes 1327112 | tf_op jit(solution)/shard_map/ppermute | solution.py:289
  98.7 21.4 %collective-permute-start.14 = (bf16[24,24,640]{2,1,0:T(8,128)(2,1)}, bf16[24,24,640]{2,1,0:T(8,128)(2,1)S(1)}, u32[]{:S(2)}, u32[]{:S(2)}) collective-permute-start(bf16[24,24,640]{2,1,0:T(8,128)(2,1)} %get-tuple-element.105), channel_id=1, source_target_pairs={{0,1},{1,2},{2,3},{3,4},{4,5},{5,6},{6,7},{7,0},{8,9},{9,10},{10,1... | collective-permute-start | bytes 2211848 | tf_op jit(solution)/shard_map/ppermute | solution.py:288
  98.7 21.3 %collective-permute-start.15 = (bf16[24,24,640]{2,1,0:T(8,128)(2,1)}, bf16[24,24,640]{2,1,0:T(8,128)(2,1)S(1)}, u32[]{:S(2)}, u32[]{:S(2)}) collective-permute-start(bf16[24,24,640]{2,1,0:T(8,128)(2,1)} %get-tuple-element.106), channel_id=1, source_target_pairs={{0,7},{1,0},{2,1},{3,2},{4,3},{5,4},{6,5},{7,6},{8,15},{9,8},{10,9... | collective-permute-start | bytes 2211848 | tf_op jit(solution)/shard_map/ppermute | solution.py:289
  105.5 26.8 %all-to-all-start = ((bf16[32,24,384]{2,1,0:T(8,128)(2,1)}), bf16[32,24,384]{2,1,0:T(8,128)(2,1)S(1)}, u32[]{:S(2)}, u32[]{:S(2)}) async-start(bf16[32,24,384]{2,1,0:T(8,128)(2,1)} %shard_map.76), calls=%async_computation | async-start | bytes 1179648 | tf_op jit(solution)/shard_map/all_to_all | solution.py:322
  122.4 13.9 %copy-start.7 = (s32[192]{0:T(256)S(1)}, s32[192]{0:T(256)}, u32[]{:S(2)}) copy-start(s32[192]{0:T(256)} %param.9) | copy-start | bytes 2308
  132.3 19.9 %all-to-all-start.1 = ((bf16[32,24,640]{2,1,0:T(8,128)(2,1)}), bf16[32,24,640]{2,1,0:T(8,128)(2,1)S(1)}, u32[]{:S(2)}, u32[]{:S(2)}) async-start(bf16[32,24,640]{2,1,0:T(8,128)(2,1)} %shard_map.77), calls=%async_computation.1 | async-start | bytes 1966080 | tf_op jit(solution)/shard_map/all_to_all | solution.py:322
  160.0 18.8 %copy-start = (s32[192]{0:T(256)S(1)}, s32[192]{0:T(256)}, u32[]{:S(2)}) copy-start(s32[192]{0:T(256)} %param.8) | copy-start | bytes 2308
  160.0 49.7 %all-to-all-start.2 = ((bf16[256,24,128]{2,1,0:T(8,128)(2,1)}), bf16[256,24,128]{2,1,0:T(8,128)(2,1)S(1)}, u32[]{:S(2)}, u32[]{:S(2)}) async-start(bf16[256,24,128]{2,1,0:T(8,128)(2,1)} %get-tuple-element.108), calls=%async_computation.2 | async-start | bytes 3145728 | tf_op jit(solution)/shard_map/all_to_all | solution.py:353
  167.8 3.1 %collective-permute-start.16 = (f32[1,8,128]{2,1,0:T(8,128)S(1)}, f32[1,8,128]{2,1,0:T(8,128)S(1)}, u32[]{:S(2)}, u32[]{:S(2)}) collective-permute-start(f32[1,8,128]{2,1,0:T(8,128)S(1)} %bitcast.17), channel_id=1, source_target_pairs={{0,8},{8,0},{16,24},{24,16},{32,40},{40,32},{48,56},{56,48},{64,72... | collective-permute-start | bytes 12296 | tf_op jit(solution)/shard_map/ppermute | solution.py:361
  170.8 3.1 %collective-permute-start.17 = (f32[2,8,128]{2,1,0:T(8,128)S(1)}, f32[2,8,128]{2,1,0:T(8,128)S(1)}, u32[]{:S(2)}, u32[]{:S(2)}) collective-permute-start(f32[2,8,128]{2,1,0:T(8,128)S(1)} %pad_maximum_fusion.4), channel_id=1, source_target_pairs={{0,16},{8,24},{16,0},{24,8},{32,48},{40,56},{48,32},{56,40},{64,80... | collective-permute-start | bytes 24584 | tf_op jit(solution)/shard_map/ppermute | solution.py:361
  173.9 4.8 %collective-permute-start.18 = (f32[4,8,128]{2,1,0:T(8,128)S(1)}, f32[4,8,128]{2,1,0:T(8,128)S(1)}, u32[]{:S(2)}, u32[]{:S(2)}) collective-permute-start(f32[4,8,128]{2,1,0:T(8,128)S(1)} %pad_maximum_fusion.2), channel_id=1, source_target_pairs={{0,32},{8,40},{16,48},{24,56},{32,0},{40,8},{48,16},{56,24},{64,96... | collective-permute-start | bytes 49160 | tf_op jit(solution)/shard_map/ppermute | solution.py:361
  178.7 3.7 %collective-permute-start.19 = (f32[8,8,128]{2,1,0:T(8,128)S(1)}, f32[8,8,128]{2,1,0:T(8,128)S(1)}, u32[]{:S(2)}, u32[]{:S(2)}) collective-permute-start(f32[8,8,128]{2,1,0:T(8,128)S(1)} %pad_maximum_fusion.1), channel_id=1, source_target_pairs={{0,64},{8,72},{16,80},{24,88},{32,96},{40,104},{48,112},{56,120},{... | collective-permute-start | bytes 98312 | tf_op jit(solution)/shard_map/ppermute | solution.py:361
  182.4 5.6 %collective-permute-start.20 = (f32[16,8,128]{2,1,0:T(8,128)S(1)}, f32[16,8,128]{2,1,0:T(8,128)S(1)}, u32[]{:S(2)}, u32[]{:S(2)}) collective-permute-start(f32[16,8,128]{2,1,0:T(8,128)S(1)} %pad_maximum_fusion), channel_id=1, source_target_pairs={{0,128},{8,136},{16,144},{24,152},{32,160},{40,168},{48,176},{56,1... | collective-permute-start | bytes 196616 | tf_op jit(solution)/shard_map/ppermute | solution.py:361

commit v4 on v3

--- a/solution.py
+++ b/solution.py
@@ -93,12 +93,9 @@
         write.wait()
 
 
-def last_kernel(
-    half, first_col, codes, scales_ref, shifts_ref, up_in, down_in, out, held, kept, table, sums, firsts, loads, stores
-):
+def own_kernel(half, first_col, codes, scales_ref, shifts_ref, out, held, kept, table, firsts, loads):
     per_group = 2 * half
     width = held.shape[3]
-    spare = sums.shape[0] - per_group
     here = lax.axis_index("group")
     table_fetches = fetch_tables((scales_ref, shifts_ref), kept, firsts)
     fetches = []
@@ -111,13 +108,6 @@
             )
         )
         fetches[-1].start()
-    sums[per_group:] = jnp.zeros((spare,) + sums.shape[1:], sums.dtype)
-    spans = ((per_group, spare), (0, half), (half, half))
-    writes = [
-        pltpu.make_async_copy(sums.at[pl.ds(*span)], out.at[pl.ds(*span)], stores.at[index])
-        for index, span in enumerate(spans)
-    ]
-    writes[0].start()
     for fetch in table_fetches:
         fetch.wait()
     scales = columns_of(kept, 0, table, here, per_group)
@@ -125,10 +115,25 @@
     for part in range(2):
         fetches[part].wait()
         for k in range(half):
-            place = part * half + k
-            value = dequantized(held[part, k], scales, shifts, place)
-            value = value + (up_in[place].astype(jnp.float32) + down_in[place].astype(jnp.float32))
-            sums[place] = value.astype(jnp.bfloat16)
+            value = dequantized(held[part, k], scales, shifts, part * half + k)
+            out[part * half + k] = value.astype(jnp.bfloat16)
+
+
+def last_kernel(own, up_in, down_in, out, sums, stores):
+    per_group = own.shape[0]
+    spare = sums.shape[0] - per_group
+    share = per_group // 4
+    sums[per_group:] = jnp.zeros((spare,) + sums.shape[1:], sums.dtype)
+    spans = [(per_group, spare)] + [(part * share, share) for part in range(4)]
+    writes = [
+        pltpu.make_async_copy(sums.at[pl.ds(*span)], out.at[pl.ds(*span)], stores.at[index])
+        for index, span in enumerate(spans)
+    ]
+    writes[0].start()
+    for part in range(4):
+        for place in range(part * share, (part + 1) * share):
+            value = up_in[place].astype(jnp.float32) + down_in[place].astype(jnp.float32)
+            sums[place] = (value + own[place].astype(jnp.float32)).astype(jnp.bfloat16)
         writes[1 + part].start()
     for write in writes:
         write.wait()
@@ -150,7 +155,7 @@
 
 def newton_kernel(shard_rows, out_width, factor_ref, *refs):
     pieces = refs[:STREAMS]
-    out_ref, norm_ref, current, raw, gram, poly, staged, stores = refs[STREAMS:]
+    out_ref, norm_ref, current, gram, poly, staged, stores = refs[STREAMS:]
     height, columns = current.shape
     row_blocks, col_blocks = blocks_of(height), blocks_of(columns)
     everything = slice(0, height)
@@ -175,14 +180,13 @@
         product = outer(
             columns_at(pieces, row_blocks[i], span), columns_at(pieces, row_blocks[j], span)
         )
-        raw[row_blocks[i], row_blocks[j]] = product
+        mirrored(gram, i, j, product)
         if i == j:
             total = total + jnp.sum(jnp.where(diagonal, product, 0.0), keepdims=True)
     norm = jnp.sqrt(total)
     norm_ref[...] = jnp.broadcast_to(norm, norm_ref.shape)
     inverse = 1.0 / (norm + epsilon)
-    for i, j in pairs:
-        mirrored(gram, i, j, raw[row_blocks[i], row_blocks[j]] * inverse * inverse)
+    scale = inverse * inverse
     writes = []
     for sweep in range(ITERS):
         if sweep > 0:
@@ -193,6 +197,9 @@
                 gram[row_blocks[i]], gram[:, row_blocks[j]], preferred_element_type=jnp.float32
             )
             block = gram[row_blocks[i], row_blocks[j]].astype(jnp.float32)
+            if sweep == 0:
+                block = block * scale
+                squared = squared * scale * scale
             mirrored(poly, i, j, second_coef * block + third_coef * squared)
         for index, cols in enumerate(col_blocks):
             before = columns_at(pieces, everything, cols) if sweep == 0 else current[:, cols]
@@ -248,8 +255,11 @@
     shifts = dither[0].T
     whole = pl.BlockSpec(memory_space=pltpu.VMEM)
     anywhere = pl.BlockSpec(memory_space=pl.ANY)
+    outside = pl.BlockSpec(memory_space=pltpu.HBM)
     scalars = pl.BlockSpec(memory_space=pltpu.SMEM)
     table_scratch = pltpu.VMEM((shard_rows, 256), jnp.float32)
+
+    lean = pltpu.CompilerParams(vmem_limit_bytes=10 * 1024 * 1024)
 
     def shape_of(count, stream):
         return jax.ShapeDtypeStruct((count, shard_rows, WIDTHS[stream]), jnp.bfloat16)
@@ -263,13 +273,16 @@
     def cost_of(count, stream):
         moved = 6 * count * shard_rows * WIDTHS[stream]
         return pl.CostEstimate(flops=0, bytes_accessed=moved, transcendentals=0)
+
+    def remote(x):
+        return pltpu.with_memory_space_constraint(x, pltpu.HBM)
 
     def hop(step, stream, tables, received):
         count = half if step == 0 else per_group
         buffers = 2 if step == 0 else 4
         return pl.pallas_call(
             functools.partial(hop_kernel, step, half, STARTS[stream], group_count),
-            in_specs=[anywhere] * 3 + [whole] * len(received),
+            in_specs=[outside] * 3 + [whole] * len(received),
             out_specs=[anywhere, anywhere],
             out_shape=[shape_of(count, stream)] * 2,
             scratch_shapes=[
@@ -282,13 +295,32 @@
                 pltpu.SemaphoreType.DMA((buffers,)),
             ],
             cost_estimate=cost_of(count, stream),
-        )(codes, *tables, *[local(x) for x in received])
+            compiler_params=lean,
+        )(remote(codes), *[remote(x) for x in tables], *[local(x) for x in received])
 
     def send(blocks):
         rising = lax.ppermute(blocks[0], "group", up)
         falling = lax.ppermute(blocks[1], "group", down)
         return rising, falling
 
+    def own(stream, tables):
+        return pl.pallas_call(
+            functools.partial(own_kernel, half, STARTS[stream]),
+            in_specs=[outside] * 3,
+            out_specs=whole,
+            out_shape=shape_of(per_group, stream),
+            scratch_shapes=[
+                buffers_of(2, stream),
+                pltpu.VMEM((2, shard_rows, matrices), jnp.float32),
+                table_scratch,
+                pltpu.SemaphoreType.DMA((2,)),
+                pltpu.SemaphoreType.DMA((2,)),
+            ],
+            cost_estimate=cost_of(per_group, stream),
+            compiler_params=lean,
+        )(remote(codes), *[remote(x) for x in tables])
+
+    owns = []
     pending = [()] * STREAMS
     tables = (scales, shifts)
     previous = None
@@ -297,28 +329,28 @@
             if previous is not None:
                 tables, blocks = lax.optimization_barrier((tables, previous[2]))
                 pending[previous[1]] = send(blocks)
+            if (step, stream) == (reach - 1, STREAMS - 1):
+                for each in range(STREAMS):
+                    owns.append(own(each, tables))
+                    tables, owns[each] = lax.optimization_barrier((tables, owns[each]))
             previous = (step, stream, hop(step, stream, tables, pending[stream]))
-    tables, blocks = lax.optimization_barrier((tables, previous[2]))
+    owns, blocks = lax.optimization_barrier((owns, previous[2]))
     pending[previous[1]] = send(blocks)
     pieces = []
     for stream in range(STREAMS):
         padded = pl.pallas_call(
-            functools.partial(last_kernel, half, STARTS[stream]),
-            in_specs=[anywhere] * 3 + [whole] * 2,
+            last_kernel,
+            in_specs=[whole] * 3,
             out_specs=anywhere,
             out_shape=shape_of(owner_count, stream),
             scratch_shapes=[
-                buffers_of(2, stream),
-                pltpu.VMEM((2, shard_rows, matrices), jnp.float32),
-                table_scratch,
                 pltpu.VMEM(shape_of(owner_count, stream).shape, jnp.bfloat16),
-                pltpu.SemaphoreType.DMA((2,)),
-                pltpu.SemaphoreType.DMA((2,)),
-                pltpu.SemaphoreType.DMA((3,)),
+                pltpu.SemaphoreType.DMA((5,)),
             ],
             cost_estimate=cost_of(owner_count, stream),
-        )(codes, *tables, *[local(x) for x in pending[stream]])
-        tables, padded = lax.optimization_barrier((tables, padded))
+            compiler_params=lean,
+        )(local(owns[stream]), *[local(x) for x in pending[stream]])
+        owns, padded = lax.optimization_barrier((owns, padded))
         arrived = lax.all_to_all(padded, "dp", split_axis=0, concat_axis=0, tiled=True)
         pieces.append(arrived.reshape(height, WIDTHS[stream]))
 
@@ -336,7 +368,6 @@
         ],
         scratch_shapes=[
             pltpu.VMEM((height, columns), jnp.bfloat16),
-            pltpu.VMEM((height, height), jnp.float32),
             pltpu.VMEM((height, height), jnp.bfloat16),
             pltpu.VMEM((height, height), jnp.bfloat16),
             pltpu.VMEM((2, TILE // out_width * owner_count, shard_rows, out_width), jnp.bfloat16),
@@ -348,7 +379,7 @@
             bytes_accessed=4 * height * columns,
             transcendentals=0,
         ),
-        compiler_params=pltpu.CompilerParams(vmem_limit_bytes=40 * 1024 * 1024),
+        compiler_params=pltpu.CompilerParams(vmem_limit_bytes=20 * 1024 * 1024),
     )(factor, *[local(x) for x in pieces])
     returned = lax.all_to_all(blocks_out, ("group", "dp"), split_axis=0, concat_axis=0, tiled=True)
     returned = returned.reshape(group_count, owner_count, shard_rows, out_width)

time: 212 us -> 207 us (0.976)
  starting transfers between devices: 55.9 us -> 52.4 us
    all_to_all x2, starting transfers between devices: 18.5 us -> 15.1 us  [program(): lax.all_to_all(padded, 'dp', split_axis=0, concat_axis=0, tiled=True)]
    pallas_call x2 -> x4, Pallas kernels: 4.41 us -> 4.62 us  [the longest x2 2.74 us: own(): pl.pallas_call(functools.partial(own_kernel, half, STARTS[stream]), in_sp...]
  transfers between devices with their start and end apart: 24 -> 24, of which waited for: 12 -> 12; matrix products, arithmetic and copies ran while one was open for 1% -> 1% of each run, Pallas kernels for 7% -> 8%
where the time goes in v4:
time: 207 us; the launch traced here: 206 us
  waiting for transfers between devices  116 us (56%)
  starting transfers between devices  52.4 us (25%)
  Pallas kernels  32.9 us (16%)
    ppermute x8, waiting for transfers between devices, send(): rising = lax.ppermute(blocks[0], 'group', up)  56.8 us
    all_to_all x2, waiting for transfers between devices, program(): lax.all_to_all(padded, 'dp', split_axis=0, concat_axis=0, tiled=True)  22.8 us
    ppermute x8, starting transfers between devices, send(): falling = lax.ppermute(blocks[1], 'group', down)  21.1 us
    pallas_call x8, Pallas kernels, hop(): pl.pallas_call(functools.partial(hop_kernel, step, half, STARTS[stream],...  20.9 us
    all_to_all x1, waiting for transfers between devices, program(): lax.all_to_all(blocks_out, ('group', 'dp'), split_axis=0, concat_axis=0,...  20.9 us
    ppermute x5, waiting for transfers between devices, program(): other = lax.ppermute(norms, 'dp', partner)  15.8 us
    all_to_all x2, starting transfers between devices, program(): lax.all_to_all(padded, 'dp', split_axis=0, concat_axis=0, tiled=True)  15.1 us
    all_to_all x1, starting transfers between devices, program(): lax.all_to_all(blocks_out, ('group', 'dp'), split_axis=0, concat_axis=0,...  7.57 us
  transfers between devices with their start and end apart: 24, of which 12 were waited for; matrix products, arithmetic and copies ran while one was open for 1% of the time, Pallas kernels for 8%

profile of v4, /device:TPU:1, one launch (start us, length us, event | category | flops | bytes accessed | tf_op | source)
XLA Modules:
  0.0 206.2 jit_solution(2780533531821931335)
XLA Ops:
  0.6 1.9 shard_map.68
  2.6 1.7 shard_map.69
  4.3 2.5 %collective-permute-start.2 = (bf16[12,24,640]{2,1,0:T(8,128)(2,1)S(1)}, bf16[12,24,640]{2,1,0:T(8,128)(2,1)S(1)}, u32[]{:S(2)}, u32[]{:S(2)}) collective-permute-start(bf16[12,24,640]{2,1,0:T(8,128)(2,1)S(1)} %get-tuple-element.75), channel_id=1, source_target_pairs={{0,1},{1,2},{2,3},{3,4},{4,5},{5,6},{6,7},{7,0},{8,9},{9,10},{10,1... | collective-permute-start | bytes 1105928 | tf_op jit(solution)/shard_map/ppermute | solution.py:302
  6.8 4.0 %collective-permute-start.3 = (bf16[12,24,640]{2,1,0:T(8,128)(2,1)S(1)}, bf16[12,24,640]{2,1,0:T(8,128)(2,1)S(1)}, u32[]{:S(2)}, u32[]{:S(2)}) collective-permute-start(bf16[12,24,640]{2,1,0:T(8,128)(2,1)S(1)} %get-tuple-element.76), channel_id=1, source_target_pairs={{0,7},{1,0},{2,1},{3,2},{4,3},{5,4},{6,5},{7,6},{8,15},{9,8},{10,9... | collective-permute-start | bytes 1105928 | tf_op jit(solution)/shard_map/ppermute | solution.py:303
  10.9 2.7 %collective-permute-start.1 = (bf16[12,24,384]{2,1,0:T(8,128)(2,1)S(1)}, bf16[12,24,384]{2,1,0:T(8,128)(2,1)S(1)}, u32[]{:S(2)}, u32[]{:S(2)}) collective-permute-start(bf16[12,24,384]{2,1,0:T(8,128)(2,1)S(1)} %get-tuple-element.70), channel_id=1, source_target_pairs={{0,7},{1,0},{2,1},{3,2},{4,3},{5,4},{6,5},{7,6},{8,15},{9,8},{10,9... | collective-permute-start | bytes 663560 | tf_op jit(solution)/shard_map/ppermute | solution.py:303
  13.5 10.3 %collective-permute-done.refs_0_ = bf16[12,24,384]{2,1,0:T(8,128)(2,1)S(1)} collective-permute-done((bf16[12,24,384]{2,1,0:T(8,128)(2,1)S(1)}, bf16[12,24,384]{2,1,0:T(8,128)(2,1)S(1)}, u32[]{:S(2)}, u32[]{:S(2)}) %collective-permute-start) | collective-permute-done | bytes 221216 | tf_op jit(solution)/shard_map/ppermute | solution.py:302
  23.8 3.1 %shard_map.70 = (bf16[24,24,384]{2,1,0:T(8,128)(2,1)S(1)}, bf16[24,24,384]{2,1,0:T(8,128)(2,1)S(1)}) custom-call(bf16[192,24,1024]{2,1,0:T(8,128)(2,1)} %bitcast.20, f32[24,192]{1,0:T(8,128)} %bitcast.31, f32[24,192]{1,0:T(8,128)} %bitcast.41, bf16[12,24,384]{2,1,0:T(8,128)(2,1)S(1)} %collective-permute-done.refs_0_, ...), custom_call_target="tpu_custom_call" | custom-call | bytes 1327104 | tf_op jit(solution)/shard_map/pallas_call | solution.py:283
  26.9 2.6 %shard_map.71 = (bf16[24,24,640]{2,1,0:T(8,128)(2,1)S(1)}, bf16[24,24,640]{2,1,0:T(8,128)(2,1)S(1)}) custom-call(bf16[192,24,1024]{2,1,0:T(8,128)(2,1)} %bitcast.21, f32[24,192]{1,0:T(8,128)} %bitcast.32, f32[24,192]{1,0:T(8,128)} %bitcast.42, bf16[12,24,640]{2,1,0:T(8,128)(2,1)S(1)} %collective-permute-done.2.refs_0_, ...), custom_call_target="tpu_custom_call" | custom-call | bytes 2211840 | tf_op jit(solution)/shard_map/pallas_call | solution.py:283
  29.6 2.7 %collective-permute-start.7 = (bf16[24,24,640]{2,1,0:T(8,128)(2,1)S(1)}, bf16[24,24,640]{2,1,0:T(8,128)(2,1)S(1)}, u32[]{:S(2)}, u32[]{:S(2)}) collective-permute-start(bf16[24,24,640]{2,1,0:T(8,128)(2,1)S(1)} %get-tuple-element.88), channel_id=1, source_target_pairs={{0,7},{1,0},{2,1},{3,2},{4,3},{5,4},{6,5},{7,6},{8,15},{9,8},{10,9... | collective-permute-start | bytes 2211848 | tf_op jit(solution)/shard_map/ppermute | solution.py:303
  32.3 2.7 %collective-permute-start.5 = (bf16[24,24,384]{2,1,0:T(8,128)(2,1)S(1)}, bf16[24,24,384]{2,1,0:T(8,128)(2,1)S(1)}, u32[]{:S(2)}, u32[]{:S(2)}) collective-permute-start(bf16[24,24,384]{2,1,0:T(8,128)(2,1)S(1)} %get-tuple-element.82), channel_id=1, source_target_pairs={{0,7},{1,0},{2,1},{3,2},{4,3},{5,4},{6,5},{7,6},{8,15},{9,8},{10,9... | collective-permute-start | bytes 1327112 | tf_op jit(solution)/shard_map/ppermute | solution.py:303
  35.0 22.1 %collective-permute-done.4.refs_0_ = bf16[24,24,384]{2,1,0:T(8,128)(2,1)S(1)} collective-permute-done((bf16[24,24,384]{2,1,0:T(8,128)(2,1)S(1)}, bf16[24,24,384]{2,1,0:T(8,128)(2,1)S(1)}, u32[]{:S(2)}, u32[]{:S(2)}) %collective-permute-start.4) | collective-permute-done | bytes 442400 | tf_op jit(solution)/shard_map/ppermute | solution.py:302
  57.1 3.1 %shard_map.72 = (bf16[24,24,384]{2,1,0:T(8,128)(2,1)S(1)}, bf16[24,24,384]{2,1,0:T(8,128)(2,1)S(1)}) custom-call(bf16[192,24,1024]{2,1,0:T(8,128)(2,1)} %bitcast.22, f32[24,192]{1,0:T(8,128)} %bitcast.33, f32[24,192]{1,0:T(8,128)} %bitcast.43, bf16[24,24,384]{2,1,0:T(8,128)(2,1)S(1)} %collective-permute-done.4.refs_0_, ...), custom_call_target="tpu_custom_call" | custom-call | bytes 1327104 | tf_op jit(solution)/shard_map/pallas_call | solution.py:283
  60.2 2.7 %shard_map.73 = (bf16[24,24,640]{2,1,0:T(8,128)(2,1)S(1)}, bf16[24,24,640]{2,1,0:T(8,128)(2,1)S(1)}) custom-call(bf16[192,24,1024]{2,1,0:T(8,128)(2,1)} %bitcast.23, f32[24,192]{1,0:T(8,128)} %bitcast.34, f32[24,192]{1,0:T(8,128)} %bitcast.44, bf16[24,24,640]{2,1,0:T(8,128)(2,1)S(1)} %collective-permute-done.6.refs_0_, ...), custom_call_target="tpu_custom_call" | custom-call | bytes 2211840 | tf_op jit(solution)/shard_map/pallas_call | solution.py:283
  62.9 1.1 collective-permute-start.10
  64.0 1.6 collective-permute-start.11
  65.6 2.7 %collective-permute-start.9 = (bf16[24,24,384]{2,1,0:T(8,128)(2,1)S(1)}, bf16[24,24,384]{2,1,0:T(8,128)(2,1)S(1)}, u32[]{:S(2)}, u32[]{:S(2)}) collective-permute-start(bf16[24,24,384]{2,1,0:T(8,128)(2,1)S(1)} %get-tuple-element.94), channel_id=1, source_target_pairs={{0,7},{1,0},{2,1},{3,2},{4,3},{5,4},{6,5},{7,6},{8,15},{9,8},{10,9... | collective-permute-start | bytes 1327112 | tf_op jit(solution)/shard_map/ppermute | solution.py:303
  68.3 21.3 %collective-permute-done.8.refs_0_ = bf16[24,24,384]{2,1,0:T(8,128)(2,1)S(1)} collective-permute-done((bf16[24,24,384]{2,1,0:T(8,128)(2,1)S(1)}, bf16[24,24,384]{2,1,0:T(8,128)(2,1)S(1)}, u32[]{:S(2)}, u32[]{:S(2)}) %collective-permute-start.8) | collective-permute-done | bytes 442400 | tf_op jit(solution)/shard_map/ppermute | solution.py:302
  89.6 3.1 %shard_map.74 = (bf16[24,24,384]{2,1,0:T(8,128)(2,1)S(1)}, bf16[24,24,384]{2,1,0:T(8,128)(2,1)S(1)}) custom-call(bf16[192,24,1024]{2,1,0:T(8,128)(2,1)} %bitcast.24, f32[24,192]{1,0:T(8,128)} %bitcast.35, f32[24,192]{1,0:T(8,128)} %bitcast.45, bf16[24,24,384]{2,1,0:T(8,128)(2,1)S(1)} %collective-permute-done.8.refs_0_, ...), custom_call_target="tpu_custom_call" | custom-call | bytes 1327104 | tf_op jit(solution)/shard_map/pallas_call | solution.py:283
  92.7 0.6 collective-permute-start.12
  93.3 2.1 %collective-permute-start.13 = (bf16[24,24,384]{2,1,0:T(8,128)(2,1)S(1)}, bf16[24,24,384]{2,1,0:T(8,128)(2,1)S(1)}, u32[]{:S(2)}, u32[]{:S(2)}) collective-permute-start(bf16[24,24,384]{2,1,0:T(8,128)(2,1)S(1)} %get-tuple-element.112), channel_id=1, source_target_pairs={{0,7},{1,0},{2,1},{3,2},{4,3},{5,4},{6,5},{7,6},{8,15},{9,8},{10,9... | collective-permute-start | bytes 1327112 | tf_op jit(solution)/shard_map/ppermute | solution.py:303
  95.4 1.3 shard_map.75.own
  96.8 1.4 shard_map.76.own
  98.2 2.8 %shard_map.77 = (bf16[24,24,640]{2,1,0:T(8,128)(2,1)}, bf16[24,24,640]{2,1,0:T(8,128)(2,1)S(1)}) custom-call(bf16[192,24,1024]{2,1,0:T(8,128)(2,1)} %bitcast.27, f32[24,192]{1,0:T(8,128)} %bitcast.38, f32[24,192]{1,0:T(8,128)} %bitcast.48, bf16[24,24,640]{2,1,0:T(8,128)(2,1)S(1)} %collective-permute-done.10.refs_0_, ...), custom_call_target="tpu_custom_call" | custom-call | bytes 2211840 | tf_op jit(solution)/shard_map/pallas_call | solution.py:283
  101.1 2.7 %collective-permute-start.15 = (bf16[24,24,640]{2,1,0:T(8,128)(2,1)S(1)}, bf16[24,24,640]{2,1,0:T(8,128)(2,1)S(1)}, u32[]{:S(2)}, u32[]{:S(2)}) collective-permute-start(bf16[24,24,640]{2,1,0:T(8,128)(2,1)S(1)} %get-tuple-element.116), channel_id=1, source_target_pairs={{0,7},{1,0},{2,1},{3,2},{4,3},{5,4},{6,5},{7,6},{8,15},{9,8},{10,9... | collective-permute-start | bytes 2211848 | tf_op jit(solution)/shard_map/ppermute | solution.py:303
  103.7 0.9 shard_map.78
  104.6 11.2 %all-to-all-start = ((bf16[32,24,384]{2,1,0:T(8,128)(2,1)}), bf16[32,24,384]{2,1,0:T(8,128)(2,1)S(1)}, u32[]{:S(2)}, u32[]{:S(2)}) async-start(bf16[32,24,384]{2,1,0:T(8,128)(2,1)} %shard_map.78), calls=%async_computation | async-start | bytes 1179648 | tf_op jit(solution)/shard_map/all_to_all | solution.py:354
  115.8 3.1 %collective-permute-done.14.up_in = bf16[24,24,640]{2,1,0:T(8,128)(2,1)S(1)} collective-permute-done((bf16[24,24,640]{2,1,0:T(8,128)(2,1)}, bf16[24,24,640]{2,1,0:T(8,128)(2,1)S(1)}, u32[]{:S(2)}, u32[]{:S(2)}) %collective-permute-start.14) | collective-permute-done | bytes 737312 | tf_op jit(solution)/shard_map/ppermute | solution.py:302
  119.0 1.0 shard_map.79
  120.0 8.1 %all-to-all-done = bf16[32,24,384]{2,1,0:T(8,128)(2,1)S(1)} async-done(((bf16[32,24,384]{2,1,0:T(8,128)(2,1)}), bf16[32,24,384]{2,1,0:T(8,128)(2,1)S(1)}, u32[]{:S(2)}, u32[]{:S(2)}) %all-to-all-start) | async-done | bytes 589856 | tf_op jit(solution)/shard_map/all_to_all | solution.py:354
  128.1 3.9 %all-to-all-start.1 = ((bf16[32,24,640]{2,1,0:T(8,128)(2,1)}), bf16[32,24,640]{2,1,0:T(8,128)(2,1)S(1)}, u32[]{:S(2)}, u32[]{:S(2)}) async-start(bf16[32,24,640]{2,1,0:T(8,128)(2,1)} %shard_map.79), calls=%async_computation.1 | async-start | bytes 1966080 | tf_op jit(solution)/shard_map/all_to_all | solution.py:354
  132.0 0.6 dynamic_slice.6
  133.3 14.7 %all-to-all-done.1 = bf16[32,24,640]{2,1,0:T(8,128)(2,1)S(1)} async-done(((bf16[32,24,640]{2,1,0:T(8,128)(2,1)}), bf16[32,24,640]{2,1,0:T(8,128)(2,1)S(1)}, u32[]{:S(2)}, u32[]{:S(2)}) %all-to-all-start.1) | async-done | bytes 983072 | tf_op jit(solution)/shard_map/all_to_all | solution.py:354
  148.0 7.4 %newton.1 = (bf16[256,24,128]{2,1,0:T(8,128)(2,1)}, f32[8,128]{1,0:T(8,128)S(1)}) custom-call(f32[1]{0:T(128)S(6)} %select_n.75.factor_ref, bf16[768,384]{1,0:T(8,128)(2,1)S(1)} %bitcast.16, bf16[768,640]{1,0:T(8,128)(2,1)S(1)} %bitcast.15), custom_call_target="tpu_custom_call" | custom-call | flops 6643777536 | bytes 3145728 | tf_op jit(solution)/shard_map/newton/pallas_call | solution.py:361
  155.4 7.6 %all-to-all-start.2 = ((bf16[256,24,128]{2,1,0:T(8,128)(2,1)}), bf16[256,24,128]{2,1,0:T(8,128)(2,1)S(1)}, u32[]{:S(2)}, u32[]{:S(2)}) async-start(bf16[256,24,128]{2,1,0:T(8,128)(2,1)} %get-tuple-element.118), calls=%async_computation.2 | async-start | bytes 3145728 | tf_op jit(solution)/shard_map/all_to_all | solution.py:384
  162.9 2.2 %collective-permute-start.16 = (f32[1,8,128]{2,1,0:T(8,128)S(1)}, f32[1,8,128]{2,1,0:T(8,128)S(1)}, u32[]{:S(2)}, u32[]{:S(2)}) collective-permute-start(f32[1,8,128]{2,1,0:T(8,128)S(1)} %bitcast.17), channel_id=1, source_target_pairs={{0,8},{8,0},{16,24},{24,16},{32,40},{40,32},{48,56},{56,48},{64,72... | collective-permute-start | bytes 12296 | tf_op jit(solution)/shard_map/ppermute | solution.py:392
  165.2 0.8 collective-permute-done.16
  166.0 3.1 %collective-permute-done.17 = f32[2,8,128]{2,1,0:T(8,128)S(1)} collective-permute-done((f32[2,8,128]{2,1,0:T(8,128)S(1)}, f32[2,8,128]{2,1,0:T(8,128)S(1)}, u32[]{:S(2)}, u32[]{:S(2)}) %collective-permute-start.17) | collective-permute-done | bytes 8224 | tf_op jit(solution)/shard_map/ppermute | solution.py:392
  169.1 1.3 collective-permute-start.18
  170.5 3.4 %collective-permute-done.18 = f32[4,8,128]{2,1,0:T(8,128)S(1)} collective-permute-done((f32[4,8,128]{2,1,0:T(8,128)S(1)}, f32[4,8,128]{2,1,0:T(8,128)S(1)}, u32[]{:S(2)}, u32[]{:S(2)}) %collective-permute-start.18) | collective-permute-done | bytes 16416 | tf_op jit(solution)/shard_map/ppermute | solution.py:392
  173.9 0.1 collective-permute-start.19
  174.1 3.5 %collective-permute-done.19 = f32[8,8,128]{2,1,0:T(8,128)S(1)} collective-permute-done((f32[8,8,128]{2,1,0:T(8,128)S(1)}, f32[8,8,128]{2,1,0:T(8,128)S(1)}, u32[]{:S(2)}, u32[]{:S(2)}) %collective-permute-start.19) | collective-permute-done | bytes 32800 | tf_op jit(solution)/shard_map/ppermute | solution.py:392
  177.5 0.4 collective-permute-start.20
  178.0 0.2 convert_reduce_fusion
  178.1 5.0 %collective-permute-done.20 = f32[16,8,128]{2,1,0:T(8,128)S(1)} collective-permute-done((f32[16,8,128]{2,1,0:T(8,128)S(1)}, f32[16,8,128]{2,1,0:T(8,128)S(1)}, u32[]{:S(2)}, u32[]{:S(2)}) %collective-permute-start.20) | collective-permute-done | bytes 65568 | tf_op jit(solution)/shard_map/ppermute | solution.py:392
  183.2 0.3 fusion.2
  183.4 0.6 fusion.3
  184.1 20.9 %all-to-all-done.2 = bf16[256,24,128]{2,1,0:T(8,128)(2,1)S(1)} async-done(((bf16[256,24,128]{2,1,0:T(8,128)(2,1)}), bf16[256,24,128]{2,1,0:T(8,128)(2,1)S(1)}, u32[]{:S(2)}, u32[]{:S(2)}) %all-to-all-start.2) | async-done | bytes 1572896 | tf_op jit(solution)/shard_map/all_to_all | solution.py:384
  204.9 1.2 slice.8
  (32 shorter events, 0.4 us)
Async XLA Ops:
  4.3 22.6 %collective-permute-start.2 = (bf16[12,24,640]{2,1,0:T(8,128)(2,1)S(1)}, bf16[12,24,640]{2,1,0:T(8,128)(2,1)S(1)}, u32[]{:S(2)}, u32[]{:S(2)}) collective-permute-start(bf16[12,24,640]{2,1,0:T(8,128)(2,1)S(1)} %get-tuple-element.75), channel_id=1, source_target_pairs={{0,1},{1,2},{2,3},{3,4},{4,5},{5,6},{6,7},{7,0},{8,9},{9,10},{10,1... | collective-permute-start | bytes 1105928 | tf_op jit(solution)/shard_map/ppermute | solution.py:302
  6.8 20.1 %collective-permute-start.3 = (bf16[12,24,640]{2,1,0:T(8,128)(2,1)S(1)}, bf16[12,24,640]{2,1,0:T(8,128)(2,1)S(1)}, u32[]{:S(2)}, u32[]{:S(2)}) collective-permute-start(bf16[12,24,640]{2,1,0:T(8,128)(2,1)S(1)} %get-tuple-element.76), channel_id=1, source_target_pairs={{0,7},{1,0},{2,1},{3,2},{4,3},{5,4},{6,5},{7,6},{8,15},{9,8},{10,9... | collective-permute-start | bytes 1105928 | tf_op jit(solution)/shard_map/ppermute | solution.py:303
  10.8 12.9 %collective-permute-start = (bf16[12,24,384]{2,1,0:T(8,128)(2,1)S(1)}, bf16[12,24,384]{2,1,0:T(8,128)(2,1)S(1)}, u32[]{:S(2)}, u32[]{:S(2)}) collective-permute-start(bf16[12,24,384]{2,1,0:T(8,128)(2,1)S(1)} %get-tuple-element.69), channel_id=1, source_target_pairs={{0,1},{1,2},{2,3},{3,4},{4,5},{5,6},{6,7},{7,0},{8,9},{9,10},{10,1... | collective-permute-start | bytes 663560 | tf_op jit(solution)/shard_map/ppermute | solution.py:302
  10.9 12.9 %collective-permute-start.1 = (bf16[12,24,384]{2,1,0:T(8,128)(2,1)S(1)}, bf16[12,24,384]{2,1,0:T(8,128)(2,1)S(1)}, u32[]{:S(2)}, u32[]{:S(2)}) collective-permute-start(bf16[12,24,384]{2,1,0:T(8,128)(2,1)S(1)} %get-tuple-element.70), channel_id=1, source_target_pairs={{0,7},{1,0},{2,1},{3,2},{4,3},{5,4},{6,5},{7,6},{8,15},{9,8},{10,9... | collective-permute-start | bytes 663560 | tf_op jit(solution)/shard_map/ppermute | solution.py:303
  29.5 30.7 %collective-permute-start.6 = (bf16[24,24,640]{2,1,0:T(8,128)(2,1)S(1)}, bf16[24,24,640]{2,1,0:T(8,128)(2,1)S(1)}, u32[]{:S(2)}, u32[]{:S(2)}) collective-permute-start(bf16[24,24,640]{2,1,0:T(8,128)(2,1)S(1)} %get-tuple-element.87), channel_id=1, source_target_pairs={{0,1},{1,2},{2,3},{3,4},{4,5},{5,6},{6,7},{7,0},{8,9},{9,10},{10,1... | collective-permute-start | bytes 2211848 | tf_op jit(solution)/shard_map/ppermute | solution.py:302
  29.6 30.6 %collective-permute-start.7 = (bf16[24,24,640]{2,1,0:T(8,128)(2,1)S(1)}, bf16[24,24,640]{2,1,0:T(8,128)(2,1)S(1)}, u32[]{:S(2)}, u32[]{:S(2)}) collective-permute-start(bf16[24,24,640]{2,1,0:T(8,128)(2,1)S(1)} %get-tuple-element.88), channel_id=1, source_target_pairs={{0,7},{1,0},{2,1},{3,2},{4,3},{5,4},{6,5},{7,6},{8,15},{9,8},{10,9... | collective-permute-start | bytes 2211848 | tf_op jit(solution)/shard_map/ppermute | solution.py:303
  32.3 24.8 %collective-permute-start.4 = (bf16[24,24,384]{2,1,0:T(8,128)(2,1)S(1)}, bf16[24,24,384]{2,1,0:T(8,128)(2,1)S(1)}, u32[]{:S(2)}, u32[]{:S(2)}) collective-permute-start(bf16[24,24,384]{2,1,0:T(8,128)(2,1)S(1)} %get-tuple-element.81), channel_id=1, source_target_pairs={{0,1},{1,2},{2,3},{3,4},{4,5},{5,6},{6,7},{7,0},{8,9},{9,10},{10,1... | collective-permute-start | bytes 1327112 | tf_op jit(solution)/shard_map/ppermute | solution.py:302
  32.3 24.8 %collective-permute-start.5 = (bf16[24,24,384]{2,1,0:T(8,128)(2,1)S(1)}, bf16[24,24,384]{2,1,0:T(8,128)(2,1)S(1)}, u32[]{:S(2)}, u32[]{:S(2)}) collective-permute-start(bf16[24,24,384]{2,1,0:T(8,128)(2,1)S(1)} %get-tuple-element.82), channel_id=1, source_target_pairs={{0,7},{1,0},{2,1},{3,2},{4,3},{5,4},{6,5},{7,6},{8,15},{9,8},{10,9... | collective-permute-start | bytes 1327112 | tf_op jit(solution)/shard_map/ppermute | solution.py:303
  62.9 35.3 %collective-permute-start.10 = (bf16[24,24,640]{2,1,0:T(8,128)(2,1)S(1)}, bf16[24,24,640]{2,1,0:T(8,128)(2,1)S(1)}, u32[]{:S(2)}, u32[]{:S(2)}) collective-permute-start(bf16[24,24,640]{2,1,0:T(8,128)(2,1)S(1)} %get-tuple-element.105), channel_id=1, source_target_pairs={{0,1},{1,2},{2,3},{3,4},{4,5},{5,6},{6,7},{7,0},{8,9},{9,10},{10,1... | collective-permute-start | bytes 2211848 | tf_op jit(solution)/shard_map/ppermute | solution.py:302
  64.0 34.2 %collective-permute-start.11 = (bf16[24,24,640]{2,1,0:T(8,128)(2,1)S(1)}, bf16[24,24,640]{2,1,0:T(8,128)(2,1)S(1)}, u32[]{:S(2)}, u32[]{:S(2)}) collective-permute-start(bf16[24,24,640]{2,1,0:T(8,128)(2,1)S(1)} %get-tuple-element.106), channel_id=1, source_target_pairs={{0,7},{1,0},{2,1},{3,2},{4,3},{5,4},{6,5},{7,6},{8,15},{9,8},{10,9... | collective-permute-start | bytes 2211848 | tf_op jit(solution)/shard_map/ppermute | solution.py:303
  65.6 24.0 %collective-permute-start.8 = (bf16[24,24,384]{2,1,0:T(8,128)(2,1)S(1)}, bf16[24,24,384]{2,1,0:T(8,128)(2,1)S(1)}, u32[]{:S(2)}, u32[]{:S(2)}) collective-permute-start(bf16[24,24,384]{2,1,0:T(8,128)(2,1)S(1)} %get-tuple-element.93), channel_id=1, source_target_pairs={{0,1},{1,2},{2,3},{3,4},{4,5},{5,6},{6,7},{7,0},{8,9},{9,10},{10,1... | collective-permute-start | bytes 1327112 | tf_op jit(solution)/shard_map/ppermute | solution.py:302
  65.6 24.0 %collective-permute-start.9 = (bf16[24,24,384]{2,1,0:T(8,128)(2,1)S(1)}, bf16[24,24,384]{2,1,0:T(8,128)(2,1)S(1)}, u32[]{:S(2)}, u32[]{:S(2)}) collective-permute-start(bf16[24,24,384]{2,1,0:T(8,128)(2,1)S(1)} %get-tuple-element.94), channel_id=1, source_target_pairs={{0,7},{1,0},{2,1},{3,2},{4,3},{5,4},{6,5},{7,6},{8,15},{9,8},{10,9... | collective-permute-start | bytes 1327112 | tf_op jit(solution)/shard_map/ppermute | solution.py:303
  92.7 11.0 %collective-permute-start.12 = (bf16[24,24,384]{2,1,0:T(8,128)(2,1)S(1)}, bf16[24,24,384]{2,1,0:T(8,128)(2,1)S(1)}, u32[]{:S(2)}, u32[]{:S(2)}) collective-permute-start(bf16[24,24,384]{2,1,0:T(8,128)(2,1)S(1)} %get-tuple-element.111), channel_id=1, source_target_pairs={{0,1},{1,2},{2,3},{3,4},{4,5},{5,6},{6,7},{7,0},{8,9},{9,10},{10,1... | collective-permute-start | bytes 1327112 | tf_op jit(solution)/shard_map/ppermute | solution.py:302
  93.3 10.4 %collective-permute-start.13 = (bf16[24,24,384]{2,1,0:T(8,128)(2,1)S(1)}, bf16[24,24,384]{2,1,0:T(8,128)(2,1)S(1)}, u32[]{:S(2)}, u32[]{:S(2)}) collective-permute-start(bf16[24,24,384]{2,1,0:T(8,128)(2,1)S(1)} %get-tuple-element.112), channel_id=1, source_target_pairs={{0,7},{1,0},{2,1},{3,2},{4,3},{5,4},{6,5},{7,6},{8,15},{9,8},{10,9... | collective-permute-start | bytes 1327112 | tf_op jit(solution)/shard_map/ppermute | solution.py:303
  101.0 18.0 %collective-permute-start.14 = (bf16[24,24,640]{2,1,0:T(8,128)(2,1)}, bf16[24,24,640]{2,1,0:T(8,128)(2,1)S(1)}, u32[]{:S(2)}, u32[]{:S(2)}) collective-permute-start(bf16[24,24,640]{2,1,0:T(8,128)(2,1)} %get-tuple-element.115), channel_id=1, source_target_pairs={{0,1},{1,2},{2,3},{3,4},{4,5},{5,6},{6,7},{7,0},{8,9},{9,10},{10,1... | collective-permute-start | bytes 2211848 | tf_op jit(solution)/shard_map/ppermute | solution.py:302
  101.1 17.9 %collective-permute-start.15 = (bf16[24,24,640]{2,1,0:T(8,128)(2,1)S(1)}, bf16[24,24,640]{2,1,0:T(8,128)(2,1)S(1)}, u32[]{:S(2)}, u32[]{:S(2)}) collective-permute-start(bf16[24,24,640]{2,1,0:T(8,128)(2,1)S(1)} %get-tuple-element.116), channel_id=1, source_target_pairs={{0,7},{1,0},{2,1},{3,2},{4,3},{5,4},{6,5},{7,6},{8,15},{9,8},{10,9... | collective-permute-start | bytes 2211848 | tf_op jit(solution)/shard_map/ppermute | solution.py:303
  104.6 23.4 %all-to-all-start = ((bf16[32,24,384]{2,1,0:T(8,128)(2,1)}), bf16[32,24,384]{2,1,0:T(8,128)(2,1)S(1)}, u32[]{:S(2)}, u32[]{:S(2)}) async-start(bf16[32,24,384]{2,1,0:T(8,128)(2,1)} %shard_map.78), calls=%async_computation | async-start | bytes 1179648 | tf_op jit(solution)/shard_map/all_to_all | solution.py:354
  120.0 12.1 %copy-start.1 = (s32[192]{0:T(256)S(1)}, s32[192]{0:T(256)}, u32[]{:S(2)}) copy-start(s32[192]{0:T(256)} %param.9) | copy-start | bytes 2308
  128.1 19.9 %all-to-all-start.1 = ((bf16[32,24,640]{2,1,0:T(8,128)(2,1)}), bf16[32,24,640]{2,1,0:T(8,128)(2,1)S(1)}, u32[]{:S(2)}, u32[]{:S(2)}) async-start(bf16[32,24,640]{2,1,0:T(8,128)(2,1)} %shard_map.79), calls=%async_computation.1 | async-start | bytes 1966080 | tf_op jit(solution)/shard_map/all_to_all | solution.py:354
  155.4 18.6 %copy-start = (s32[192]{0:T(256)S(1)}, s32[192]{0:T(256)}, u32[]{:S(2)}) copy-start(s32[192]{0:T(256)} %param.8) | copy-start | bytes 2308
  155.4 49.6 %all-to-all-start.2 = ((bf16[256,24,128]{2,1,0:T(8,128)(2,1)}), bf16[256,24,128]{2,1,0:T(8,128)(2,1)S(1)}, u32[]{:S(2)}, u32[]{:S(2)}) async-start(bf16[256,24,128]{2,1,0:T(8,128)(2,1)} %get-tuple-element.118), calls=%async_computation.2 | async-start | bytes 3145728 | tf_op jit(solution)/shard_map/all_to_all | solution.py:384
  162.9 3.1 %collective-permute-start.16 = (f32[1,8,128]{2,1,0:T(8,128)S(1)}, f32[1,8,128]{2,1,0:T(8,128)S(1)}, u32[]{:S(2)}, u32[]{:S(2)}) collective-permute-start(f32[1,8,128]{2,1,0:T(8,128)S(1)} %bitcast.17), channel_id=1, source_target_pairs={{0,8},{8,0},{16,24},{24,16},{32,40},{40,32},{48,56},{56,48},{64,72... | collective-permute-start | bytes 12296 | tf_op jit(solution)/shard_map/ppermute | solution.py:392
  166.0 3.1 %collective-permute-start.17 = (f32[2,8,128]{2,1,0:T(8,128)S(1)}, f32[2,8,128]{2,1,0:T(8,128)S(1)}, u32[]{:S(2)}, u32[]{:S(2)}) collective-permute-start(f32[2,8,128]{2,1,0:T(8,128)S(1)} %pad_maximum_fusion.4), channel_id=1, source_target_pairs={{0,16},{8,24},{16,0},{24,8},{32,48},{40,56},{48,32},{56,40},{64,80... | collective-permute-start | bytes 24584 | tf_op jit(solution)/shard_map/ppermute | solution.py:392
  169.1 4.8 %collective-permute-start.18 = (f32[4,8,128]{2,1,0:T(8,128)S(1)}, f32[4,8,128]{2,1,0:T(8,128)S(1)}, u32[]{:S(2)}, u32[]{:S(2)}) collective-permute-start(f32[4,8,128]{2,1,0:T(8,128)S(1)} %pad_maximum_fusion.2), channel_id=1, source_target_pairs={{0,32},{8,40},{16,48},{24,56},{32,0},{40,8},{48,16},{56,24},{64,96... | collective-permute-start | bytes 49160 | tf_op jit(solution)/shard_map/ppermute | solution.py:392
  173.9 3.7 %collective-permute-start.19 = (f32[8,8,128]{2,1,0:T(8,128)S(1)}, f32[8,8,128]{2,1,0:T(8,128)S(1)}, u32[]{:S(2)}, u32[]{:S(2)}) collective-permute-start(f32[8,8,128]{2,1,0:T(8,128)S(1)} %pad_maximum_fusion.1), channel_id=1, source_target_pairs={{0,64},{8,72},{16,80},{24,88},{32,96},{40,104},{48,112},{56,120},{... | collective-permute-start | bytes 98312 | tf_op jit(solution)/shard_map/ppermute | solution.py:392
  177.5 5.6 %collective-permute-start.20 = (f32[16,8,128]{2,1,0:T(8,128)S(1)}, f32[16,8,128]{2,1,0:T(8,128)S(1)}, u32[]{:S(2)}, u32[]{:S(2)}) collective-permute-start(f32[16,8,128]{2,1,0:T(8,128)S(1)} %pad_maximum_fusion), channel_id=1, source_target_pairs={{0,128},{8,136},{16,144},{24,152},{32,160},{40,168},{48,176},{56,1... | collective-permute-start | bytes 196616 | tf_op jit(solution)/shard_map/ppermute | solution.py:392
